TPU v7x, 512 devices: a whole 4x8x8 slice. The times are simulated.
512 devices in a mesh: prow: 16 (over z_hi, y), pcol: 32 (over z_lo, x, core).
Axes of the slice: x: 4, y: 8, z: 8 (z_hi: 2, z_lo: 4; z = z_hi * 4 + z_lo), core: 2. Of those that a mesh axis runs over, the one named last changes fastest.
Arguments:
- latent: bfloat16 [64, 128, 1280], P('prow', 'pcol'), may hold values from -8 to 8
- norm_scale: float32 [3, 1280], replicated, may hold values from 0.25 to 1.75
- norm_shift: float32 [3, 1280], replicated, may hold values from -3 to 3
- time_shift: float32 [1280], replicated, may hold values from -4 to 4
- conv_bias: float32 [2, 1280], replicated, may hold values from -3 to 3
- conv_one: bfloat16 [3, 3, 1280, 1280], P(None, None, 'prow'), may hold values from -0.0546875 to 0.0546875
- conv_two: bfloat16 [3, 3, 1280, 1280], P(None, None, 'prow'), may hold values from -0.0546875 to 0.0546875
- w_qkv: bfloat16 [3072, 1280], P('prow'), may hold values from -0.3125 to 0.3125
- w_out: bfloat16 [1280, 1024], P('prow'), may hold values from -0.1875 to 0.1875
- stale_kv: bfloat16 [64, 128, 16, 128], P(None, 'pcol', 'prow'), may hold values from -36 to 36
Outputs:
- next_latent: bfloat16 [64, 128, 1280], P('prow', 'pcol')
- fresh_kv: bfloat16 [64, 128, 16, 128], P(None, 'pcol', 'prow')
All inputs are finite; a program needn't handle non-finite values.
Results may differ from a plain program's by a relative error of at most 0.028.
Values may be sent and summed in bfloat16 or wider, within the bound.
No kernel may reach another device: no remote copies, remote signals or barrier semaphores. Data moves between devices by JAX's collectives and lax.ppermute only.
A program may use at most 64 MiB of HBM per device.

v0:
```python
import functools

import jax
import jax.numpy as jnp
from jax import lax
from jax.sharding import Mesh
from jax.sharding import PartitionSpec as P

GROUPS = 32
HEAD = 64
PROW_PCOL = ("prow_0", "prow_1", "pcol_0", "pcol_1", "pcol_2")
PROW = ("prow_0", "prow_1")
PCOL = ("pcol_0", "pcol_1", "pcol_2")


EPSILON = 1e-05


def over_axes(x, axes):
    return functools.reduce(lax.psum, axes, x)


def sent_to_all(x, axis):
    copies = jnp.broadcast_to(x, (lax.axis_size(axis), *x.shape))
    return lax.all_to_all(copies, axis, split_axis=0, concat_axis=0, tiled=True)


def in_order(blocks, dim):
    shape = list(blocks.shape[1:])
    shape[dim] *= blocks.shape[0]
    return jnp.moveaxis(blocks, 0, dim).reshape(shape)


def collect(x, axis, dim):
    blocks = sent_to_all(x, axis)
    return in_order(blocks, dim)


def padded(cells, sides, width):
    for axis, dim in sides:
        count = lax.axis_size(axis)
        ends = count - 1
        head = lax.slice_in_dim(cells, 0, width, axis=dim)
        tail = lax.slice_in_dim(cells, cells.shape[dim] - width, cells.shape[dim], axis=dim)
        cells = jnp.concatenate(
            [
                lax.ppermute(tail, axis, [(i, (i + 1) % count) for i in range(ends)]),
                cells,
                lax.ppermute(head, axis, [((i + 1) % count, i) for i in range(ends)]),
            ],
            axis=dim,
        )
    return cells


def times_rows(left, right):
    return lax.dot_general(
        left, right, (((1,), (1,)), ((), ())), preferred_element_type=jnp.float32
    )


def group_norm(field, scale, shift, population):
    rows_here, cols_here, width = field.shape
    grouped = field.reshape(rows_here * cols_here, GROUPS, width // GROUPS)
    summed, squared = (
        over_axes(jnp.sum(grouped, axis=(0, 2)), PROW_PCOL),
        over_axes(jnp.sum(grouped * grouped, axis=(0, 2)), PROW_PCOL),
    )
    average = summed / population
    variance = squared / population - average * average
    centered = grouped - average[None, :, None]
    normed = centered * lax.rsqrt(variance + EPSILON)[None, :, None]
    return normed.reshape(field.shape) * scale + shift


def conv_terms(field, weight):
    rows_here, cols_here, width = field.shape
    out_width = weight.shape[2]
    parties = lax.axis_size(PROW)
    cells = rows_here * cols_here
    strip = collect(field, PROW, 0)
    widened = padded(strip, ((PCOL, 1),), 1)
    framed = jnp.pad(widened, ((1, 1), (0, 0), (0, 0)))
    lines = strip.shape[0]
    total = jnp.zeros((parties * cells, out_width), jnp.float32)
    for row_tap in range(3):
        for col_tap in range(3):
            total = total + times_rows(
                framed[row_tap : row_tap + lines, col_tap : col_tap + cols_here, :].reshape(
                    -1, width
                ),
                weight[row_tap, col_tap],
            )
    returned = lax.all_to_all(
        total.reshape(parties, cells, out_width).astype(jnp.bfloat16),
        PROW,
        split_axis=0,
        concat_axis=2,
        tiled=True,
    ).astype(jnp.float32)
    return returned.reshape(cells, parties * out_width)


def partial_softmax(queries, pairs, scale):
    keys = pairs[..., :HEAD]
    values = pairs[..., HEAD:]
    scores = jnp.einsum("qhd,khd->hqk", queries, keys, preferred_element_type=jnp.float32) * scale
    highest = jnp.max(scores, axis=-1)
    weights = jnp.exp(scores - highest[..., None])
    denominator = jnp.sum(weights, axis=-1)
    weighted = jnp.einsum(
        "hqk,khd->qhd", weights.astype(jnp.bfloat16), values, preferred_element_type=jnp.float32
    )
    return (highest, denominator, weighted)


def shards(
    latent,
    norm_scale,
    norm_shift,
    time_shift,
    conv_bias,
    conv_one,
    conv_two,
    w_qkv,
    w_out,
    stale_kv,
):
    rows_here, cols_here, width = latent.shape
    cells = rows_here * cols_here
    parties = lax.axis_size(PROW)
    population = float(cells * lax.axis_size(PROW) * lax.axis_size(PCOL) * (width // GROUPS))
    inputs = latent.astype(jnp.float32)
    first_act = jax.nn.silu(group_norm(inputs, norm_scale[0], norm_shift[0], population)).astype(
        jnp.bfloat16
    )
    first_conv = conv_terms(first_act, conv_one).reshape(latent.shape) + conv_bias[0] + time_shift
    second_act = jax.nn.silu(
        group_norm(first_conv, norm_scale[1], norm_shift[1], population)
    ).astype(jnp.bfloat16)
    second_conv = conv_terms(second_act, conv_two).reshape(latent.shape) + conv_bias[1]
    resnet_out = (inputs + second_conv).astype(jnp.bfloat16)
    attn_in = group_norm(
        resnet_out.astype(jnp.float32), norm_scale[2], norm_shift[2], population
    ).astype(jnp.bfloat16)
    column_width = w_qkv.shape[0]
    heads_here = column_width // (3 * HEAD)
    piece = collect(attn_in, PROW, 0)
    mapped = times_rows(piece.reshape(-1, width), w_qkv)
    strip_qkv = mapped.astype(jnp.bfloat16).reshape(piece.shape[0], cols_here, column_width)
    strip_rows = strip_qkv.shape[0]
    parted = strip_qkv.reshape(strip_rows * cols_here, heads_here, 3, HEAD)
    queries = parted[:, :, 0, :]
    fresh = jnp.concatenate([parted[:, :, 1, :], parted[:, :, 2, :]], axis=-1)
    scale = HEAD ** (-0.5)
    column = lax.axis_index(PCOL)
    initial = partial_softmax(queries, fresh, scale)
    piece = lax.all_gather(stale_kv, PCOL, axis=1, tiled=True)
    highest, denominator, weighted = initial
    columns = lax.iota(jnp.int32, piece.shape[1])
    foreign = jnp.broadcast_to((columns // cols_here != column)[None, :], piece.shape[:2]).reshape(
        -1
    )
    pairs = piece.reshape(-1, heads_here, 2 * HEAD)
    scores = (
        jnp.einsum("qhd,khd->hqk", queries, pairs[:, :, :HEAD], preferred_element_type=jnp.float32)
        * scale
    )
    scores = jnp.where(foreign[None, None, :], scores, -jnp.inf)
    raised = jnp.maximum(highest, jnp.max(scores, axis=-1))
    factor = jnp.exp(highest - raised)
    weights = jnp.exp(scores - raised[..., None])
    denominator = denominator * factor + jnp.sum(weights, axis=-1)
    update = jnp.einsum(
        "hqk,khd->qhd",
        weights.astype(jnp.bfloat16),
        pairs[:, :, HEAD:],
        preferred_element_type=jnp.float32,
    )
    weighted = weighted * factor.T[..., None] + update
    highest, denominator, weighted = (raised, denominator, weighted)
    attended = (
        (weighted / denominator.T[..., None]).astype(jnp.bfloat16).reshape(-1, heads_here * HEAD)
    )
    out_width = w_out.shape[0]
    summed = times_rows(collect(attended, PROW, 1), w_out)
    added = (
        lax.all_to_all(
            summed.reshape(parties, cells, out_width).astype(jnp.bfloat16),
            PROW,
            split_axis=0,
            concat_axis=2,
            tiled=True,
        )
        .astype(jnp.float32)
        .reshape(cells, width)
    )
    next_latent = (
        (resnet_out.astype(jnp.float32).reshape(cells, width) + added)
        .astype(jnp.bfloat16)
        .reshape(latent.shape)
    )
    return (next_latent, fresh.reshape(strip_rows, cols_here, heads_here, 2 * HEAD))


def solution(mesh):
    torus = Mesh(
        mesh.devices.reshape(2, 8, 4, 4, 2), ("prow_0", "prow_1", "pcol_0", "pcol_1", "pcol_2")
    )
    in_specs = (
        P(PROW, PCOL, None),
        P(),
        P(),
        P(),
        P(),
        P(None, None, PROW, None),
        P(None, None, PROW, None),
        P(PROW, None),
        P(PROW, None),
        P(None, PCOL, PROW, None),
    )
    out_specs = (P(PROW, PCOL, None), P(None, PCOL, PROW, None))
    return jax.shard_map(
        shards, mesh=torus, in_specs=in_specs, out_specs=out_specs, check_vma=False
    )
```

profile of v0, /device:TPU:1, one launch (start us, length us, event | category | flops | bytes accessed | tf_op | source)
XLA Modules:
  0.0 418.5 jit_solution(3332623059287962505)
XLA Ops:
  8.5 11.9 %all-reduce.16 = (f32[32]{0:T(128)S(1)}, f32[32]{0:T(128)S(1)}) all-reduce(f32[32]{0:T(128)S(1)} %reduce_sum.96, f32[32]{0:T(128)S(1)} %reduce_sum.90), channel_id=1, replica_groups=mesh['prow_0'=2,'prow_1'=8,'pcol_0'=4,'pcol_1'=4,'pcol_2'=2] {'prow_0'}, use_global_device_ids=true, to_apply=%region_9.0 | all-reduce | flops 64 | bytes 512 | tf_op jit(solution)/shard_map/psum | solution.py:20
  20.3 13.8 %all-reduce.4 = (f32[32]{0:T(128)S(1)}, f32[32]{0:T(128)S(1)}) all-reduce(f32[32]{0:T(128)S(1)} %get-tuple-element.44, f32[32]{0:T(128)S(1)} %get-tuple-element.45), channel_id=1, replica_groups=mesh['prow_0'=2,'prow_1'=8,'pcol_0'=4,'pcol_1'=4,'pcol_2'=2] {'prow_1'}, use_global_device_ids=true, to_apply=%region_10.0 | all-reduce | flops 64 | bytes 512 | tf_op jit(solution)/shard_map/psum | solution.py:20
  34.2 9.6 %all-reduce.10 = (f32[32]{0:T(128)S(1)}, f32[32]{0:T(128)S(1)}) all-reduce(f32[32]{0:T(128)S(1)} %get-tuple-element.20, f32[32]{0:T(128)S(1)} %get-tuple-element.21), channel_id=1, replica_groups=mesh['prow_0'=2,'prow_1'=8,'pcol_0'=4,'pcol_1'=4,'pcol_2'=2] {'pcol_0'}, use_global_device_ids=true, to_apply=%region_11.0 | all-reduce | flops 64 | bytes 512 | tf_op jit(solution)/shard_map/psum | solution.py:20
  43.8 8.5 %all-reduce.7 = (f32[32]{0:T(128)S(1)}, f32[32]{0:T(128)S(1)}) all-reduce(f32[32]{0:T(128)S(1)} %get-tuple-element.32, f32[32]{0:T(128)S(1)} %get-tuple-element.33), channel_id=1, replica_groups=mesh['prow_0'=2,'prow_1'=8,'pcol_0'=4,'pcol_1'=4,'pcol_2'=2] {'pcol_1'}, use_global_device_ids=true, to_apply=%region_12.13 | all-reduce | flops 64 | bytes 512 | tf_op jit(solution)/shard_map/psum | solution.py:20
  52.3 11.4 %all-reduce.13 = (f32[32]{0:T(128)S(1)}, f32[32]{0:T(128)S(1)}) all-reduce(f32[32]{0:T(128)S(1)} %get-tuple-element.26, f32[32]{0:T(128)S(1)} %get-tuple-element.27), channel_id=1, replica_groups=mesh['prow_0'=2,'prow_1'=8,'pcol_0'=4,'pcol_1'=4,'pcol_2'=2] {'pcol_2'}, use_global_device_ids=true, to_apply=%region_13.14 | all-reduce | flops 64 | bytes 512 | tf_op jit(solution)/shard_map/psum | solution.py:20
  67.5 9.5 %all-to-all-start = ((bf16[16,4,4,1280]{3,2,1,0:T(4,128)(2,1)}), bf16[16,4,4,1280]{3,2,1,0:T(4,128)(2,1)S(1)}, u32[]{:S(2)}, u32[]{:S(2)}) async-start(bf16[16,4,4,1280]{3,2,1,0:T(4,128)(2,1)} %broadcast_in_dim.24), calls=%async_computation | async-start | bytes 1310720 | tf_op jit(solution)/shard_map/all_to_all | solution.py:25
  77.1 20.8 %all-to-all-done = bf16[16,4,4,1280]{3,2,1,0:T(4,128)(2,1)S(1)} async-done(((bf16[16,4,4,1280]{3,2,1,0:T(4,128)(2,1)}), bf16[16,4,4,1280]{3,2,1,0:T(4,128)(2,1)S(1)}, u32[]{:S(2)}, u32[]{:S(2)}) %all-to-all-start) | async-done | bytes 655392 | tf_op jit(solution)/shard_map/all_to_all | solution.py:25
  140.7 11.2 %all-to-all-done.1 = bf16[16,16,80]{2,1,0:T(8,128)(2,1)S(1)} async-done(((bf16[16,16,80]{2,1,0:T(8,128)(2,1)}), bf16[16,16,80]{2,1,0:T(8,128)(2,1)S(1)}, u32[]{:S(2)}, u32[]{:S(2)}) %all-to-all-start.1) | async-done | bytes 40992 | tf_op jit(solution)/shard_map/all_to_all | solution.py:94
  152.6 7.7 %all-reduce.15 = (f32[32]{0:T(128)S(1)}, f32[32]{0:T(128)S(1)}) all-reduce(f32[32]{0:T(128)S(1)} %reduce_sum.125, f32[32]{0:T(128)S(1)} %reduce_sum.99), channel_id=1, replica_groups=mesh['prow_0'=2,'prow_1'=8,'pcol_0'=4,'pcol_1'=4,'pcol_2'=2] {'prow_0'}, use_global_device_ids=true, to_apply=%region_23.24 | all-reduce | flops 64 | bytes 512 | tf_op jit(solution)/shard_map/psum | solution.py:20
  160.3 11.4 %all-reduce.3 = (f32[32]{0:T(128)S(1)}, f32[32]{0:T(128)S(1)}) all-reduce(f32[32]{0:T(128)S(1)} %get-tuple-element.42, f32[32]{0:T(128)S(1)} %get-tuple-element.43), channel_id=1, replica_groups=mesh['prow_0'=2,'prow_1'=8,'pcol_0'=4,'pcol_1'=4,'pcol_2'=2] {'prow_1'}, use_global_device_ids=true, to_apply=%region_24.25 | all-reduce | flops 64 | bytes 512 | tf_op jit(solution)/shard_map/psum | solution.py:20
  171.7 6.6 %all-reduce.9 = (f32[32]{0:T(128)S(1)}, f32[32]{0:T(128)S(1)}) all-reduce(f32[32]{0:T(128)S(1)} %get-tuple-element.18, f32[32]{0:T(128)S(1)} %get-tuple-element.19), channel_id=1, replica_groups=mesh['prow_0'=2,'prow_1'=8,'pcol_0'=4,'pcol_1'=4,'pcol_2'=2] {'pcol_0'}, use_global_device_ids=true, to_apply=%region_25.26 | all-reduce | flops 64 | bytes 512 | tf_op jit(solution)/shard_map/psum | solution.py:20
  178.3 7.8 %all-reduce.6 = (f32[32]{0:T(128)S(1)}, f32[32]{0:T(128)S(1)}) all-reduce(f32[32]{0:T(128)S(1)} %get-tuple-element.30, f32[32]{0:T(128)S(1)} %get-tuple-element.31), channel_id=1, replica_groups=mesh['prow_0'=2,'prow_1'=8,'pcol_0'=4,'pcol_1'=4,'pcol_2'=2] {'pcol_1'}, use_global_device_ids=true, to_apply=%region_26.27 | all-reduce | flops 64 | bytes 512 | tf_op jit(solution)/shard_map/psum | solution.py:20
  186.1 14.2 %all-reduce.12 = (f32[32]{0:T(128)S(1)}, f32[32]{0:T(128)S(1)}) all-reduce(f32[32]{0:T(128)S(1)} %get-tuple-element.24, f32[32]{0:T(128)S(1)} %get-tuple-element.25), channel_id=1, replica_groups=mesh['prow_0'=2,'prow_1'=8,'pcol_0'=4,'pcol_1'=4,'pcol_2'=2] {'pcol_2'}, use_global_device_ids=true, to_apply=%region_27.28 | all-reduce | flops 64 | bytes 512 | tf_op jit(solution)/shard_map/psum | solution.py:20
  206.5 20.2 %all-to-all-done.2 = bf16[16,4,4,1280]{3,2,1,0:T(4,128)(2,1)S(1)} async-done(((bf16[16,4,4,1280]{3,2,1,0:T(4,128)(2,1)}), bf16[16,4,4,1280]{3,2,1,0:T(4,128)(2,1)S(1)}, u32[]{:S(2)}, u32[]{:S(2)}) %all-to-all-start.2) | async-done | bytes 655392 | tf_op jit(solution)/shard_map/all_to_all | solution.py:25
  265.4 15.8 %all_to_all.47 = bf16[16,16,80]{2,1,0:T(8,128)(2,1)S(1)} all-to-all(bf16[16,16,80]{2,1,0:T(8,128)(2,1)S(1)} %bitcast.183), channel_id=1, replica_groups=mesh['prow_0'=2,'prow_1'=8,'pcol_0'=4,'pcol_1'=4,'pcol_2'=2] {'prow_0','..., dimensions={0} | all-to-all | bytes 81920 | tf_op jit(solution)/shard_map/all_to_all | solution.py:94
  281.9 7.7 %all-reduce.14 = (f32[32]{0:T(128)S(1)}, f32[32]{0:T(128)S(1)}) all-reduce(f32[32]{0:T(128)S(1)} %reduce_sum.131, f32[32]{0:T(128)S(1)} %reduce_sum.128), channel_id=1, replica_groups=mesh['prow_0'=2,'prow_1'=8,'pcol_0'=4,'pcol_1'=4,'pcol_2'=2] {'prow_0'}, use_global_device_ids=true, to_apply=%region_37.38 | all-reduce | flops 64 | bytes 512 | tf_op jit(solution)/shard_map/psum | solution.py:20
  289.6 11.4 %all-reduce.2 = (f32[32]{0:T(128)S(1)}, f32[32]{0:T(128)S(1)}) all-reduce(f32[32]{0:T(128)S(1)} %get-tuple-element.40, f32[32]{0:T(128)S(1)} %get-tuple-element.41), channel_id=1, replica_groups=mesh['prow_0'=2,'prow_1'=8,'pcol_0'=4,'pcol_1'=4,'pcol_2'=2] {'prow_1'}, use_global_device_ids=true, to_apply=%region_38.39 | all-reduce | flops 64 | bytes 512 | tf_op jit(solution)/shard_map/psum | solution.py:20
  301.0 6.7 %all-reduce.8 = (f32[32]{0:T(128)S(1)}, f32[32]{0:T(128)S(1)}) all-reduce(f32[32]{0:T(128)S(1)} %get-tuple-element.16, f32[32]{0:T(128)S(1)} %get-tuple-element.17), channel_id=1, replica_groups=mesh['prow_0'=2,'prow_1'=8,'pcol_0'=4,'pcol_1'=4,'pcol_2'=2] {'pcol_0'}, use_global_device_ids=true, to_apply=%region_39.40 | all-reduce | flops 64 | bytes 512 | tf_op jit(solution)/shard_map/psum | solution.py:20
  307.7 9.5 %all-reduce.5 = (f32[32]{0:T(128)S(1)}, f32[32]{0:T(128)S(1)}) all-reduce(f32[32]{0:T(128)S(1)} %get-tuple-element.28, f32[32]{0:T(128)S(1)} %get-tuple-element.29), channel_id=1, replica_groups=mesh['prow_0'=2,'prow_1'=8,'pcol_0'=4,'pcol_1'=4,'pcol_2'=2] {'pcol_1'}, use_global_device_ids=true, to_apply=%region_40.41 | all-reduce | flops 64 | bytes 512 | tf_op jit(solution)/shard_map/psum | solution.py:20
  317.2 14.3 %all-reduce.11 = (f32[32]{0:T(128)S(1)}, f32[32]{0:T(128)S(1)}) all-reduce(f32[32]{0:T(128)S(1)} %get-tuple-element.22, f32[32]{0:T(128)S(1)} %get-tuple-element.23), channel_id=1, replica_groups=mesh['prow_0'=2,'prow_1'=8,'pcol_0'=4,'pcol_1'=4,'pcol_2'=2] {'pcol_2'}, use_global_device_ids=true, to_apply=%region_41.42 | all-reduce | flops 64 | bytes 512 | tf_op jit(solution)/shard_map/psum | solution.py:20
  339.9 17.9 %all-to-all-done.4 = bf16[16,4,4,1280]{3,2,1,0:T(4,128)(2,1)S(1)} async-done(((bf16[16,4,4,1280]{3,2,1,0:T(4,128)(2,1)}), bf16[16,4,4,1280]{3,2,1,0:T(4,128)(2,1)S(1)}, u32[]{:S(2)}, u32[]{:S(2)}) %all-to-all-start.4) | async-done | bytes 655392 | tf_op jit(solution)/shard_map/all_to_all | solution.py:25
  373.5 16.6 %all-to-all-done.5 = bf16[16,256,64]{1,2,0:T(8,128)(2,1)S(1)} async-done(((bf16[16,256,64]{1,2,0:T(8,128)(2,1)}), bf16[16,256,64]{1,2,0:T(8,128)(2,1)S(1)}, u32[]{:S(2)}, u32[]{:S(2)}) %all-to-all-start.5) | async-done | bytes 524320 | tf_op jit(solution)/shard_map/all_to_all | solution.py:25
  392.7 6.9 %all-to-all-start.6 = ((bf16[16,16,80]{2,1,0:T(8,128)(2,1)}), bf16[16,16,80]{2,1,0:T(8,128)(2,1)S(1)}, u32[]{:S(2)}, u32[]{:S(2)}) async-start(bf16[16,16,80]{2,1,0:T(8,128)(2,1)} %convolution_convert_fusion.1), calls=%async_computation.6 | async-start | bytes 131072 | tf_op jit(solution)/shard_map/all_to_all | solution.py:188
  400.3 10.5 %all-to-all-done.6 = bf16[16,16,80]{2,1,0:T(8,128)(2,1)S(1)} async-done(((bf16[16,16,80]{2,1,0:T(8,128)(2,1)}), bf16[16,16,80]{2,1,0:T(8,128)(2,1)S(1)}, u32[]{:S(2)}, u32[]{:S(2)}) %all-to-all-start.6) | async-done | bytes 40992 | tf_op jit(solution)/shard_map/all_to_all | solution.py:188
  (177 shorter events, 121.8 us)
Async XLA Ops:
  7.2 351.6 %copy-start = (bf16[192,1280]{1,0:T(8,128)(2,1)S(1)}, bf16[192,1280]{1,0:T(8,128)(2,1)}, u32[]{:S(2)}) copy-start(bf16[192,1280]{1,0:T(8,128)(2,1)} %param.17) | copy-start | bytes 1474564
  7.2 69.8 %copy-start.19 = (f32[1280]{0:T(1024)S(1)}, f32[1280]{0:T(1024)}, u32[]{:S(2)}) copy-start(f32[1280]{0:T(1024)} %param.13) | copy-start | bytes 15364
  67.5 30.4 %all-to-all-start = ((bf16[16,4,4,1280]{3,2,1,0:T(4,128)(2,1)}), bf16[16,4,4,1280]{3,2,1,0:T(4,128)(2,1)S(1)}, u32[]{:S(2)}, u32[]{:S(2)}) async-start(bf16[16,4,4,1280]{3,2,1,0:T(4,128)(2,1)} %broadcast_in_dim.24), calls=%async_computation | async-start | bytes 1310720 | tf_op jit(solution)/shard_map/all_to_all | solution.py:25
  98.3 8.5 %collective-permute-start.1 = (bf16[64,1,1280]{2,1,0:T(2,128)(2,1)S(1)}, bf16[64,1,1280]{2,1,0:T(2,128)(2,1)S(1)}, u32[]{:S(2)}, u32[]{:S(2)}) collective-permute-start(bf16[64,1,1280]{2,1,0:T(2,128)(2,1)S(1)} %get-tuple-element.68), channel_id=1, source_target_pairs={{1,0},{2,1},{3,2},{4,3},{5,4},{6,5},{7,6},{8,7},{9,8},{10,9},{11,1... | collective-permute-start | bytes 491528 | tf_op jit(solution)/shard_map/ppermute | solution.py:49
  102.8 5.9 %collective-permute-start = (bf16[64,1,1280]{2,1,0:T(2,128)(2,1)S(1)}, bf16[64,1,1280]{2,1,0:T(2,128)(2,1)S(1)}, u32[]{:S(2)}, u32[]{:S(2)}) collective-permute-start(bf16[64,1,1280]{2,1,0:T(2,128)(2,1)S(1)} %get-tuple-element.67), channel_id=1, source_target_pairs={{0,1},{1,2},{2,3},{3,4},{4,5},{5,6},{6,7},{7,8},{8,9},{9,10},{10,1... | collective-permute-start | bytes 491528 | tf_op jit(solution)/shard_map/ppermute | solution.py:47
  124.5 4.8 %copy-start.5 = (bf16[64,4,1280]{2,1,0:T(4,128)(2,1)S(1)}, bf16[64,4,1280]{2,1,0:T(4,128)(2,1)}, u32[]{:S(2)}) copy-start(bf16[64,4,1280]{2,1,0:T(4,128)(2,1)} %get-tuple-element.59) | copy-start | bytes 1966084
  131.5 9.1 %copy-start.21 = (f32[2,1280]{1,0:T(2,128)S(1)}, f32[2,1280]{1,0:T(2,128)}, u32[]{:S(2)}) copy-start(f32[2,1280]{1,0:T(2,128)} %param.14) | copy-start | bytes 30724
  131.7 68.9 %copy-start.17 = (f32[1280]{0:T(1024)S(1)}, f32[1280]{0:T(1024)}, u32[]{:S(2)}) copy-start(f32[1280]{0:T(1024)} %get-tuple-element.13) | copy-start | bytes 15364
  131.7 68.9 %copy-start.18 = (f32[1280]{0:T(1024)S(1)}, f32[1280]{0:T(1024)}, u32[]{:S(2)}) copy-start(f32[1280]{0:T(1024)} %get-tuple-element.81) | copy-start | bytes 15364
  131.7 68.9 %copy-start.20 = (f32[1280]{0:T(1024)S(1)}, f32[1280]{0:T(1024)}, u32[]{:S(2)}) copy-start(f32[1280]{0:T(1024)} %param.13) | copy-start | bytes 15364
  134.5 71.4 %copy-start.16 = (bf16[64,4,1,128]{3,1,2,0:T(4,128)(2,1)S(1)}, bf16[64,4,1,128]{3,1,2,0:T(4,128)(2,1)}, u32[]{:S(2)}) copy-start(bf16[64,4,1,128]{3,1,2,0:T(4,128)(2,1)} %param.19) | copy-start | bytes 196612
  135.2 16.7 %all-to-all-start.1 = ((bf16[16,16,80]{2,1,0:T(8,128)(2,1)}), bf16[16,16,80]{2,1,0:T(8,128)(2,1)S(1)}, u32[]{:S(2)}, u32[]{:S(2)}) async-start(bf16[16,16,80]{2,1,0:T(8,128)(2,1)} %bitcast.10), calls=%async_computation.1 | async-start | bytes 131072 | tf_op jit(solution)/shard_map/all_to_all | solution.py:94
  201.8 24.9 %all-to-all-start.2 = ((bf16[16,4,4,1280]{3,2,1,0:T(4,128)(2,1)}), bf16[16,4,4,1280]{3,2,1,0:T(4,128)(2,1)S(1)}, u32[]{:S(2)}, u32[]{:S(2)}) async-start(bf16[16,4,4,1280]{3,2,1,0:T(4,128)(2,1)} %broadcast_in_dim.42), calls=%async_computation.2 | async-start | bytes 1310720 | tf_op jit(solution)/shard_map/all_to_all | solution.py:25
  205.8 131.2 %all-gather.2.cloned.1.call-start = ((), (), s32[]{:S(2)}) async-start(), calls=%async_computation.7 | async-start | bytes 2162688 | tf_op jit(solution)/shard_map/all_gather | solution.py:158
  227.1 11.7 %collective-permute-start.3 = (bf16[64,1,1280]{2,1,0:T(2,128)(2,1)S(1)}, bf16[64,1,1280]{2,1,0:T(2,128)(2,1)S(1)}, u32[]{:S(2)}, u32[]{:S(2)}) collective-permute-start(bf16[64,1,1280]{2,1,0:T(2,128)(2,1)S(1)} %get-tuple-element.64), channel_id=1, source_target_pairs={{1,0},{2,1},{3,2},{4,3},{5,4},{6,5},{7,6},{8,7},{9,8},{10,9},{11,1... | collective-permute-start | bytes 491528 | tf_op jit(solution)/shard_map/ppermute | solution.py:49
  231.6 8.4 %collective-permute-start.2 = (bf16[64,1,1280]{2,1,0:T(2,128)(2,1)S(1)}, bf16[64,1,1280]{2,1,0:T(2,128)(2,1)S(1)}, u32[]{:S(2)}, u32[]{:S(2)}) collective-permute-start(bf16[64,1,1280]{2,1,0:T(2,128)(2,1)S(1)} %get-tuple-element.63), channel_id=1, source_target_pairs={{0,1},{1,2},{2,3},{3,4},{4,5},{5,6},{6,7},{7,8},{8,9},{9,10},{10,1... | collective-permute-start | bytes 491528 | tf_op jit(solution)/shard_map/ppermute | solution.py:47
  250.3 4.8 %copy-start.7 = (bf16[64,4,1280]{2,1,0:T(4,128)(2,1)S(1)}, bf16[64,4,1280]{2,1,0:T(4,128)(2,1)}, u32[]{:S(2)}) copy-start(bf16[64,4,1280]{2,1,0:T(4,128)(2,1)} %get-tuple-element.53) | copy-start | bytes 1966084
  257.3 5.4 %copy-start.4 = (bf16[256,1280]{1,0:T(8,128)(2,1)S(1)}, bf16[256,1280]{1,0:T(8,128)(2,1)}, u32[]{:S(2)}) copy-start(bf16[256,1280]{1,0:T(8,128)(2,1)} %reshape.285) | copy-start | bytes 1966084
  258.7 5.3 %copy-start.12 = (f32[256,80]{0,1:T(8,128)S(1)}, f32[256,80]{0,1:T(8,128)}, u32[]{:S(2)}) copy-start(f32[256,80]{0,1:T(8,128)} %fusion.36) | copy-start | bytes 245764
  262.7 18.8 %copy-start.10 = (bf16[4,4,1280]{2,1,0:T(4,128)(2,1)S(1)}, bf16[4,4,1280]{2,1,0:T(4,128)(2,1)}, u32[]{:S(2)}) copy-start(bf16[4,4,1280]{2,1,0:T(4,128)(2,1)} %param.10) | copy-start | bytes 122884
  332.9 24.9 %all-to-all-start.4 = ((bf16[16,4,4,1280]{3,2,1,0:T(4,128)(2,1)}), bf16[16,4,4,1280]{3,2,1,0:T(4,128)(2,1)S(1)}, u32[]{:S(2)}, u32[]{:S(2)}) async-start(bf16[16,4,4,1280]{3,2,1,0:T(4,128)(2,1)} %broadcast_in_dim.43), calls=%async_computation.4 | async-start | bytes 1310720 | tf_op jit(solution)/shard_map/all_to_all | solution.py:25
  366.9 23.1 %all-to-all-start.5 = ((bf16[16,256,64]{1,2,0:T(8,128)(2,1)}), bf16[16,256,64]{1,2,0:T(8,128)(2,1)S(1)}, u32[]{:S(2)}, u32[]{:S(2)}) async-start(bf16[16,256,64]{1,2,0:T(8,128)(2,1)} %broadcast_in_dim.48), calls=%async_computation.5 | async-start | bytes 1048576 | tf_op jit(solution)/shard_map/all_to_all | solution.py:25
  373.2 18.5 %copy-start.15 = (bf16[80,1024]{1,0:T(8,128)(2,1)S(1)}, bf16[80,1024]{1,0:T(8,128)(2,1)}, u32[]{:S(2)}) copy-start(bf16[80,1024]{1,0:T(8,128)(2,1)} %param.18) | copy-start | bytes 491524
  392.7 18.2 %all-to-all-start.6 = ((bf16[16,16,80]{2,1,0:T(8,128)(2,1)}), bf16[16,16,80]{2,1,0:T(8,128)(2,1)S(1)}, u32[]{:S(2)}, u32[]{:S(2)}) async-start(bf16[16,16,80]{2,1,0:T(8,128)(2,1)} %convolution_convert_fusion.1), calls=%async_computation.6 | async-start | bytes 131072 | tf_op jit(solution)/shard_map/all_to_all | solution.py:188
  (9 other events, 19.5 us)
Sparse Core Ops, SparseCore 0:
  209.3 63.3 all-gather.1
where the time goes:
time: 422 us; the launch traced here: 419 us
  blocking collectives  168 us (40%)
  waiting for transfers between devices  103 us (24%)
  starting transfers between devices  50.7 us (12%)
  local copies, waits for them, and re-layouts  35.3 us (8%)
  matrix products  34 us (8%)
  between operations  14.8 us (4%)
  other arithmetic  12.5 us (3%)
    psum x15, blocking collectives, over_axes(): return functools.reduce(lax.psum, axes, x)  152 us
    all_to_all x4, waiting for transfers between devices, sent_to_all(): return lax.all_to_all(copies, axis, split_axis=0, concat_axis=0, tiled=True)  75.4 us
    dot_general x20, matrix products, times_rows(): lax.dot_general(left, right, (((1,), (1,)), ((), ())), preferred_element_...  29.6 us
    all_to_all x4, starting transfers between devices, sent_to_all(): return lax.all_to_all(copies, axis, split_axis=0, concat_axis=0, tiled=True)  23.7 us
    all_to_all x1, blocking collectives, conv_terms(): lax.all_to_all(total.reshape(parties, cells, out_width).astype(jnp.bfloat...  15.8 us
    reshape x18, local copies, waits for them, and re-layouts, conv_terms(): framed[row_tap:row_tap + lines, col_tap:col_tap + cols_here, :]  12.8 us
    all_to_all x1, waiting for transfers between devices, conv_terms(): lax.all_to_all(total.reshape(parties, cells, out_width).astype(jnp.bfloat...  11.2 us
    all_to_all x1, waiting for transfers between devices, shards(): lax.all_to_all(summed.reshape(parties, cells, out_width).astype(jnp.bfloa...  10.5 us
  transfers between devices with their start and end apart: 11, of which 10 were waited for; matrix products, arithmetic and copies ran while one was open for 8% of the time, Pallas kernels for 0%

commit v1 on v0

v1 whole, which is shorter than its diff:
```python
import functools

import jax
import jax.numpy as jnp
from jax import lax
from jax.experimental import pallas as pl
from jax.experimental.pallas import tpu as pltpu
from jax.sharding import Mesh
from jax.sharding import PartitionSpec as P

GROUPS = 32
HEAD = 64
PROW = ("prow_0", "prow_1")
PCOL = ("pcol_0", "pcol_1", "pcol_2")
EPSILON = 1e-05
F32 = jnp.float32
BF16 = jnp.bfloat16

C = 1280
GC = C // GROUPS
NP = 16
NS = 32
LR = 64
PC = 4
CELLS = LR * PC
OC = C // NP
POPULATION = float(LR * PC * NS * GC)


def iota(shape, dim):
    return lax.broadcasted_iota(jnp.int32, shape, dim)


def one_hot(mask, dtype):
    return jnp.where(mask, 1.0, 0.0).astype(dtype)


def nt(left, right, precision=None):
    return lax.dot_general(
        left, right, (((1,), (1,)), ((), ())), precision=precision, preferred_element_type=F32
    )


def nn(left, right, precision=None):
    return lax.dot_general(
        left, right, (((1,), (0,)), ((), ())), precision=precision, preferred_element_type=F32
    )


def strip_order():
    o = iota((CELLS, CELLS), 0)
    i = iota((CELLS, CELLS), 1)
    return one_hot((o % LR) * PC + o // LR == i, BF16)


def cell_order():
    o = iota((CELLS, CELLS), 1)
    i = iota((CELLS, CELLS), 0)
    return one_hot((o % LR) * PC + o // LR == i, BF16)


def moments(sums_ref):
    sums = jnp.sum(sums_ref[...], axis=0)
    mean = sums / POPULATION
    square = pltpu.roll(mean, 128 - GROUPS, 1)
    return mean, lax.rsqrt(jnp.maximum(square - mean * mean, 0.0) + EPSILON)


def silu(v):
    return v / (1.0 + jnp.exp(-v))


def stats_cells_kernel(x_ref, out_ref):
    x = x_ref[...].astype(F32)
    first = jnp.sum(x, axis=0, keepdims=True)
    second = jnp.sum(x * x, axis=0, keepdims=True)
    both = jnp.concatenate([first, second, jnp.zeros((6, C), F32)], axis=0)
    groups = one_hot(iota((C, 128), 0) // GC == iota((C, 128), 1), F32)
    reduced = nn(both, groups, lax.Precision.HIGHEST)
    row = reduced[0:1, :] + pltpu.roll(reduced, GROUPS, 1)[1:2, :]
    out_ref[...] = jnp.broadcast_to(row[None], out_ref.shape)


def stats_channels_kernel(x_ref, out_ref):
    firsts, seconds = [], []
    for pair in range(NP):
        x = x_ref[OC * pair : OC * (pair + 1), :].astype(F32)
        y = x * x
        x = x[:, :128] + x[:, 128:]
        y = y[:, :128] + y[:, 128:]
        for half in range(2):
            firsts.append(jnp.sum(x[GC * half : GC * (half + 1)], axis=0, keepdims=True))
            seconds.append(jnp.sum(y[GC * half : GC * (half + 1)], axis=0, keepdims=True))
    first = jnp.sum(jnp.concatenate(firsts, axis=0), axis=1, keepdims=True)
    second = jnp.sum(jnp.concatenate(seconds, axis=0), axis=1, keepdims=True)
    group = iota((GROUPS, 128), 0)
    lane = iota((GROUPS, 128), 1)
    spread = jnp.where(group == lane, first, 0.0) + jnp.where(group + GROUPS == lane, second, 0.0)
    out_ref[...] = jnp.broadcast_to(jnp.sum(spread, axis=0, keepdims=True)[None], out_ref.shape)


def conv_combine(products, mid_ref, to_left_ref, to_right_ref):
    lane = iota((OC, CELLS), 1)
    row = lane % LR

    def tap(a, b):
        at = (3 * a + b) * OC
        return products[at : at + OC, :]

    def rows_summed(b):
        above = jnp.where(row > 0, pltpu.roll(tap(0, b), 1, 1), 0.0)
        below = jnp.where(row < LR - 1, pltpu.roll(tap(2, b), CELLS - 1, 1), 0.0)
        return tap(1, b) + above + below

    before = rows_summed(0)
    after = rows_summed(2)
    to_right_ref[...] = before[:, CELLS - LR :]
    to_left_ref[...] = after[:, :LR]
    mid_ref[...] = (
        rows_summed(1)
        + jnp.where(lane >= LR, pltpu.roll(before, LR, 1), 0.0)
        + jnp.where(lane < CELLS - LR, pltpu.roll(after, CELLS - LR, 1), 0.0)
    )


def conv_cells_kernel(
    at_ref, x_ref, sums_ref, scale_ref, shift_ref, w_ref, mid_ref, left_ref, right_ref, own_ref
):
    mean, rstd = moments(sums_ref)
    both = jnp.concatenate([mean, rstd, jnp.zeros((6, 128), F32)], axis=0)
    groups = one_hot(iota((128, C), 1) // GC == iota((128, C), 0), F32)
    spread = nn(both, groups, lax.Precision.HIGHEST)
    gain = spread[1:2, :] * scale_ref[0:1, :]
    offset = shift_ref[0:1, :] - spread[0:1, :] * gain
    cells = nn(strip_order(), x_ref[...])
    pick = one_hot(iota((OC, C), 1) == iota((OC, C), 0) + at_ref[0] * OC, BF16)
    own_ref[...] = nt(pick, cells.astype(BF16))
    act = silu(cells * gain + offset).astype(BF16)
    conv_combine(nt(w_ref[...], act), mid_ref, left_ref, right_ref)


def normed_channels(x_ref, sums_ref, cols_ref, col, act_ref, apply):
    mean, rstd = moments(sums_ref)
    for pair in range(NP):
        parts = []
        for half in range(2):
            g = 2 * pair + half
            rows = slice(GC * g, GC * (g + 1))
            gain = cols_ref[rows, col : col + 1] * rstd[:, g : g + 1]
            offset = cols_ref[rows, col + 1 : col + 2] - mean[:, g : g + 1] * gain
            parts.append((gain, offset))
        gain = jnp.concatenate([parts[0][0], parts[1][0]], axis=0)
        offset = jnp.concatenate([parts[0][1], parts[1][1]], axis=0)
        rows = slice(OC * pair, OC * (pair + 1))
        act_ref[rows, :] = apply(x_ref[rows, :].astype(F32) * gain + offset).astype(BF16)


def conv_channels_kernel(x_ref, sums_ref, cols_ref, w_ref, mid_ref, left_ref, right_ref, act_ref):
    normed_channels(x_ref, sums_ref, cols_ref, 0, act_ref, silu)
    conv_combine(nn(w_ref[...], act_ref[...]), mid_ref, left_ref, right_ref)


def finish_kernel(which, at_ref, mid_ref, from_left_ref, from_right_ref, bias_ref, extra_ref, out_ref):
    row = bias_ref[which : which + 1, :]
    if which == 0:
        row = row + extra_ref[...]
    pick = iota((OC, C), 1) == iota((OC, C), 0) + at_ref[0] * OC
    bias = jnp.sum(jnp.where(pick, row, 0.0), axis=1, keepdims=True)
    sides = jnp.concatenate(
        [from_left_ref[...], jnp.zeros((OC, CELLS - 2 * LR), F32), from_right_ref[...]], axis=1
    )
    total = mid_ref[...] + sides + bias
    if which == 1:
        total = extra_ref[...] + total
    out_ref[...] = jnp.broadcast_to(total.astype(BF16)[None], out_ref.shape)


def attention_kernel(
    at_ref, x_ref, sums_ref, cols_ref, w_ref, pairs_ref, att_ref, fresh_ref, own_ref, act_ref
):
    normed_channels(x_ref, sums_ref, cols_ref, 2, act_ref, lambda v: v)
    mapped = nn(w_ref[...], act_ref[...])
    queries = jnp.transpose(mapped[:HEAD]).astype(BF16)
    fresh = jnp.transpose(mapped[HEAD:]).astype(BF16)
    queries = (queries.astype(F32) * HEAD ** (-0.5)).astype(BF16)
    queries = jnp.concatenate([queries, jnp.zeros((CELLS, HEAD), BF16)], axis=1)
    order = cell_order()
    fresh_ref[...] = nn(order, fresh).astype(BF16)
    pick = one_hot(
        iota((NP, CELLS), 1)
        == (iota((NP, CELLS), 0) % PC) * LR + at_ref[0] * PC + iota((NP, CELLS), 0) // PC,
        BF16,
    )
    own_ref[...] = nt(pick, x_ref[...])
    chunk = 4
    highest = jnp.full((CELLS, 1), -jnp.inf, F32)
    denominator = jnp.zeros((CELLS, 1), F32)
    weighted = jnp.zeros((CELLS, 2 * HEAD), F32)
    for step in range(NS // chunk):
        blocks = []
        for k in range(chunk):
            strip = chunk * step + k
            blocks.append(jnp.where(at_ref[1] == strip, fresh, pairs_ref[strip]))
        pairs = jnp.concatenate(blocks, axis=0)
        scores = nt(queries, pairs)
        raised = jnp.maximum(highest, jnp.max(scores, axis=1, keepdims=True))
        factor = jnp.exp(highest - raised)
        weights = jnp.exp(scores - raised)
        denominator = denominator * factor + jnp.sum(weights, axis=1, keepdims=True)
        weighted = weighted * factor + nn(weights.astype(BF16), pairs)
        highest = raised
    attended = (weighted / denominator).astype(BF16)
    att_ref[...] = nn(order, attended)[:, HEAD:].astype(BF16)


def output_kernel(att_ref, w_ref, own_ref, out_ref):
    att = jnp.concatenate([att_ref[k] for k in range(NP)], axis=1)
    out_ref[...] = (own_ref[...] + nt(att, w_ref[...])).astype(BF16)


def call(kernel, name, outs, scalars=0, scratch=()):
    def run(*args):
        specs = [pl.BlockSpec(memory_space=pltpu.SMEM)] * scalars
        specs += [pl.BlockSpec(memory_space=pltpu.VMEM)] * (len(args) - scalars)
        return pl.pallas_call(
            kernel,
            out_shape=[jax.ShapeDtypeStruct(*out) for out in outs],
            in_specs=specs,
            out_specs=[pl.BlockSpec(memory_space=pltpu.VMEM)] * len(outs),
            scratch_shapes=list(scratch),
            name=name,
        )(*args)

    return run


def to_every(copies, axis):
    return lax.all_to_all(copies, axis, split_axis=0, concat_axis=0, tiled=True)


def beside(value, step):
    pairs = [(i, i + step) for i in range(NS) if 0 <= i + step < NS]
    return lax.ppermute(value, PCOL, pairs)


def shards(
    latent,
    norm_scale,
    norm_shift,
    time_shift,
    conv_bias,
    conv_one,
    conv_two,
    w_qkv,
    w_out,
    stale_kv,
):
    at = jnp.stack([lax.axis_index(PROW), lax.axis_index(PCOL)]).astype(jnp.int32)
    cols = jnp.stack([norm_scale[1], norm_shift[1], norm_scale[2], norm_shift[2]]).T
    pairs = lax.all_gather(stale_kv.reshape(CELLS, 2 * HEAD), PCOL, axis=0)
    w_out_all = lax.all_gather(w_out, PROW, axis=0, tiled=True)
    sums_out = ((NS, 1, 128), F32)
    conv_out = [((OC, CELLS), F32), ((OC, LR), F32), ((OC, LR), F32)]
    act = pltpu.VMEM((C, CELLS), BF16)

    patch = latent.reshape(NP, C)
    strip = to_every(jnp.broadcast_to(patch, (NP, NP, C)), PROW).reshape(CELLS, C)
    (sums,) = call(stats_cells_kernel, "stats0", [sums_out])(strip)
    sums = to_every(sums, PCOL)
    mid, left, right, own = call(
        conv_cells_kernel, "conv1", conv_out + [((OC, CELLS), F32)], scalars=1
    )(at, strip, sums, norm_scale, norm_shift, conv_one.reshape(9 * OC, C))
    (block,) = call(
        functools.partial(finish_kernel, 0), "finish1", [((NP, OC, CELLS), BF16)], scalars=1
    )(at, mid, beside(right, 1), beside(left, -1), conv_bias, time_shift.reshape(1, C))

    field = to_every(block, PROW).reshape(C, CELLS)
    (sums,) = call(stats_channels_kernel, "stats1", [sums_out])(field)
    sums = to_every(sums, PCOL)
    mid, left, right = call(conv_channels_kernel, "conv2", conv_out, scratch=[act])(
        field, sums, cols, conv_two.reshape(9 * OC, C)
    )
    (block,) = call(
        functools.partial(finish_kernel, 1), "finish2", [((NP, OC, CELLS), BF16)], scalars=1
    )(at, mid, beside(right, 1), beside(left, -1), conv_bias, own)

    field = to_every(block, PROW).reshape(C, CELLS)
    (sums,) = call(stats_channels_kernel, "stats2", [sums_out])(field)
    sums = to_every(sums, PCOL)
    attended, fresh, resnet_own = call(
        attention_kernel,
        "attention",
        [((CELLS, HEAD), BF16), ((CELLS, 2 * HEAD), BF16), ((NP, C), F32)],
        scalars=1,
        scratch=[act],
    )(at, field, sums, cols, w_qkv, pairs)
    heads = to_every(attended.reshape(NP, NP, HEAD), PROW)
    (out,) = call(output_kernel, "output", [((NP, C), BF16)])(heads, w_out_all, resnet_own)
    return out.reshape(latent.shape), fresh.reshape(LR, PC, 1, 2 * HEAD)


def solution(mesh):
    torus = Mesh(
        mesh.devices.reshape(2, 8, 4, 4, 2), ("prow_0", "prow_1", "pcol_0", "pcol_1", "pcol_2")
    )
    in_specs = (
        P(PROW, PCOL, None),
        P(),
        P(),
        P(),
        P(),
        P(None, None, PROW, None),
        P(None, None, PROW, None),
        P(PROW, None),
        P(PROW, None),
        P(None, PCOL, PROW, None),
    )
    out_specs = (P(PROW, PCOL, None), P(None, PCOL, PROW, None))
    return jax.shard_map(
        shards, mesh=torus, in_specs=in_specs, out_specs=out_specs, check_vma=False
    )
```

time: 422 us -> 237 us (0.56)
  blocking collectives: 168 us -> 71.3 us
  waiting for transfers between devices: 103 us -> 62.8 us
  matrix products: 34 us -> 0 us
  Pallas kernels: 0 us -> 30.5 us
  local copies, waits for them, and re-layouts: 35.3 us -> 10.7 us
  other arithmetic: 12.5 us -> 0.68 us
  starting transfers between devices: 50.7 us -> 45.4 us
    psum x15 -> x0, blocking collectives: 152 us -> none  [over_axes(): return functools.reduce(lax.psum, axes, x)]
    all_to_all x1 -> x3, blocking collectives: 15.8 us -> 71.3 us  [to_every(): return lax.all_to_all(copies, axis, split_axis=0, concat_axis=0, tiled=True)]
    all_to_all x6 -> x4, waiting for transfers between devices: 97.2 us -> 54.5 us  [to_every(): return lax.all_to_all(copies, axis, split_axis=0, concat_axis=0, tiled=True)]
    dot_general x24 -> x0, matrix products: 34 us -> none  [the longest x20 29.6 us: times_rows(): lax.dot_general(left, right, (((1,), (1,)), ((), ())), preferred_element_...]
    pallas_call x0 -> x9, Pallas kernels: none -> 30.5 us  [run(): pl.pallas_call(kernel, out_shape=[jax.ShapeDtypeStruct(*out) for out in o...]
    reshape x18 -> x3, local copies, waits for them, and re-layouts: 12.8 us -> 2.8 us  [the longest x1 1.41 us: shards(): return (out.reshape(latent.shape), fresh.reshape(LR, PC, 1, 2 * HEAD))]
    slice x9 -> x1, local copies, waits for them, and re-layouts: 7.83 us -> 0.02 us  [shards(): norm_scale[1]]
    concatenate x5 -> x0, other arithmetic: 7.69 us -> none  [the longest x4 6.95 us: padded(): jnp.concatenate([lax.ppermute(tail, axis, [(i, (i + 1) % count) for i in...]
  transfers between devices with their start and end apart: 11 -> 10, of which waited for: 10 -> 6; matrix products, arithmetic and copies ran while one was open for 8% -> 2% of each run, Pallas kernels for 0% -> 12%
where the time goes in v1:
time: 237 us; the launch traced here: 236 us
  blocking collectives  71.3 us (30%)
  waiting for transfers between devices  62.8 us (26%)
  starting transfers between devices  45.4 us (19%)
  Pallas kernels  30.5 us (13%)
  between operations  14.2 us (6%)
  local copies, waits for them, and re-layouts  10.7 us (5%)
    all_to_all x3, blocking collectives, to_every(): return lax.all_to_all(copies, axis, split_axis=0, concat_axis=0, tiled=True)  71.3 us
    all_to_all x4, waiting for transfers between devices, to_every(): return lax.all_to_all(copies, axis, split_axis=0, concat_axis=0, tiled=True)  54.5 us
    all_to_all x4, starting transfers between devices, to_every(): return lax.all_to_all(copies, axis, split_axis=0, concat_axis=0, tiled=True)  36.1 us
    pallas_call x9, Pallas kernels, run(): pl.pallas_call(kernel, out_shape=[jax.ShapeDtypeStruct(*out) for out in o...  30.5 us
    ppermute x4, starting transfers between devices, beside(): return lax.ppermute(value, PCOL, pairs)  9.29 us
    ppermute x4, waiting for transfers between devices, beside(): return lax.ppermute(value, PCOL, pairs)  6.9 us
    unnamed x24, local copies, waits for them, and re-layouts  5.83 us
  transfers between devices with their start and end apart: 10, of which 6 were waited for; matrix products, arithmetic and copies ran while one was open for 2% of the time, Pallas kernels for 12%

profile of v1, /device:TPU:1, one launch (start us, length us, event | category | flops | bytes accessed | tf_op | source)
XLA Modules:
  0.0 235.6 jit_solution(15860521660095577232)
XLA Ops:
  10.4 16.3 %all-to-all-start = ((bf16[16,16,1280]{2,1,0:T(8,128)(2,1)}), bf16[16,16,1280]{2,1,0:T(8,128)(2,1)S(1)}, u32[]{:S(2)}, u32[]{:S(2)}) async-start(bf16[16,16,1280]{2,1,0:T(8,128)(2,1)} %broadcast_in_dim.3), calls=%async_computation | async-start | bytes 1310720 | tf_op jit(solution)/shard_map/all_to_all | solution.py:238
  26.7 21.0 %all-to-all-done = bf16[16,16,1280]{2,1,0:T(8,128)(2,1)S(1)} async-done(((bf16[16,16,1280]{2,1,0:T(8,128)(2,1)}), bf16[16,16,1280]{2,1,0:T(8,128)(2,1)S(1)}, u32[]{:S(2)}, u32[]{:S(2)}) %all-to-all-start) | async-done | bytes 655392 | tf_op jit(solution)/shard_map/all_to_all | solution.py:238
  48.5 2.3 stats0.1
  50.9 9.2 %all-to-all-start.1 = ((f32[32,1,128]{2,1,0:T(1,128)}), f32[32,1,128]{2,1,0:T(1,128)S(1)}, u32[]{:S(2)}, u32[]{:S(2)}) async-start(f32[32,1,128]{2,1,0:T(1,128)} %stats0.1), calls=%async_computation.1 | async-start | bytes 32768 | tf_op jit(solution)/shard_map/all_to_all | solution.py:238
  60.8 6.6 %all-to-all-done.1.sums_ref = f32[32,1,128]{2,1,0:T(1,128)S(1)} async-done(((f32[32,1,128]{2,1,0:T(1,128)}), f32[32,1,128]{2,1,0:T(1,128)S(1)}, u32[]{:S(2)}, u32[]{:S(2)}) %all-to-all-start.1) | async-done | bytes 16416 | tf_op jit(solution)/shard_map/all_to_all | solution.py:238
  68.0 4.1 %conv1.1 = (f32[80,256]{1,0:T(8,128)}, f32[80,64]{1,0:T(8,128)}, f32[80,64]{1,0:T(8,128)}, f32[80,256]{1,0:T(8,128)}) custom-call(s32[2]{0:T(128)} %pad_add_fusion.at_ref, bf16[256,1280]{1,0:T(8,128)(2,1)} %bitcast.14, f32[32,1,128]{2,1,0:T(1,128)} %copy-done.3, f32[3,1280]{1,0:T(4,128)} %scale_ref.1, f32[3,1280]{1,0:T(4,128)} %shift_ref.1, ...), custom_call_target="tpu_custom_call" | custom-call | tf_op jit(solution)/shard_map/conv1/pallas_call | solution.py:225
  72.1 2.7 %collective-permute-start = (f32[80,64]{1,0:T(8,128)}, f32[80,64]{1,0:T(8,128)S(1)}, u32[]{:S(2)}, u32[]{:S(2)}) collective-permute-start(f32[80,64]{1,0:T(8,128)} %get-tuple-element.13), channel_id=1, source_target_pairs={{0,1},{1,2},{2,3},{3,4},{4,5},{5,6},{6,7},{7,8},{8,9},{9,10},{10,1... | collective-permute-start | bytes 61448 | tf_op jit(solution)/shard_map/ppermute | solution.py:243
  77.4 3.0 %collective-permute-done.1.from_right_ref = f32[80,64]{1,0:T(8,128)S(1)} collective-permute-done((f32[80,64]{1,0:T(8,128)}, f32[80,64]{1,0:T(8,128)S(1)}, u32[]{:S(2)}, u32[]{:S(2)}) %collective-permute-start.1) | collective-permute-done | bytes 20512 | tf_op jit(solution)/shard_map/ppermute | solution.py:243
  81.0 2.0 finish1.1
  83.0 5.0 %all-to-all-start.2 = ((bf16[16,80,256]{2,1,0:T(8,128)(2,1)}), bf16[16,80,256]{2,1,0:T(8,128)(2,1)S(1)}, u32[]{:S(2)}, u32[]{:S(2)}) async-start(bf16[16,80,256]{2,1,0:T(8,128)(2,1)} %finish1.1), calls=%async_computation.2 | async-start | bytes 1310720 | tf_op jit(solution)/shard_map/all_to_all | solution.py:238
  88.0 20.8 %all-to-all-done.2 = bf16[16,80,256]{2,1,0:T(8,128)(2,1)S(1)} async-done(((bf16[16,80,256]{2,1,0:T(8,128)(2,1)}), bf16[16,80,256]{2,1,0:T(8,128)(2,1)S(1)}, u32[]{:S(2)}, u32[]{:S(2)}) %all-to-all-start.2) | async-done | bytes 655392 | tf_op jit(solution)/shard_map/all_to_all | solution.py:238
  109.7 2.0 stats1.1
  111.7 5.5 %all-to-all-start.3 = ((f32[32,1,128]{2,1,0:T(1,128)}), f32[32,1,128]{2,1,0:T(1,128)S(1)}, u32[]{:S(2)}, u32[]{:S(2)}) async-start(f32[32,1,128]{2,1,0:T(1,128)} %stats1.1), calls=%async_computation.3 | async-start | bytes 32768 | tf_op jit(solution)/shard_map/all_to_all | solution.py:238
  118.4 6.1 %all-to-all-done.3.sums_ref = f32[32,1,128]{2,1,0:T(1,128)S(1)} async-done(((f32[32,1,128]{2,1,0:T(1,128)}), f32[32,1,128]{2,1,0:T(1,128)S(1)}, u32[]{:S(2)}, u32[]{:S(2)}) %all-to-all-start.3) | async-done | bytes 16416 | tf_op jit(solution)/shard_map/all_to_all | solution.py:238
  125.1 4.3 %conv2.1 = (f32[80,256]{1,0:T(8,128)}, f32[80,64]{1,0:T(8,128)}, f32[80,64]{1,0:T(8,128)}) custom-call(bf16[1280,256]{1,0:T(8,128)(2,1)} %bitcast.16, f32[32,1,128]{2,1,0:T(1,128)} %copy-done.2, f32[1280,4]{1,0:T(8,128)} %bitcast.19, bf16[720,1280]{1,0:T(8,128)(2,1)} %bitcast.21), custom_call_target="tpu_custom_call" | custom-call | tf_op jit(solution)/shard_map/conv2/pallas_call | solution.py:225
  129.4 2.7 %collective-permute-start.2 = (f32[80,64]{1,0:T(8,128)}, f32[80,64]{1,0:T(8,128)S(1)}, u32[]{:S(2)}, u32[]{:S(2)}) collective-permute-start(f32[80,64]{1,0:T(8,128)} %get-tuple-element.16), channel_id=1, source_target_pairs={{0,1},{1,2},{2,3},{3,4},{4,5},{5,6},{6,7},{7,8},{8,9},{9,10},{10,1... | collective-permute-start | bytes 61448 | tf_op jit(solution)/shard_map/ppermute | solution.py:243
  134.1 3.9 %collective-permute-done.3.from_right_ref = f32[80,64]{1,0:T(8,128)S(1)} collective-permute-done((f32[80,64]{1,0:T(8,128)}, f32[80,64]{1,0:T(8,128)S(1)}, u32[]{:S(2)}, u32[]{:S(2)}) %collective-permute-start.3) | collective-permute-done | bytes 20512 | tf_op jit(solution)/shard_map/ppermute | solution.py:243
  138.6 2.0 finish2.1
  140.6 30.1 %all_to_all.35 = bf16[16,80,256]{2,1,0:T(8,128)(2,1)} all-to-all(bf16[16,80,256]{2,1,0:T(8,128)(2,1)} %finish2.1), channel_id=1, replica_groups=mesh['prow_0'=2,'prow_1'=8,'pcol_0'=4,'pcol_1'=4,'pcol_2'=2] {'prow_0','..., dimensions={0} | all-to-all | bytes 1310720 | tf_op jit(solution)/shard_map/all_to_all | solution.py:238
  170.8 2.0 stats2.1
  172.8 16.4 %all_to_all.36.sums_ref = f32[32,1,128]{2,1,0:T(1,128)} all-to-all(f32[32,1,128]{2,1,0:T(1,128)} %stats2.1), channel_id=1, replica_groups=mesh['prow_0'=2,'prow_1'=8,'pcol_0'=4,'pcol_1'=4,'pcol_2'=2] {'pcol_0','..., dimensions={0} | all-to-all | bytes 32768 | tf_op jit(solution)/shard_map/all_to_all | solution.py:238
  189.2 8.6 %attention.1 = (bf16[256,64]{1,0:T(8,128)(2,1)}, bf16[256,128]{1,0:T(8,128)(2,1)}, f32[16,1280]{1,0:T(8,128)}) custom-call(s32[2]{0:T(128)} %pad_add_fusion.at_ref, bf16[1280,256]{1,0:T(8,128)(2,1)} %bitcast.18, f32[32,1,128]{2,1,0:T(1,128)} %all_to_all.36.sums_ref, f32[1280,4]{1,0:T(8,128)} %bitcast.20, bf16[192,1280]{1,0:T(8,128)(2,1)} %w_ref.1, ...), custom_call_target="tpu_custom_call" | custom-call | tf_op jit(solution)/shard_map/attention/pallas_call | solution.py:225
  198.7 24.8 %all_to_all.37 = bf16[16,2,512]{2,1,0:T(2,128)(2,1)S(1)} all-to-all(bf16[16,2,512]{2,1,0:T(2,128)(2,1)S(1)} %reshape.44), channel_id=1, replica_groups=mesh['prow_0'=2,'prow_1'=8,'pcol_0'=4,'pcol_1'=4,'pcol_2'=2] {'prow_0','..., dimensions={0} | all-to-all | bytes 65536 | tf_op jit(solution)/shard_map/all_to_all | solution.py:238
  224.2 3.1 %output.1 = bf16[16,1280]{1,0:T(8,128)(2,1)} custom-call(bf16[16,16,64]{2,1,0:T(8,128)(2,1)} %reshape.45.att_ref, bf16[1280,1024]{1,0:T(8,128)(2,1)} %all-gather.5.cloned.1.call-done.w_ref, f32[16,1280]{1,0:T(8,128)} %get-tuple-element.20.own_ref), custom_call_target="tpu_custom_call" | custom-call | tf_op jit(solution)/shard_map/output/pallas_call | solution.py:225
  (42 shorter events, 16.7 us)
Async XLA Ops:
  7.2 182.0 %all-gather.3.cloned.1.call-start = ((), (), s32[]{:S(2)}) async-start(), calls=%async_computation.7 | async-start | bytes 2162688 | tf_op jit(solution)/shard_map/all_gather | solution.py:260
  7.9 216.3 %all-gather.5.cloned.1.call-start = ((), (), s32[]{:S(2)}) async-start(), calls=%async_computation.8 | async-start | bytes 2785280 | tf_op jit(solution)/shard_map/all_gather | solution.py:261
  10.4 66.4 %copy-start.10 = (f32[1280]{0:T(1024)S(1)}, f32[1280]{0:T(1024)}, u32[]{:S(2)}) copy-start(f32[1280]{0:T(1024)} %param.13) | copy-start | bytes 15364
  10.4 37.3 %all-to-all-start = ((bf16[16,16,1280]{2,1,0:T(8,128)(2,1)}), bf16[16,16,1280]{2,1,0:T(8,128)(2,1)S(1)}, u32[]{:S(2)}, u32[]{:S(2)}) async-start(bf16[16,16,1280]{2,1,0:T(8,128)(2,1)} %broadcast_in_dim.3), calls=%async_computation | async-start | bytes 1310720 | tf_op jit(solution)/shard_map/all_to_all | solution.py:238
  47.7 0.9 copy-start
  50.9 16.5 %all-to-all-start.1 = ((f32[32,1,128]{2,1,0:T(1,128)}), f32[32,1,128]{2,1,0:T(1,128)S(1)}, u32[]{:S(2)}, u32[]{:S(2)}) async-start(f32[32,1,128]{2,1,0:T(1,128)} %stats0.1), calls=%async_computation.1 | async-start | bytes 32768 | tf_op jit(solution)/shard_map/all_to_all | solution.py:238
  67.4 0.6 copy-start.3
  68.0 20.0 %copy-start.4 = (f32[3,1280]{1,0:T(4,128)S(1)}, f32[3,1280]{1,0:T(4,128)}, u32[]{:S(2)}) copy-start(f32[3,1280]{1,0:T(4,128)} %scale_ref.1) | copy-start | bytes 46084
  68.0 20.0 %copy-start.5 = (f32[3,1280]{1,0:T(4,128)S(1)}, f32[3,1280]{1,0:T(4,128)}, u32[]{:S(2)}) copy-start(f32[3,1280]{1,0:T(4,128)} %shift_ref.1) | copy-start | bytes 46084
  72.1 5.3 %collective-permute-start = (f32[80,64]{1,0:T(8,128)}, f32[80,64]{1,0:T(8,128)S(1)}, u32[]{:S(2)}, u32[]{:S(2)}) collective-permute-start(f32[80,64]{1,0:T(8,128)} %get-tuple-element.13), channel_id=1, source_target_pairs={{0,1},{1,2},{2,3},{3,4},{4,5},{5,6},{6,7},{7,8},{8,9},{9,10},{10,1... | collective-permute-start | bytes 61448 | tf_op jit(solution)/shard_map/ppermute | solution.py:243
  74.9 5.5 %collective-permute-start.1 = (f32[80,64]{1,0:T(8,128)}, f32[80,64]{1,0:T(8,128)S(1)}, u32[]{:S(2)}, u32[]{:S(2)}) collective-permute-start(f32[80,64]{1,0:T(8,128)} %get-tuple-element.14), channel_id=1, source_target_pairs={{1,0},{2,1},{3,2},{4,3},{5,4},{6,5},{7,6},{8,7},{9,8},{10,9},{11,1... | collective-permute-start | bytes 61448 | tf_op jit(solution)/shard_map/ppermute | solution.py:243
  77.4 3.0 %copy-start.7 = (f32[80,64]{1,0:T(8,128)}, f32[80,64]{1,0:T(8,128)S(1)}, u32[]{:S(2)}) copy-start(f32[80,64]{1,0:T(8,128)S(1)} %collective-permute-done.from_left_ref) | copy-start | bytes 61444
  80.4 0.6 copy-start.9
  83.0 25.8 %all-to-all-start.2 = ((bf16[16,80,256]{2,1,0:T(8,128)(2,1)}), bf16[16,80,256]{2,1,0:T(8,128)(2,1)S(1)}, u32[]{:S(2)}, u32[]{:S(2)}) async-start(bf16[16,80,256]{2,1,0:T(8,128)(2,1)} %finish1.1), calls=%async_computation.2 | async-start | bytes 1310720 | tf_op jit(solution)/shard_map/all_to_all | solution.py:238
  108.8 0.8 copy-start.1
  111.7 12.8 %all-to-all-start.3 = ((f32[32,1,128]{2,1,0:T(1,128)}), f32[32,1,128]{2,1,0:T(1,128)S(1)}, u32[]{:S(2)}, u32[]{:S(2)}) async-start(f32[32,1,128]{2,1,0:T(1,128)} %stats1.1), calls=%async_computation.3 | async-start | bytes 32768 | tf_op jit(solution)/shard_map/all_to_all | solution.py:238
  124.5 0.6 copy-start.2
  129.4 4.7 %collective-permute-start.2 = (f32[80,64]{1,0:T(8,128)}, f32[80,64]{1,0:T(8,128)S(1)}, u32[]{:S(2)}, u32[]{:S(2)}) collective-permute-start(f32[80,64]{1,0:T(8,128)} %get-tuple-element.16), channel_id=1, source_target_pairs={{0,1},{1,2},{2,3},{3,4},{4,5},{5,6},{6,7},{7,8},{8,9},{9,10},{10,1... | collective-permute-start | bytes 61448 | tf_op jit(solution)/shard_map/ppermute | solution.py:243
  132.1 5.8 %collective-permute-start.3 = (f32[80,64]{1,0:T(8,128)}, f32[80,64]{1,0:T(8,128)S(1)}, u32[]{:S(2)}, u32[]{:S(2)}) collective-permute-start(f32[80,64]{1,0:T(8,128)} %get-tuple-element.17), channel_id=1, source_target_pairs={{1,0},{2,1},{3,2},{4,3},{5,4},{6,5},{7,6},{8,7},{9,8},{10,9},{11,1... | collective-permute-start | bytes 61448 | tf_op jit(solution)/shard_map/ppermute | solution.py:243
  134.1 3.9 %copy-start.6 = (f32[80,64]{1,0:T(8,128)}, f32[80,64]{1,0:T(8,128)S(1)}, u32[]{:S(2)}) copy-start(f32[80,64]{1,0:T(8,128)S(1)} %collective-permute-done.2.from_left_ref) | copy-start | bytes 61444
  138.0 0.6 copy-start.8
Sparse Core Ops, SparseCore 0:
  10.1 76.3 all-gather.2
  89.7 121.8 all-gather.4

commit v2 on v1

v2 whole, which is shorter than its diff:
```python
import functools

import jax
import jax.numpy as jnp
from jax import lax
from jax.experimental import pallas as pl
from jax.experimental.pallas import tpu as pltpu
from jax.sharding import Mesh
from jax.sharding import PartitionSpec as P

GROUPS = 32
HEAD = 64
PROW = ("prow_0", "prow_1")
PCOL = ("pcol_0", "pcol_1", "pcol_2")
EPSILON = 1e-05
F32 = jnp.float32
BF16 = jnp.bfloat16

C = 1280
GC = C // GROUPS
NP = 16
NS = 32
LR = 64
PC = 4
CELLS = LR * PC
OC = C // NP
POPULATION = float(LR * PC * NS * GC)


def iota(shape, dim):
    return lax.broadcasted_iota(jnp.int32, shape, dim)


def one_hot(mask, dtype):
    return jnp.where(mask, 1.0, 0.0).astype(dtype)


def nt(left, right, precision=None):
    return lax.dot_general(
        left, right, (((1,), (1,)), ((), ())), precision=precision, preferred_element_type=F32
    )


def nn(left, right, precision=None):
    return lax.dot_general(
        left, right, (((1,), (0,)), ((), ())), precision=precision, preferred_element_type=F32
    )


def strip_order():
    o = iota((CELLS, CELLS), 0)
    i = iota((CELLS, CELLS), 1)
    return one_hot((o % LR) * PC + o // LR == i, BF16)


def cell_order():
    o = iota((CELLS, CELLS), 1)
    i = iota((CELLS, CELLS), 0)
    return one_hot((o % LR) * PC + o // LR == i, BF16)


ROWS = OC // 5 * C // 128
PIECE = 48
BLOCK = ROWS + PIECE


def moments(sums_ref):
    sums = jnp.sum(sums_ref[...], axis=0)
    mean = sums / POPULATION
    square = pltpu.roll(mean, 128 - GROUPS, 1)
    return mean, lax.rsqrt(jnp.maximum(square - mean * mean, 0.0) + EPSILON)


def silu(v):
    return v / (1.0 + jnp.exp(-v))


def pack_kernel(latent_ref, w_ref, out_ref):
    rows = [latent_ref[r].astype(F32) for r in range(PC)]
    patch = jnp.concatenate(rows, axis=0).astype(BF16)
    for j in range(C // 128):
        chunk = patch[:, 128 * j : 128 * (j + 1)]
        out_ref[:, NP * j : NP * (j + 1), :] = jnp.broadcast_to(chunk[None], (NP, NP, 128))
    lane = iota((PIECE, 128), 1)
    for k in range(NP // 2):
        w = w_ref[:, 128 * k : 128 * (k + 1)].astype(F32)
        turned = pltpu.roll(w, HEAD, 1)
        blank = jnp.zeros((2 * PIECE - OC, 128), F32)

        def halves(left, right):
            low = jnp.concatenate([right[PIECE:], blank], axis=0)
            return jnp.where(lane < HEAD, left[:PIECE], low).astype(BF16)

        out_ref[2 * k, ROWS:, :] = halves(w, turned)
        out_ref[2 * k + 1, ROWS:, :] = halves(turned, w)


def unpack_kernel(block_ref, out_ref):
    lane = iota((PIECE, 128), 1)
    for p in range(NP):
        piece = block_ref[p, ROWS:, :].astype(F32)
        high = jnp.where(lane >= HEAD, pltpu.roll(piece, HEAD, 1), 0.0)
        low = jnp.where(lane >= HEAD, piece, 0.0)
        both = jnp.concatenate([high, low[: OC - PIECE]], axis=0)
        out_ref[OC * p : OC * (p + 1), :] = both.astype(BF16)


def columns_kernel(at_ref, scale_ref, shift_ref, bias_ref, time_ref, out_ref):
    pick = iota((OC, C), 1) == iota((OC, C), 0) + at_ref[0] * OC
    lane = iota((OC, 128), 1)
    total = jnp.zeros((OC, 128), F32)
    rows = [
        bias_ref[0:1, :] + time_ref[...],
        scale_ref[1:2, :],
        shift_ref[1:2, :],
        bias_ref[1:2, :],
        scale_ref[2:3, :],
        shift_ref[2:3, :],
    ]
    for k, row in enumerate(rows):
        col = jnp.sum(jnp.where(pick, row, 0.0), axis=1, keepdims=True)
        total = jnp.where(lane == k, col, total)
    out_ref[...] = total


def stats_cells_kernel(block_ref, out_ref):
    firsts, seconds = [], []
    for j in range(C // 128):
        x = block_ref[:, NP * j : NP * (j + 1), :].astype(F32).reshape(CELLS, 128)
        firsts.append(jnp.sum(x, axis=0, keepdims=True))
        seconds.append(jnp.sum(x * x, axis=0, keepdims=True))
    first = jnp.concatenate(firsts, axis=1)
    second = jnp.concatenate(seconds, axis=1)
    both = jnp.concatenate([first, second, jnp.zeros((6, C), F32)], axis=0)
    groups = one_hot(iota((C, 128), 0) // GC == iota((C, 128), 1), F32)
    reduced = nn(both, groups, lax.Precision.HIGHEST)
    row = reduced[0:1, :] + pltpu.roll(reduced, GROUPS, 1)[1:2, :]
    out_ref[...] = jnp.broadcast_to(row[None], out_ref.shape)


def conv_combine(products, mid_ref, to_left_ref, to_right_ref):
    lane = iota((OC, CELLS), 1)
    row = lane % LR

    def tap(a, b):
        at = (3 * a + b) * OC
        return products[at : at + OC, :]

    def rows_summed(b):
        above = jnp.where(row > 0, pltpu.roll(tap(0, b), 1, 1), 0.0)
        below = jnp.where(row < LR - 1, pltpu.roll(tap(2, b), CELLS - 1, 1), 0.0)
        return tap(1, b) + above + below

    before = rows_summed(0)
    after = rows_summed(2)
    to_right_ref[...] = before[:, CELLS - LR :]
    to_left_ref[...] = after[:, :LR]
    mid_ref[...] = (
        rows_summed(1)
        + jnp.where(lane >= LR, pltpu.roll(before, LR, 1), 0.0)
        + jnp.where(lane < CELLS - LR, pltpu.roll(after, CELLS - LR, 1), 0.0)
    )


def conv_cells_kernel(
    at_ref, block_ref, sums_ref, scale_ref, shift_ref, w_ref, mid_ref, left_ref, right_ref, own_ref
):
    mean, rstd = moments(sums_ref)
    both = jnp.concatenate([mean, rstd, jnp.zeros((6, 128), F32)], axis=0)
    groups = one_hot(iota((128, C), 1) // GC == iota((128, C), 0), F32)
    spread = nn(both, groups, lax.Precision.HIGHEST)
    gain = spread[1:2, :] * scale_ref[0:1, :]
    offset = shift_ref[0:1, :] - spread[0:1, :] * gain
    chunks = [
        block_ref[:, NP * j : NP * (j + 1), :].reshape(CELLS, 128) for j in range(C // 128)
    ]
    cells = nn(strip_order(), jnp.concatenate(chunks, axis=1))
    pick = one_hot(iota((OC, C), 1) == iota((OC, C), 0) + at_ref[0] * OC, BF16)
    own_ref[...] = nt(pick, cells.astype(BF16))
    act = silu(cells * gain + offset).astype(BF16)
    conv_combine(nt(w_ref[...], act), mid_ref, left_ref, right_ref)


def conv_channels_kernel(x_ref, w_ref, mid_ref, left_ref, right_ref):
    conv_combine(nn(w_ref[...], x_ref[...]), mid_ref, left_ref, right_ref)


def whole(x):
    return jnp.sum(jnp.sum(x, axis=0, keepdims=True), axis=1, keepdims=True)


def finish_kernel(which, mid_ref, from_left_ref, from_right_ref, cols_ref, *refs):
    total_ref, sums_ref = refs[-2:]
    sides = jnp.concatenate(
        [from_left_ref[...], jnp.zeros((OC, CELLS - 2 * LR), F32), from_right_ref[...]], axis=1
    )
    total = mid_ref[...] + sides + cols_ref[:, 3 * which : 3 * which + 1]
    if which == 1:
        total = refs[0][...] + total
        total_ref[...] = total.astype(BF16)
        total = total.astype(BF16).astype(F32)
    else:
        total_ref[...] = total
    lane = iota((1, 128), 1)
    row = jnp.zeros((1, 128), F32)
    for k in range(2):
        half = total[GC * k : GC * (k + 1)]
        row = jnp.where(lane == k, whole(half), row)
        row = jnp.where(lane == k + GROUPS, whole(half * half), row)
    sums_ref[...] = jnp.broadcast_to(row[None], sums_ref.shape)


def norm_kernel(which, total_ref, sums_ref, cols_ref, out_ref):
    mean, rstd = moments(sums_ref)
    upper = iota((OC, 1), 0) < GC
    gain = jnp.where(upper, rstd[:, 0:1], rstd[:, 1:2]) * cols_ref[:, 3 * which + 1 : 3 * which + 2]
    shift = cols_ref[:, 3 * which + 2 : 3 * which + 3]
    offset = shift - jnp.where(upper, mean[:, 0:1], mean[:, 1:2]) * gain
    value = total_ref[...].astype(F32) * gain + offset
    if which == 0:
        value = silu(value)
    out_ref[...] = jnp.broadcast_to(value.astype(BF16)[None], out_ref.shape)


def attention_kernel(at_ref, x_ref, w_ref, pairs_ref, w_out_ref, own_ref, part_ref, fresh_ref):
    mapped = nn(w_ref[...], x_ref[...])
    queries = jnp.transpose(mapped[:HEAD]).astype(BF16)
    fresh = jnp.transpose(mapped[HEAD:]).astype(BF16)
    queries = (queries.astype(F32) * HEAD ** (-0.5)).astype(BF16)
    queries = jnp.concatenate([queries, jnp.zeros((CELLS, HEAD), BF16)], axis=1)
    order = cell_order()
    fresh_ref[...] = nn(order, fresh).astype(BF16)
    chunk = 4
    highest = jnp.full((CELLS, 1), -jnp.inf, F32)
    denominator = jnp.zeros((CELLS, 1), F32)
    weighted = jnp.zeros((CELLS, 2 * HEAD), F32)
    for step in range(NS // chunk):
        blocks = []
        for k in range(chunk):
            strip = chunk * step + k
            blocks.append(jnp.where(at_ref[1] == strip, fresh, pairs_ref[strip]))
        pairs = jnp.concatenate(blocks, axis=0)
        scores = nt(queries, pairs)
        raised = jnp.maximum(highest, jnp.max(scores, axis=1, keepdims=True))
        factor = jnp.exp(highest - raised)
        weights = jnp.exp(scores - raised)
        denominator = denominator * factor + jnp.sum(weights, axis=1, keepdims=True)
        weighted = weighted * factor + nn(weights.astype(BF16), pairs)
        highest = raised
    attended = nn(order, (weighted / denominator).astype(BF16)).astype(BF16)
    own = nt(order, own_ref[...]).astype(BF16)
    pick = one_hot(iota((OC, C), 1) == iota((OC, C), 0) + at_ref[0] * OC, BF16)
    part = nt(attended, w_out_ref[...]) + nn(own, pick)
    part_ref[...] = part.astype(BF16).reshape(part_ref.shape)


def output_kernel(parts_ref, out_ref):
    total = jnp.sum(parts_ref[...].astype(F32), axis=0)
    for r in range(PC):
        out_ref[r] = total[PC * r : PC * (r + 1), :].astype(BF16)


def call(kernel, name, outs, scalars=0, mib=16):
    def run(*args):
        specs = [pl.BlockSpec(memory_space=pltpu.SMEM)] * scalars
        specs += [pl.BlockSpec(memory_space=pltpu.VMEM)] * (len(args) - scalars)
        return pl.pallas_call(
            kernel,
            out_shape=[jax.ShapeDtypeStruct(*out) for out in outs],
            in_specs=specs,
            out_specs=[pl.BlockSpec(memory_space=pltpu.VMEM)] * len(outs),
            compiler_params=pltpu.CompilerParams(vmem_limit_bytes=mib * 2**20),
            name=name,
        )(*args)

    return run


def to_every(copies, axis):
    return lax.all_to_all(copies, axis, split_axis=0, concat_axis=0, tiled=True)


def beside(value, step):
    pairs = [(i, i + step) for i in range(NS) if 0 <= i + step < NS]
    return lax.ppermute(value, PCOL, pairs)


def shards(
    latent,
    norm_scale,
    norm_shift,
    time_shift,
    conv_bias,
    conv_one,
    conv_two,
    w_qkv,
    w_out,
    stale_kv,
):
    depth, line, core = (lax.axis_index(axis) for axis in PCOL)
    at = jnp.stack([lax.axis_index(PROW), core * 16 + line * 4 + depth]).astype(jnp.int32)
    pairs = stale_kv.reshape(CELLS, 2 * HEAD)
    for axis in PCOL:
        pairs = lax.all_gather(pairs, axis, axis=0)
    pairs = pairs.reshape(NS, CELLS, 2 * HEAD)
    sums_out = ((NS, 1, 128), F32)
    every = ((NP, OC, CELLS), BF16)
    conv_out = [((OC, CELLS), F32), ((OC, LR), F32), ((OC, LR), F32)]
    (cols,) = call(columns_kernel, "columns", [((OC, 128), F32)], scalars=1)(
        at, norm_scale, norm_shift, conv_bias, time_shift.reshape(1, C)
    )

    def finish(which, mid, left, right, *more):
        kind = (F32, BF16)[which]
        total, sums = call(
            functools.partial(finish_kernel, which),
            f"finish{which}",
            [((OC, CELLS), kind), sums_out],
        )(mid, beside(right, 1), beside(left, -1), cols, *more)
        (copies,) = call(functools.partial(norm_kernel, which), f"norm{which}", [every])(
            total, to_every(sums, PCOL), cols
        )
        return total, to_every(copies, PROW).reshape(C, CELLS)

    (block,) = call(pack_kernel, "pack", [((NP, BLOCK, 128), BF16)])(latent, w_out)
    block = to_every(block, PROW)
    (sums,) = call(stats_cells_kernel, "stats", [sums_out])(block)
    sums = to_every(sums, PCOL)
    (w_part,) = call(unpack_kernel, "unpack", [((C, 128), BF16)])(block)
    mid, left, right, own = call(
        conv_cells_kernel, "conv1", conv_out + [((OC, CELLS), F32)], scalars=1
    )(at, block, sums, norm_scale, norm_shift, conv_one.reshape(9 * OC, C))
    _, field = finish(0, mid, left, right)
    mid, left, right = call(conv_channels_kernel, "conv2", conv_out)(
        field, conv_two.reshape(9 * OC, C)
    )
    resnet, field = finish(1, mid, left, right, own)
    parts, fresh = call(
        attention_kernel,
        "attention",
        [((NP, NP, C), BF16), ((CELLS, 2 * HEAD), BF16)],
        scalars=1,
        mib=32,
    )(at, field, w_qkv, pairs, w_part, resnet)
    (out,) = call(output_kernel, "output", [((PC, PC, C), BF16)])(to_every(parts, PROW))
    return out, fresh.reshape(LR, PC, 1, 2 * HEAD)


def solution(mesh):
    torus = Mesh(
        mesh.devices.reshape(2, 8, 4, 4, 2), ("prow_0", "prow_1", "pcol_0", "pcol_1", "pcol_2")
    )
    in_specs = (
        P(PROW, PCOL, None),
        P(),
        P(),
        P(),
        P(),
        P(None, None, PROW, None),
        P(None, None, PROW, None),
        P(PROW, None),
        P(PROW, None),
        P(None, PCOL, PROW, None),
    )
    out_specs = (P(PROW, PCOL, None), P(None, PCOL, PROW, None))
    return jax.shard_map(
        shards, mesh=torus, in_specs=in_specs, out_specs=out_specs, check_vma=False
    )
```

time: 237 us -> 226 us (0.954)
  Pallas kernels: 30.5 us -> 15.4 us
  blocking collectives: 71.3 us -> 81.1 us
  starting transfers between devices: 45.4 us -> 53.7 us
  local copies, waits for them, and re-layouts: 10.7 us -> 3.32 us
  waiting for transfers between devices: 62.8 us -> 55.8 us
    all_gather x0 -> x1, blocking collectives: none -> 27.8 us  [shards(): pairs = lax.all_gather(pairs, axis, axis=0)]
    all_to_all x3, blocking collectives: 71.3 us -> 53.3 us  [to_every(): return lax.all_to_all(copies, axis, split_axis=0, concat_axis=0, tiled=True)]
    pallas_call x9 -> x12, Pallas kernels: 30.5 us -> 15.4 us  [run(): pl.pallas_call(kernel, out_shape=[jax.ShapeDtypeStruct(*out) for out in o...]
    all_to_all x4, starting transfers between devices: 36.1 us -> 42.6 us  [to_every(): return lax.all_to_all(copies, axis, split_axis=0, concat_axis=0, tiled=True)]
    all_to_all x4, waiting for transfers between devices: 54.5 us -> 48.2 us  [to_every(): return lax.all_to_all(copies, axis, split_axis=0, concat_axis=0, tiled=True)]
    unnamed x24 -> x22, local copies, waits for them, and re-layouts: 5.83 us -> 3.32 us
  transfers between devices with their start and end apart: 10 -> 10, of which waited for: 6 -> 5; matrix products, arithmetic and copies ran while one was open for 2% -> 0% of each run, Pallas kernels for 12% -> 4%
where the time goes in v2:
time: 226 us; the launch traced here: 224 us
  blocking collectives  81.1 us (36%)
  waiting for transfers between devices  55.8 us (25%)
  starting transfers between devices  53.7 us (24%)
  Pallas kernels  15.4 us (7%)
  between operations  14.3 us (6%)
  local copies, waits for them, and re-layouts  3.32 us (1%)
    all_to_all x3, blocking collectives, to_every(): return lax.all_to_all(copies, axis, split_axis=0, concat_axis=0, tiled=True)  53.3 us
    all_to_all x4, waiting for transfers between devices, to_every(): return lax.all_to_all(copies, axis, split_axis=0, concat_axis=0, tiled=True)  48.2 us
    all_to_all x4, starting transfers between devices, to_every(): return lax.all_to_all(copies, axis, split_axis=0, concat_axis=0, tiled=True)  42.6 us
    all_gather x1, blocking collectives, shards(): pairs = lax.all_gather(pairs, axis, axis=0)  27.8 us
    pallas_call x12, Pallas kernels, run(): pl.pallas_call(kernel, out_shape=[jax.ShapeDtypeStruct(*out) for out in o...  15.4 us
    ppermute x4, starting transfers between devices, beside(): return lax.ppermute(value, PCOL, pairs)  11 us
    ppermute x4, waiting for transfers between devices, beside(): return lax.ppermute(value, PCOL, pairs)  6.8 us
  transfers between devices with their start and end apart: 10, of which 5 were waited for; matrix products, arithmetic and copies ran while one was open for 0% of the time, Pallas kernels for 4%

profile of v2, /device:TPU:1, one launch (start us, length us, event | category | flops | bytes accessed | tf_op | source)
XLA Modules:
  0.0 223.6 jit_solution(15619155007369688782)
XLA Ops:
  8.9 1.0 pack.1
  9.9 16.3 %all-to-all-start = ((bf16[16,208,128]{2,1,0:T(8,128)(2,1)}), bf16[16,208,128]{2,1,0:T(8,128)(2,1)S(1)}, u32[]{:S(2)}, u32[]{:S(2)}) async-start(bf16[16,208,128]{2,1,0:T(8,128)(2,1)} %pack.1), calls=%async_computation | async-start | bytes 1703936 | tf_op jit(solution)/shard_map/all_to_all | solution.py:280
  26.3 27.8 %all_gather.15 = bf16[4,256,128]{2,1,0:T(8,128)(2,1)} all-gather(bf16[1,256,128]{2,1,0:T(8,128)(2,1)S(1)} %bitcast.18), channel_id=1, replica_groups=mesh['prow_0'=2,'prow_1'=8,'pcol_0'=4,'pcol_1'=4,'pcol_2'=2] {'pcol_0'}, dimensions={0}, use_global_device_ids=true | all-gather | bytes 327680 | tf_op jit(solution)/shard_map/all_gather | solution.py:304
  54.1 1.4 stats.1
  55.5 8.6 %all-to-all-start.1 = ((f32[32,1,128]{2,1,0:T(1,128)}), f32[32,1,128]{2,1,0:T(1,128)S(1)}, u32[]{:S(2)}, u32[]{:S(2)}) async-start(f32[32,1,128]{2,1,0:T(1,128)} %stats.1), calls=%async_computation.1 | async-start | bytes 32768 | tf_op jit(solution)/shard_map/all_to_all | solution.py:280
  64.2 7.2 %all-to-all-done.1.sums_ref = f32[32,1,128]{2,1,0:T(1,128)S(1)} async-done(((f32[32,1,128]{2,1,0:T(1,128)}), f32[32,1,128]{2,1,0:T(1,128)S(1)}, u32[]{:S(2)}, u32[]{:S(2)}) %all-to-all-start.1) | async-done | bytes 16416 | tf_op jit(solution)/shard_map/all_to_all | solution.py:280
  71.4 2.3 %conv1.1 = (f32[80,256]{1,0:T(8,128)S(1)}, f32[80,64]{1,0:T(8,128)S(1)}, f32[80,64]{1,0:T(8,128)S(1)}, f32[80,256]{1,0:T(8,128)S(1)}) custom-call(s32[2]{0:T(128)S(1)} %pad_add_fusion.at_ref, bf16[16,208,128]{2,1,0:T(8,128)(2,1)S(1)} %all-to-all-done.block_ref, f32[32,1,128]{2,1,0:T(1,128)S(1)} %all-to-all-done.1.sums_ref, f32[3,1280]{1,0:T(4,128)S(1)} %copy-done.5, ...), custom_call_target="tpu_custom_call" | custom-call | tf_op jit(solution)/shard_map/conv1/pallas_call | solution.py:267
  73.6 2.9 %collective-permute-start = (f32[80,64]{1,0:T(8,128)S(1)}, f32[80,64]{1,0:T(8,128)S(1)}, u32[]{:S(2)}, u32[]{:S(2)}) collective-permute-start(f32[80,64]{1,0:T(8,128)S(1)} %get-tuple-element.16), channel_id=1, source_target_pairs={{0,1},{1,2},{2,3},{3,4},{4,5},{5,6},{6,7},{7,8},{8,9},{9,10},{10,1... | collective-permute-start | bytes 61448 | tf_op jit(solution)/shard_map/ppermute | solution.py:285
  76.5 1.9 collective-permute-start.1
  79.4 3.4 %collective-permute-done.1.from_right_ref = f32[80,64]{1,0:T(8,128)S(1)} collective-permute-done((f32[80,64]{1,0:T(8,128)S(1)}, f32[80,64]{1,0:T(8,128)S(1)}, u32[]{:S(2)}, u32[]{:S(2)}) %collective-permute-start.1) | collective-permute-done | bytes 20512 | tf_op jit(solution)/shard_map/ppermute | solution.py:285
  83.0 12.6 %all_to_all.35.sums_ref = f32[32,1,128]{2,1,0:T(1,128)S(1)} all-to-all(f32[32,1,128]{2,1,0:T(1,128)S(1)} %get-tuple-element.19), channel_id=1, replica_groups=mesh['prow_0'=2,'prow_1'=8,'pcol_0'=4,'pcol_1'=4,'pcol_2'=2] {'pcol_0','..., dimensions={0} | all-to-all | bytes 32768 | tf_op jit(solution)/shard_map/all_to_all | solution.py:280
  95.6 1.2 norm0.1
  96.8 12.5 %all-to-all-start.3 = ((bf16[16,80,256]{2,1,0:T(8,128)(2,1)}), bf16[16,80,256]{2,1,0:T(8,128)(2,1)S(1)}, u32[]{:S(2)}, u32[]{:S(2)}) async-start(bf16[16,80,256]{2,1,0:T(8,128)(2,1)} %norm0.1), calls=%async_computation.3 | async-start | bytes 1310720 | tf_op jit(solution)/shard_map/all_to_all | solution.py:280
  110.0 20.2 %all-to-all-done.3 = bf16[16,80,256]{2,1,0:T(8,128)(2,1)S(1)} async-done(((bf16[16,80,256]{2,1,0:T(8,128)(2,1)}), bf16[16,80,256]{2,1,0:T(8,128)(2,1)S(1)}, u32[]{:S(2)}, u32[]{:S(2)}) %all-to-all-start.3) | async-done | bytes 655392 | tf_op jit(solution)/shard_map/all_to_all | solution.py:280
  131.1 4.3 %collective-permute-start.2 = (f32[80,64]{1,0:T(8,128)S(1)}, f32[80,64]{1,0:T(8,128)S(1)}, u32[]{:S(2)}, u32[]{:S(2)}) collective-permute-start(f32[80,64]{1,0:T(8,128)S(1)} %get-tuple-element.21), channel_id=1, source_target_pairs={{0,1},{1,2},{2,3},{3,4},{4,5},{5,6},{6,7},{7,8},{8,9},{9,10},{10,1... | collective-permute-start | bytes 61448 | tf_op jit(solution)/shard_map/ppermute | solution.py:285
  135.4 1.9 collective-permute-start.3
  137.3 3.4 %collective-permute-done.3.from_right_ref = f32[80,64]{1,0:T(8,128)S(1)} collective-permute-done((f32[80,64]{1,0:T(8,128)S(1)}, f32[80,64]{1,0:T(8,128)S(1)}, u32[]{:S(2)}, u32[]{:S(2)}) %collective-permute-start.3) | collective-permute-done | bytes 20512 | tf_op jit(solution)/shard_map/ppermute | solution.py:285
  140.9 13.7 %all_to_all.36.sums_ref = f32[32,1,128]{2,1,0:T(1,128)S(1)} all-to-all(f32[32,1,128]{2,1,0:T(1,128)S(1)} %get-tuple-element.25), channel_id=1, replica_groups=mesh['prow_0'=2,'prow_1'=8,'pcol_0'=4,'pcol_1'=4,'pcol_2'=2] {'pcol_0','..., dimensions={0} | all-to-all | bytes 32768 | tf_op jit(solution)/shard_map/all_to_all | solution.py:280
  154.6 1.2 norm1.1
  155.7 5.2 %all-to-all-start.5 = ((bf16[16,80,256]{2,1,0:T(8,128)(2,1)}), bf16[16,80,256]{2,1,0:T(8,128)(2,1)S(1)}, u32[]{:S(2)}, u32[]{:S(2)}) async-start(bf16[16,80,256]{2,1,0:T(8,128)(2,1)} %norm1.1), calls=%async_computation.5 | async-start | bytes 1310720 | tf_op jit(solution)/shard_map/all_to_all | solution.py:280
  161.1 20.8 %all-to-all-done.5 = bf16[16,80,256]{2,1,0:T(8,128)(2,1)S(1)} async-done(((bf16[16,80,256]{2,1,0:T(8,128)(2,1)}), bf16[16,80,256]{2,1,0:T(8,128)(2,1)S(1)}, u32[]{:S(2)}, u32[]{:S(2)}) %all-to-all-start.5) | async-done | bytes 655392 | tf_op jit(solution)/shard_map/all_to_all | solution.py:280
  182.0 1.6 copy-done
  183.5 5.5 %attention.1 = (bf16[16,16,1280]{2,1,0:T(8,128)(2,1)S(1)}, bf16[256,128]{1,0:T(8,128)(2,1)}) custom-call(s32[2]{0:T(128)S(1)} %pad_add_fusion.at_ref, bf16[1280,256]{1,0:T(8,128)(2,1)S(1)} %bitcast.13, bf16[192,1280]{1,0:T(8,128)(2,1)S(1)} %copy-done.3, bf16[32,256,128]{2,1,0:T(8,128)(2,1)S(1)} %bitcast.14, bf16[1280,128]{1,0:T(8,128)(2,1)S(1)} %unpack.1.w_out_ref, ...), custom_call_target="tpu_custom_call" | custom-call | tf_op jit(solution)/shard_map/attention/pallas_call | solution.py:267
  189.1 27.0 %all_to_all.37.parts_ref = bf16[16,16,1280]{2,1,0:T(8,128)(2,1)S(1)} all-to-all(bf16[16,16,1280]{2,1,0:T(8,128)(2,1)S(1)} %get-tuple-element.26), channel_id=1, replica_groups=mesh['prow_0'=2,'prow_1'=8,'pcol_0'=4,'pcol_1'=4,'pcol_2'=2] {'prow_0','..., dimensions={0} | all-to-all | bytes 1310720 | tf_op jit(solution)/shard_map/all_to_all | solution.py:280
  (38 shorter events, 5.5 us)
Async XLA Ops:
  7.2 0.9 copy-start.4
  8.1 0.8 copy-start.7
  8.9 17.4 %copy-start.9 = (bf16[64,4,1,128]{3,1,2,0:T(4,128)(2,1)S(1)}, bf16[64,4,1,128]{3,1,2,0:T(4,128)(2,1)}, u32[]{:S(2)}) copy-start(bf16[64,4,1,128]{3,1,2,0:T(4,128)(2,1)} %param.19) | copy-start | bytes 196612
  9.9 61.5 %copy-start.2 = (bf16[3,3,80,1280]{3,2,1,0:T(8,128)(2,1)S(1)}, bf16[3,3,80,1280]{3,2,1,0:T(8,128)(2,1)}, u32[]{:S(2)}) copy-start(bf16[3,3,80,1280]{3,2,1,0:T(8,128)(2,1)} %param.15) | copy-start | bytes 5529604
  9.9 61.5 %copy-start.5 = (f32[3,1280]{1,0:T(4,128)S(1)}, f32[3,1280]{1,0:T(4,128)}, u32[]{:S(2)}) copy-start(f32[3,1280]{1,0:T(4,128)} %scale_ref.3) | copy-start | bytes 46084
  9.9 61.5 %copy-start.6 = (f32[3,1280]{1,0:T(4,128)S(1)}, f32[3,1280]{1,0:T(4,128)}, u32[]{:S(2)}) copy-start(f32[3,1280]{1,0:T(4,128)} %shift_ref.3) | copy-start | bytes 46084
  9.9 44.2 %all-to-all-start = ((bf16[16,208,128]{2,1,0:T(8,128)(2,1)}), bf16[16,208,128]{2,1,0:T(8,128)(2,1)S(1)}, u32[]{:S(2)}, u32[]{:S(2)}) async-start(bf16[16,208,128]{2,1,0:T(8,128)(2,1)} %pack.1), calls=%async_computation | async-start | bytes 1703936 | tf_op jit(solution)/shard_map/all_to_all | solution.py:280
  26.2 83.1 %all-gather.5.cloned.1.call-start = ((), (), s32[]{:S(2)}) async-start(), calls=%async_computation.7 | async-start | bytes 1310720 | tf_op jit(solution)/shard_map/all_gather | solution.py:304
  54.1 24.3 %copy-start.10 = (f32[1280]{0:T(1024)S(1)}, f32[1280]{0:T(1024)}, u32[]{:S(2)}) copy-start(f32[1280]{0:T(1024)} %param.13) | copy-start | bytes 15364
  54.1 24.4 %copy-start.8 = (f32[2,1280]{1,0:T(2,128)S(1)}, f32[2,1280]{1,0:T(2,128)}, u32[]{:S(2)}) copy-start(f32[2,1280]{1,0:T(2,128)} %bias_ref.1) | copy-start | bytes 30724
  55.5 15.9 %all-to-all-start.1 = ((f32[32,1,128]{2,1,0:T(1,128)}), f32[32,1,128]{2,1,0:T(1,128)S(1)}, u32[]{:S(2)}, u32[]{:S(2)}) async-start(f32[32,1,128]{2,1,0:T(1,128)} %stats.1), calls=%async_computation.1 | async-start | bytes 32768 | tf_op jit(solution)/shard_map/all_to_all | solution.py:280
  73.6 56.6 %copy-start.1 = (bf16[3,3,80,1280]{3,2,1,0:T(8,128)(2,1)S(1)}, bf16[3,3,80,1280]{3,2,1,0:T(8,128)(2,1)}, u32[]{:S(2)}) copy-start(bf16[3,3,80,1280]{3,2,1,0:T(8,128)(2,1)} %param.16) | copy-start | bytes 5529604
  73.6 5.7 %collective-permute-start = (f32[80,64]{1,0:T(8,128)S(1)}, f32[80,64]{1,0:T(8,128)S(1)}, u32[]{:S(2)}, u32[]{:S(2)}) collective-permute-start(f32[80,64]{1,0:T(8,128)S(1)} %get-tuple-element.16), channel_id=1, source_target_pairs={{0,1},{1,2},{2,3},{3,4},{4,5},{5,6},{6,7},{7,8},{8,9},{9,10},{10,1... | collective-permute-start | bytes 61448 | tf_op jit(solution)/shard_map/ppermute | solution.py:285
  76.5 6.3 %collective-permute-start.1 = (f32[80,64]{1,0:T(8,128)S(1)}, f32[80,64]{1,0:T(8,128)S(1)}, u32[]{:S(2)}, u32[]{:S(2)}) collective-permute-start(f32[80,64]{1,0:T(8,128)S(1)} %get-tuple-element.17), channel_id=1, source_target_pairs={{1,0},{2,1},{3,2},{4,3},{5,4},{6,5},{7,6},{8,7},{9,8},{10,9},{11,1... | collective-permute-start | bytes 61448 | tf_op jit(solution)/shard_map/ppermute | solution.py:285
  96.8 33.5 %all-to-all-start.3 = ((bf16[16,80,256]{2,1,0:T(8,128)(2,1)}), bf16[16,80,256]{2,1,0:T(8,128)(2,1)S(1)}, u32[]{:S(2)}, u32[]{:S(2)}) async-start(bf16[16,80,256]{2,1,0:T(8,128)(2,1)} %norm0.1), calls=%async_computation.3 | async-start | bytes 1310720 | tf_op jit(solution)/shard_map/all_to_all | solution.py:280
  109.3 51.8 %all-gather.7.cloned.1.call-start = ((), (), s32[]{:S(2)}) async-start(), calls=%async_computation.8 | async-start | bytes 3145728 | tf_op jit(solution)/shard_map/all_gather | solution.py:304
  131.1 50.9 %copy-start.3 = (bf16[192,1280]{1,0:T(8,128)(2,1)S(1)}, bf16[192,1280]{1,0:T(8,128)(2,1)}, u32[]{:S(2)}) copy-start(bf16[192,1280]{1,0:T(8,128)(2,1)} %w_ref.3) | copy-start | bytes 1474564
  131.1 6.2 %collective-permute-start.2 = (f32[80,64]{1,0:T(8,128)S(1)}, f32[80,64]{1,0:T(8,128)S(1)}, u32[]{:S(2)}, u32[]{:S(2)}) collective-permute-start(f32[80,64]{1,0:T(8,128)S(1)} %get-tuple-element.21), channel_id=1, source_target_pairs={{0,1},{1,2},{2,3},{3,4},{4,5},{5,6},{6,7},{7,8},{8,9},{9,10},{10,1... | collective-permute-start | bytes 61448 | tf_op jit(solution)/shard_map/ppermute | solution.py:285
  135.4 5.3 %collective-permute-start.3 = (f32[80,64]{1,0:T(8,128)S(1)}, f32[80,64]{1,0:T(8,128)S(1)}, u32[]{:S(2)}, u32[]{:S(2)}) collective-permute-start(f32[80,64]{1,0:T(8,128)S(1)} %get-tuple-element.22), channel_id=1, source_target_pairs={{1,0},{2,1},{3,2},{4,3},{5,4},{6,5},{7,6},{8,7},{9,8},{10,9},{11,1... | collective-permute-start | bytes 61448 | tf_op jit(solution)/shard_map/ppermute | solution.py:285
  155.7 26.2 %all-to-all-start.5 = ((bf16[16,80,256]{2,1,0:T(8,128)(2,1)}), bf16[16,80,256]{2,1,0:T(8,128)(2,1)S(1)}, u32[]{:S(2)}, u32[]{:S(2)}) async-start(bf16[16,80,256]{2,1,0:T(8,128)(2,1)} %norm1.1), calls=%async_computation.5 | async-start | bytes 1310720 | tf_op jit(solution)/shard_map/all_to_all | solution.py:280
  181.9 1.6 copy-start
Sparse Core Ops, SparseCore 0:
  54.2 30.9 all-gather.4
  112.2 19.5 all-gather.6

commit v3 on v2

--- a/solution.py
+++ b/solution.py
@@ -12,6 +12,7 @@
 HEAD = 64
 PROW = ("prow_0", "prow_1")
 PCOL = ("pcol_0", "pcol_1", "pcol_2")
+HOPS = (("pcol_0", 1), ("pcol_0", 2), ("pcol_1", 1), ("pcol_1", 2), ("pcol_2", 1))
 EPSILON = 1e-05
 F32 = jnp.float32
 BF16 = jnp.bfloat16
@@ -222,7 +223,15 @@
     out_ref[...] = jnp.broadcast_to(value.astype(BF16)[None], out_ref.shape)
 
 
-def attention_kernel(at_ref, x_ref, w_ref, pairs_ref, w_out_ref, own_ref, part_ref, fresh_ref):
+def join_kernel(left_ref, right_ref, out_ref):
+    count = left_ref.shape[0]
+    out_ref[:count] = left_ref[...]
+    out_ref[count:] = right_ref[...]
+
+
+def attention_kernel(
+    at_ref, x_ref, w_ref, near_ref, far_ref, w_out_ref, own_ref, part_ref, fresh_ref
+):
     mapped = nn(w_ref[...], x_ref[...])
     queries = jnp.transpose(mapped[:HEAD]).astype(BF16)
     fresh = jnp.transpose(mapped[HEAD:]).astype(BF16)
@@ -235,11 +244,11 @@
     denominator = jnp.zeros((CELLS, 1), F32)
     weighted = jnp.zeros((CELLS, 2 * HEAD), F32)
     for step in range(NS // chunk):
-        blocks = []
-        for k in range(chunk):
-            strip = chunk * step + k
-            blocks.append(jnp.where(at_ref[1] == strip, fresh, pairs_ref[strip]))
-        pairs = jnp.concatenate(blocks, axis=0)
+        half = (near_ref, far_ref)[step // (NS // chunk // 2)]
+        start = chunk * step % (NS // 2)
+        pairs = half[start : start + chunk].reshape(chunk * CELLS, 2 * HEAD)
+        if step == 0:
+            pairs = jnp.concatenate([fresh, pairs[CELLS:]], axis=0)
         scores = nt(queries, pairs)
         raised = jnp.maximum(highest, jnp.max(scores, axis=1, keepdims=True))
         factor = jnp.exp(highest - raised)
@@ -260,7 +269,7 @@
         out_ref[r] = total[PC * r : PC * (r + 1), :].astype(BF16)
 
 
-def call(kernel, name, outs, scalars=0, mib=16):
+def call(kernel, outs, scalars=0, mib=8):
     def run(*args):
         specs = [pl.BlockSpec(memory_space=pltpu.SMEM)] * scalars
         specs += [pl.BlockSpec(memory_space=pltpu.VMEM)] * (len(args) - scalars)
@@ -270,7 +279,6 @@
             in_specs=specs,
             out_specs=[pl.BlockSpec(memory_space=pltpu.VMEM)] * len(outs),
             compiler_params=pltpu.CompilerParams(vmem_limit_bytes=mib * 2**20),
-            name=name,
         )(*args)
 
     return run
@@ -297,52 +305,46 @@
     w_out,
     stale_kv,
 ):
-    depth, line, core = (lax.axis_index(axis) for axis in PCOL)
-    at = jnp.stack([lax.axis_index(PROW), core * 16 + line * 4 + depth]).astype(jnp.int32)
-    pairs = stale_kv.reshape(CELLS, 2 * HEAD)
-    for axis in PCOL:
-        pairs = lax.all_gather(pairs, axis, axis=0)
-    pairs = pairs.reshape(NS, CELLS, 2 * HEAD)
+    at = lax.axis_index(PROW).astype(jnp.int32).reshape(1)
+    near = stale_kv.reshape(1, CELLS, 2 * HEAD)
+    for step, (axis, bit) in enumerate(HOPS):
+        count = lax.axis_size(axis)
+        far = lax.ppermute(near, axis, [(i, i ^ bit) for i in range(count)])
+        if step < len(HOPS) - 1:
+            out = ((2 * near.shape[0], CELLS, 2 * HEAD), BF16)
+            (near,) = call(join_kernel, [out])(near, far)
     sums_out = ((NS, 1, 128), F32)
     every = ((NP, OC, CELLS), BF16)
     conv_out = [((OC, CELLS), F32), ((OC, LR), F32), ((OC, LR), F32)]
-    (cols,) = call(columns_kernel, "columns", [((OC, 128), F32)], scalars=1)(
+    (cols,) = call(columns_kernel, [((OC, 128), F32)], scalars=1)(
         at, norm_scale, norm_shift, conv_bias, time_shift.reshape(1, C)
     )
 
     def finish(which, mid, left, right, *more):
         kind = (F32, BF16)[which]
         total, sums = call(
-            functools.partial(finish_kernel, which),
-            f"finish{which}",
-            [((OC, CELLS), kind), sums_out],
+            functools.partial(finish_kernel, which), [((OC, CELLS), kind), sums_out]
         )(mid, beside(right, 1), beside(left, -1), cols, *more)
-        (copies,) = call(functools.partial(norm_kernel, which), f"norm{which}", [every])(
+        (copies,) = call(functools.partial(norm_kernel, which), [every])(
             total, to_every(sums, PCOL), cols
         )
         return total, to_every(copies, PROW).reshape(C, CELLS)
 
-    (block,) = call(pack_kernel, "pack", [((NP, BLOCK, 128), BF16)])(latent, w_out)
+    (block,) = call(pack_kernel, [((NP, BLOCK, 128), BF16)])(latent, w_out)
     block = to_every(block, PROW)
-    (sums,) = call(stats_cells_kernel, "stats", [sums_out])(block)
+    (sums,) = call(stats_cells_kernel, [sums_out])(block)
     sums = to_every(sums, PCOL)
-    (w_part,) = call(unpack_kernel, "unpack", [((C, 128), BF16)])(block)
+    (w_part,) = call(unpack_kernel, [((C, 128), BF16)])(block)
     mid, left, right, own = call(
-        conv_cells_kernel, "conv1", conv_out + [((OC, CELLS), F32)], scalars=1
+        conv_cells_kernel, conv_out + [((OC, CELLS), F32)], scalars=1
     )(at, block, sums, norm_scale, norm_shift, conv_one.reshape(9 * OC, C))
     _, field = finish(0, mid, left, right)
-    mid, left, right = call(conv_channels_kernel, "conv2", conv_out)(
-        field, conv_two.reshape(9 * OC, C)
-    )
+    mid, left, right = call(conv_channels_kernel, conv_out)(field, conv_two.reshape(9 * OC, C))
     resnet, field = finish(1, mid, left, right, own)
     parts, fresh = call(
-        attention_kernel,
-        "attention",
-        [((NP, NP, C), BF16), ((CELLS, 2 * HEAD), BF16)],
-        scalars=1,
-        mib=32,
-    )(at, field, w_qkv, pairs, w_part, resnet)
-    (out,) = call(output_kernel, "output", [((PC, PC, C), BF16)])(to_every(parts, PROW))
+        attention_kernel, [((NP, NP, C), BF16), ((CELLS, 2 * HEAD), BF16)], scalars=1, mib=16
+    )(at, field, w_qkv, near, far, w_part, resnet)
+    (out,) = call(output_kernel, [((PC, PC, C), BF16)])(to_every(parts, PROW))
     return out, fresh.reshape(LR, PC, 1, 2 * HEAD)
 
 
@@ -363,6 +365,7 @@
         P(None, PCOL, PROW, None),
     )
     out_specs = (P(PROW, PCOL, None), P(None, PCOL, PROW, None))
+
     return jax.shard_map(
         shards, mesh=torus, in_specs=in_specs, out_specs=out_specs, check_vma=False
     )

time: 226 us -> 229 us (1.013)
  blocking collectives: 81.1 us -> 97.2 us
  between operations: 14.3 us -> 0.91 us
  waiting for transfers between devices: 55.8 us -> 51.2 us
  local copies, waits for them, and re-layouts: 3.32 us -> 6.63 us
  starting transfers between devices: 53.7 us -> 56.1 us
    all_to_all x3 -> x4, blocking collectives: 53.3 us -> 97.2 us  [to_every(): return lax.all_to_all(copies, axis, split_axis=0, concat_axis=0, tiled=True)]
    all_gather x1 -> x0, blocking collectives: 27.8 us -> none  [shards(): pairs = lax.all_gather(pairs, axis, axis=0)]
    all_to_all x4 -> x3, waiting for transfers between devices: 48.2 us -> 21 us  [to_every(): return lax.all_to_all(copies, axis, split_axis=0, concat_axis=0, tiled=True)]
    ppermute x0 -> x5, waiting for transfers between devices: none -> 23.4 us  [shards(): far = lax.ppermute(near, axis, [(i, i ^ bit) for i in range(count)])]
    all_to_all x4 -> x3, starting transfers between devices: 42.6 us -> 28.1 us  [to_every(): return lax.all_to_all(copies, axis, split_axis=0, concat_axis=0, tiled=True)]
    ppermute x0 -> x5, starting transfers between devices: none -> 14.4 us  [shards(): far = lax.ppermute(near, axis, [(i, i ^ bit) for i in range(count)])]
    unnamed x22 -> x24, local copies, waits for them, and re-layouts: 3.32 us -> 6.62 us
    ppermute x4, starting transfers between devices: 11 us -> 13.5 us  [beside(): return lax.ppermute(value, PCOL, pairs)]
  transfers between devices with their start and end apart: 10 -> 12, of which waited for: 5 -> 8; matrix products, arithmetic and copies ran while one was open for 0% -> 0% of each run, Pallas kernels for 4% -> 2%
where the time goes in v3:
time: 229 us; the launch traced here: 226 us
  blocking collectives  97.2 us (42%)
  starting transfers between devices  56.1 us (24%)
  waiting for transfers between devices  51.2 us (22%)
  Pallas kernels  14.1 us (6%)
  local copies, waits for them, and re-layouts  6.63 us (3%)
    all_to_all x4, blocking collectives, to_every(): return lax.all_to_all(copies, axis, split_axis=0, concat_axis=0, tiled=True)  97.2 us
    all_to_all x3, starting transfers between devices, to_every(): return lax.all_to_all(copies, axis, split_axis=0, concat_axis=0, tiled=True)  28.1 us
    ppermute x5, waiting for transfers between devices, shards(): far = lax.ppermute(near, axis, [(i, i ^ bit) for i in range(count)])  23.4 us
    all_to_all x3, waiting for transfers between devices, to_every(): return lax.all_to_all(copies, axis, split_axis=0, concat_axis=0, tiled=True)  21 us
    ppermute x5, starting transfers between devices, shards(): far = lax.ppermute(near, axis, [(i, i ^ bit) for i in range(count)])  14.4 us
    pallas_call x16, Pallas kernels, run(): pl.pallas_call(kernel, out_shape=[jax.ShapeDtypeStruct(*out) for out in o...  14.1 us
    ppermute x4, starting transfers between devices, beside(): return lax.ppermute(value, PCOL, pairs)  13.5 us
    ppermute x4, waiting for transfers between devices, beside(): return lax.ppermute(value, PCOL, pairs)  6.79 us
  transfers between devices with their start and end apart: 12, of which 8 were waited for; matrix products, arithmetic and copies ran while one was open for 0% of the time, Pallas kernels for 2%

profile of v3, /device:TPU:1, one launch (start us, length us, event | category | flops | bytes accessed | tf_op | source)
XLA Modules:
  0.0 226.1 jit_solution(5365860874224787701)
XLA Ops:
  2.6 41.6 %all_to_all.35.block_ref = bf16[16,208,128]{2,1,0:T(8,128)(2,1)S(1)} all-to-all(bf16[16,208,128]{2,1,0:T(8,128)(2,1)S(1)} %shard_map.113), channel_id=1, replica_groups=mesh['prow_0'=2,'prow_1'=8,'pcol_0'=4,'pcol_1'=4,'pcol_2'=2] {'prow_0','..., dimensions={0} | all-to-all | bytes 1703936 | tf_op jit(solution)/shard_map/all_to_all | solution.py:288
  45.6 9.0 %all-to-all-start.1 = ((f32[32,1,128]{2,1,0:T(1,128)}), f32[32,1,128]{2,1,0:T(1,128)S(1)}, u32[]{:S(2)}, u32[]{:S(2)}) async-start(f32[32,1,128]{2,1,0:T(1,128)} %shard_map.114), calls=%async_computation.1 | async-start | bytes 32768 | tf_op jit(solution)/shard_map/all_to_all | solution.py:288
  54.6 7.3 %all-to-all-done.1.sums_ref = f32[32,1,128]{2,1,0:T(1,128)S(1)} async-done(((f32[32,1,128]{2,1,0:T(1,128)}), f32[32,1,128]{2,1,0:T(1,128)S(1)}, u32[]{:S(2)}, u32[]{:S(2)}) %all-to-all-start.1) | async-done | bytes 16416 | tf_op jit(solution)/shard_map/all_to_all | solution.py:288
  63.6 2.9 %collective-permute-start = (f32[80,64]{1,0:T(8,128)S(1)}, f32[80,64]{1,0:T(8,128)S(1)}, u32[]{:S(2)}, u32[]{:S(2)}) collective-permute-start(f32[80,64]{1,0:T(8,128)S(1)} %get-tuple-element.16), channel_id=1, source_target_pairs={{0,1},{1,2},{2,3},{3,4},{4,5},{5,6},{6,7},{7,8},{8,9},{9,10},{10,1... | collective-permute-start | bytes 61448 | tf_op jit(solution)/shard_map/ppermute | solution.py:293
  66.5 1.9 collective-permute-start.1
  68.8 3.0 %collective-permute-done.1.from_right_ref = f32[80,64]{1,0:T(8,128)S(1)} collective-permute-done((f32[80,64]{1,0:T(8,128)S(1)}, f32[80,64]{1,0:T(8,128)S(1)}, u32[]{:S(2)}, u32[]{:S(2)}) %collective-permute-start.1) | collective-permute-done | bytes 20512 | tf_op jit(solution)/shard_map/ppermute | solution.py:293
  72.0 13.5 %all_to_all.36.sums_ref = f32[32,1,128]{2,1,0:T(1,128)S(1)} all-to-all(f32[32,1,128]{2,1,0:T(1,128)S(1)} %get-tuple-element.19), channel_id=1, replica_groups=mesh['prow_0'=2,'prow_1'=8,'pcol_0'=4,'pcol_1'=4,'pcol_2'=2] {'pcol_0','..., dimensions={0} | all-to-all | bytes 32768 | tf_op jit(solution)/shard_map/all_to_all | solution.py:288
  86.7 4.5 %all-to-all-start.3 = ((bf16[16,80,256]{2,1,0:T(8,128)(2,1)}), bf16[16,80,256]{2,1,0:T(8,128)(2,1)S(1)}, u32[]{:S(2)}, u32[]{:S(2)}) async-start(bf16[16,80,256]{2,1,0:T(8,128)(2,1)} %shard_map.118), calls=%async_computation.3 | async-start | bytes 1310720 | tf_op jit(solution)/shard_map/all_to_all | solution.py:288
  91.2 2.2 collective-permute-start.4
  93.4 4.2 %collective-permute-done.4.right_ref = bf16[1,256,128]{2,1,0:T(8,128)(2,1)S(1)} collective-permute-done((bf16[1,256,128]{2,1,0:T(8,128)(2,1)S(1)}, bf16[1,256,128]{2,1,0:T(8,128)(2,1)S(1)}, u32[]{:S(2)}, u32[]{:S(2)}) %collective-permute-start.4) | collective-permute-done | bytes 65568 | tf_op jit(solution)/shard_map/ppermute | solution.py:312
  97.7 2.4 %collective-permute-start.5 = (bf16[2,256,128]{2,1,0:T(8,128)(2,1)S(1)}, bf16[2,256,128]{2,1,0:T(8,128)(2,1)S(1)}, u32[]{:S(2)}, u32[]{:S(2)}) collective-permute-start(bf16[2,256,128]{2,1,0:T(8,128)(2,1)S(1)} %shard_map.122.left_ref), channel_id=1, source_target_pairs={{0,16},{8,24},{16,0},{24,8},{1,17},{9,25},{17,1},{25,9},{2,18},{10... | collective-permute-start | bytes 393224 | tf_op jit(solution)/shard_map/ppermute | solution.py:312
  100.1 12.9 %collective-permute-done.5.right_ref = bf16[2,256,128]{2,1,0:T(8,128)(2,1)S(1)} collective-permute-done((bf16[2,256,128]{2,1,0:T(8,128)(2,1)S(1)}, bf16[2,256,128]{2,1,0:T(8,128)(2,1)S(1)}, u32[]{:S(2)}, u32[]{:S(2)}) %collective-permute-start.5) | collective-permute-done | bytes 131104 | tf_op jit(solution)/shard_map/ppermute | solution.py:312
  113.0 4.6 %collective-permute-start.6 = (bf16[4,256,128]{2,1,0:T(8,128)(2,1)S(1)}, bf16[4,256,128]{2,1,0:T(8,128)(2,1)S(1)}, u32[]{:S(2)}, u32[]{:S(2)}) collective-permute-start(bf16[4,256,128]{2,1,0:T(8,128)(2,1)S(1)} %shard_map.123.left_ref), channel_id=1, source_target_pairs={{0,2},{2,0},{4,6},{6,4},{1,3},{3,1},{5,7},{7,5},{8,10},{10,8},{12,... | collective-permute-start | bytes 786440 | tf_op jit(solution)/shard_map/ppermute | solution.py:312
  117.6 4.2 %collective-permute-done.6.right_ref = bf16[4,256,128]{2,1,0:T(8,128)(2,1)S(1)} collective-permute-done((bf16[4,256,128]{2,1,0:T(8,128)(2,1)S(1)}, bf16[4,256,128]{2,1,0:T(8,128)(2,1)S(1)}, u32[]{:S(2)}, u32[]{:S(2)}) %collective-permute-start.6) | collective-permute-done | bytes 262176 | tf_op jit(solution)/shard_map/ppermute | solution.py:312
  121.8 2.4 %collective-permute-start.7 = (bf16[8,256,128]{2,1,0:T(8,128)(2,1)S(1)}, bf16[8,256,128]{2,1,0:T(8,128)(2,1)}, u32[]{:S(2)}, u32[]{:S(2)}) collective-permute-start(bf16[8,256,128]{2,1,0:T(8,128)(2,1)S(1)} %shard_map.124.left_ref), channel_id=1, source_target_pairs={{0,4},{2,6},{4,0},{6,2},{1,5},{3,7},{5,1},{7,3},{8,12},{10,14},{12... | collective-permute-start | bytes 1572872 | tf_op jit(solution)/shard_map/ppermute | solution.py:312
  126.5 6.9 %collective-permute-start.2 = (f32[80,64]{1,0:T(8,128)S(1)}, f32[80,64]{1,0:T(8,128)S(1)}, u32[]{:S(2)}, u32[]{:S(2)}) collective-permute-start(f32[80,64]{1,0:T(8,128)S(1)} %get-tuple-element.21), channel_id=1, source_target_pairs={{0,1},{1,2},{2,3},{3,4},{4,5},{5,6},{6,7},{7,8},{8,9},{9,10},{10,1... | collective-permute-start | bytes 61448 | tf_op jit(solution)/shard_map/ppermute | solution.py:293
  135.3 3.8 %collective-permute-done.3.from_right_ref = f32[80,64]{1,0:T(8,128)S(1)} collective-permute-done((f32[80,64]{1,0:T(8,128)S(1)}, f32[80,64]{1,0:T(8,128)S(1)}, u32[]{:S(2)}, u32[]{:S(2)}) %collective-permute-start.3) | collective-permute-done | bytes 20512 | tf_op jit(solution)/shard_map/ppermute | solution.py:293
  139.3 15.1 %all_to_all.37.sums_ref = f32[32,1,128]{2,1,0:T(1,128)S(1)} all-to-all(f32[32,1,128]{2,1,0:T(1,128)S(1)} %get-tuple-element.25), channel_id=1, replica_groups=mesh['prow_0'=2,'prow_1'=8,'pcol_0'=4,'pcol_1'=4,'pcol_2'=2] {'pcol_0','..., dimensions={0} | all-to-all | bytes 32768 | tf_op jit(solution)/shard_map/all_to_all | solution.py:288
  155.6 14.5 %all-to-all-start.5 = ((bf16[16,80,256]{2,1,0:T(8,128)(2,1)}), bf16[16,80,256]{2,1,0:T(8,128)(2,1)S(1)}, u32[]{:S(2)}, u32[]{:S(2)}) async-start(bf16[16,80,256]{2,1,0:T(8,128)(2,1)} %shard_map.121), calls=%async_computation.5 | async-start | bytes 1310720 | tf_op jit(solution)/shard_map/all_to_all | solution.py:288
  171.3 2.8 %collective-permute-start.8 = (bf16[16,256,128]{2,1,0:T(8,128)(2,1)S(1)}, bf16[16,256,128]{2,1,0:T(8,128)(2,1)S(1)}, u32[]{:S(2)}, u32[]{:S(2)}) collective-permute-start(bf16[16,256,128]{2,1,0:T(8,128)(2,1)S(1)} %shard_map.125.near_ref), channel_id=1, source_target_pairs={{0,1},{1,0},{2,3},{3,2},{4,5},{5,4},{6,7},{7,6},{8,9},{9,8},{10,11... | collective-permute-start | bytes 3145736 | tf_op jit(solution)/shard_map/ppermute | solution.py:312
  174.3 2.1 collective-permute-done.8.far_ref
  177.4 13.7 %all-to-all-done.5 = bf16[16,80,256]{2,1,0:T(8,128)(2,1)S(1)} async-done(((bf16[16,80,256]{2,1,0:T(8,128)(2,1)}), bf16[16,80,256]{2,1,0:T(8,128)(2,1)S(1)}, u32[]{:S(2)}, u32[]{:S(2)}) %all-to-all-start.5) | async-done | bytes 655392 | tf_op jit(solution)/shard_map/all_to_all | solution.py:288
  193.4 5.0 %shard_map.127 = (bf16[16,16,1280]{2,1,0:T(8,128)(2,1)S(1)}, bf16[256,128]{1,0:T(8,128)(2,1)}) custom-call(s32[1]{0:T(128)} %bitcast.at_ref, bf16[1280,256]{1,0:T(8,128)(2,1)S(1)} %bitcast.10, bf16[192,1280]{1,0:T(8,128)(2,1)S(1)} %copy-done.4, bf16[16,256,128]{2,1,0:T(8,128)(2,1)S(1)} %shard_map.125.near_ref, bf16[16,256,128]{2,1,0:T(8,128)(2,1)S(1)} %copy-done.3, ...), custom_call_target="tpu_custom_call" | custom-call | tf_op jit(solution)/shard_map/pallas_call | solution.py:276
  198.4 27.0 %all_to_all.38.parts_ref = bf16[16,16,1280]{2,1,0:T(8,128)(2,1)S(1)} all-to-all(bf16[16,16,1280]{2,1,0:T(8,128)(2,1)S(1)} %get-tuple-element.26), channel_id=1, replica_groups=mesh['prow_0'=2,'prow_1'=8,'pcol_0'=4,'pcol_1'=4,'pcol_2'=2] {'prow_0','..., dimensions={0} | all-to-all | bytes 1310720 | tf_op jit(solution)/shard_map/all_to_all | solution.py:288
  (45 shorter events, 17.7 us)
Async XLA Ops:
  0.6 61.2 %copy-start.1 = (bf16[3,3,80,1280]{3,2,1,0:T(8,128)(2,1)S(1)}, bf16[3,3,80,1280]{3,2,1,0:T(8,128)(2,1)}, u32[]{:S(2)}) copy-start(bf16[3,3,80,1280]{3,2,1,0:T(8,128)(2,1)} %param.15) | copy-start | bytes 5529604
  0.6 1.1 copy-start.5
  1.7 0.8 copy-start.9
  2.5 59.4 %copy-start.6 = (f32[3,1280]{1,0:T(4,128)S(1)}, f32[3,1280]{1,0:T(4,128)}, u32[]{:S(2)}) copy-start(f32[3,1280]{1,0:T(4,128)} %scale_ref.3) | copy-start | bytes 46084
  2.5 59.4 %copy-start.7 = (f32[3,1280]{1,0:T(4,128)S(1)}, f32[3,1280]{1,0:T(4,128)}, u32[]{:S(2)}) copy-start(f32[3,1280]{1,0:T(4,128)} %shift_ref.3) | copy-start | bytes 46084
  44.2 24.2 %copy-start.11 = (f32[1280]{0:T(1024)S(1)}, f32[1280]{0:T(1024)}, u32[]{:S(2)}) copy-start(f32[1280]{0:T(1024)} %param.13) | copy-start | bytes 15364
  44.2 24.2 %copy-start.10 = (f32[2,1280]{1,0:T(2,128)S(1)}, f32[2,1280]{1,0:T(2,128)}, u32[]{:S(2)}) copy-start(f32[2,1280]{1,0:T(2,128)} %bias_ref.1) | copy-start | bytes 30724
  45.6 16.3 %all-to-all-start.1 = ((f32[32,1,128]{2,1,0:T(1,128)}), f32[32,1,128]{2,1,0:T(1,128)S(1)}, u32[]{:S(2)}, u32[]{:S(2)}) async-start(f32[32,1,128]{2,1,0:T(1,128)} %shard_map.114), calls=%async_computation.1 | async-start | bytes 32768 | tf_op jit(solution)/shard_map/all_to_all | solution.py:288
  63.6 27.6 %copy-start.8 = (bf16[64,4,1,128]{3,1,2,0:T(4,128)(2,1)S(1)}, bf16[64,4,1,128]{3,1,2,0:T(4,128)(2,1)}, u32[]{:S(2)}) copy-start(bf16[64,4,1,128]{3,1,2,0:T(4,128)(2,1)} %param.19) | copy-start | bytes 196612
  63.6 5.2 %collective-permute-start = (f32[80,64]{1,0:T(8,128)S(1)}, f32[80,64]{1,0:T(8,128)S(1)}, u32[]{:S(2)}, u32[]{:S(2)}) collective-permute-start(f32[80,64]{1,0:T(8,128)S(1)} %get-tuple-element.16), channel_id=1, source_target_pairs={{0,1},{1,2},{2,3},{3,4},{4,5},{5,6},{6,7},{7,8},{8,9},{9,10},{10,1... | collective-permute-start | bytes 61448 | tf_op jit(solution)/shard_map/ppermute | solution.py:293
  66.5 5.3 %collective-permute-start.1 = (f32[80,64]{1,0:T(8,128)S(1)}, f32[80,64]{1,0:T(8,128)S(1)}, u32[]{:S(2)}, u32[]{:S(2)}) collective-permute-start(f32[80,64]{1,0:T(8,128)S(1)} %get-tuple-element.17), channel_id=1, source_target_pairs={{1,0},{2,1},{3,2},{4,3},{5,4},{6,5},{7,6},{8,7},{9,8},{10,9},{11,1... | collective-permute-start | bytes 61448 | tf_op jit(solution)/shard_map/ppermute | solution.py:293
  86.7 37.6 %all-to-all-start.3 = ((bf16[16,80,256]{2,1,0:T(8,128)(2,1)}), bf16[16,80,256]{2,1,0:T(8,128)(2,1)S(1)}, u32[]{:S(2)}, u32[]{:S(2)}) async-start(bf16[16,80,256]{2,1,0:T(8,128)(2,1)} %shard_map.118), calls=%async_computation.3 | async-start | bytes 1310720 | tf_op jit(solution)/shard_map/all_to_all | solution.py:288
  91.2 6.4 %collective-permute-start.4 = (bf16[1,256,128]{2,1,0:T(8,128)(2,1)S(1)}, bf16[1,256,128]{2,1,0:T(8,128)(2,1)S(1)}, u32[]{:S(2)}, u32[]{:S(2)}) collective-permute-start(bf16[1,256,128]{2,1,0:T(8,128)(2,1)S(1)} %bitcast.13), channel_id=1, source_target_pairs={{0,8},{8,0},{16,24},{24,16},{1,9},{9,1},{17,25},{25,17},{2,10},{10... | collective-permute-start | bytes 196616 | tf_op jit(solution)/shard_map/ppermute | solution.py:312
  97.7 15.3 %collective-permute-start.5 = (bf16[2,256,128]{2,1,0:T(8,128)(2,1)S(1)}, bf16[2,256,128]{2,1,0:T(8,128)(2,1)S(1)}, u32[]{:S(2)}, u32[]{:S(2)}) collective-permute-start(bf16[2,256,128]{2,1,0:T(8,128)(2,1)S(1)} %shard_map.122.left_ref), channel_id=1, source_target_pairs={{0,16},{8,24},{16,0},{24,8},{1,17},{9,25},{17,1},{25,9},{2,18},{10... | collective-permute-start | bytes 393224 | tf_op jit(solution)/shard_map/ppermute | solution.py:312
  113.0 8.8 %collective-permute-start.6 = (bf16[4,256,128]{2,1,0:T(8,128)(2,1)S(1)}, bf16[4,256,128]{2,1,0:T(8,128)(2,1)S(1)}, u32[]{:S(2)}, u32[]{:S(2)}) collective-permute-start(bf16[4,256,128]{2,1,0:T(8,128)(2,1)S(1)} %shard_map.123.left_ref), channel_id=1, source_target_pairs={{0,2},{2,0},{4,6},{6,4},{1,3},{3,1},{5,7},{7,5},{8,10},{10,8},{12,... | collective-permute-start | bytes 786440 | tf_op jit(solution)/shard_map/ppermute | solution.py:312
  121.8 48.4 %collective-permute-start.7 = (bf16[8,256,128]{2,1,0:T(8,128)(2,1)S(1)}, bf16[8,256,128]{2,1,0:T(8,128)(2,1)}, u32[]{:S(2)}, u32[]{:S(2)}) collective-permute-start(bf16[8,256,128]{2,1,0:T(8,128)(2,1)S(1)} %shard_map.124.left_ref), channel_id=1, source_target_pairs={{0,4},{2,6},{4,0},{6,2},{1,5},{3,7},{5,1},{7,3},{8,12},{10,14},{12... | collective-permute-start | bytes 1572872 | tf_op jit(solution)/shard_map/ppermute | solution.py:312
  124.2 1.5 copy-start
  126.5 8.8 %collective-permute-start.2 = (f32[80,64]{1,0:T(8,128)S(1)}, f32[80,64]{1,0:T(8,128)S(1)}, u32[]{:S(2)}, u32[]{:S(2)}) collective-permute-start(f32[80,64]{1,0:T(8,128)S(1)} %get-tuple-element.21), channel_id=1, source_target_pairs={{0,1},{1,2},{2,3},{3,4},{4,5},{5,6},{6,7},{7,8},{8,9},{9,10},{10,1... | collective-permute-start | bytes 61448 | tf_op jit(solution)/shard_map/ppermute | solution.py:293
  133.4 5.7 %collective-permute-start.3 = (f32[80,64]{1,0:T(8,128)S(1)}, f32[80,64]{1,0:T(8,128)S(1)}, u32[]{:S(2)}, u32[]{:S(2)}) collective-permute-start(f32[80,64]{1,0:T(8,128)S(1)} %get-tuple-element.22), channel_id=1, source_target_pairs={{1,0},{2,1},{3,2},{4,3},{5,4},{6,5},{7,6},{8,7},{9,8},{10,9},{11,1... | collective-permute-start | bytes 61448 | tf_op jit(solution)/shard_map/ppermute | solution.py:293
  155.6 35.5 %all-to-all-start.5 = ((bf16[16,80,256]{2,1,0:T(8,128)(2,1)}), bf16[16,80,256]{2,1,0:T(8,128)(2,1)S(1)}, u32[]{:S(2)}, u32[]{:S(2)}) async-start(bf16[16,80,256]{2,1,0:T(8,128)(2,1)} %shard_map.121), calls=%async_computation.5 | async-start | bytes 1310720 | tf_op jit(solution)/shard_map/all_to_all | solution.py:288
  171.3 5.1 %collective-permute-start.8 = (bf16[16,256,128]{2,1,0:T(8,128)(2,1)S(1)}, bf16[16,256,128]{2,1,0:T(8,128)(2,1)S(1)}, u32[]{:S(2)}, u32[]{:S(2)}) collective-permute-start(bf16[16,256,128]{2,1,0:T(8,128)(2,1)S(1)} %shard_map.125.near_ref), channel_id=1, source_target_pairs={{0,1},{1,0},{2,3},{3,2},{4,5},{5,4},{6,7},{7,6},{8,9},{9,8},{10,11... | collective-permute-start | bytes 3145736 | tf_op jit(solution)/shard_map/ppermute | solution.py:312
  176.4 1.0 copy-start.2
  191.2 1.2 copy-start.3
  192.4 1.0 copy-start.4

commit v4 on v3

--- a/solution.py
+++ b/solution.py
@@ -76,12 +76,20 @@
     return v / (1.0 + jnp.exp(-v))
 
 
-def pack_kernel(latent_ref, w_ref, out_ref):
+def pack_kernel(latent_hbm, w_hbm, out_ref, latent_ref, w_ref, sems):
+    copies = [
+        pltpu.make_async_copy(latent_hbm, latent_ref, sems.at[0]),
+        pltpu.make_async_copy(w_hbm, w_ref, sems.at[1]),
+    ]
+    for copy in copies:
+        copy.start()
+    copies[0].wait()
     rows = [latent_ref[r].astype(F32) for r in range(PC)]
     patch = jnp.concatenate(rows, axis=0).astype(BF16)
     for j in range(C // 128):
         chunk = patch[:, 128 * j : 128 * (j + 1)]
         out_ref[:, NP * j : NP * (j + 1), :] = jnp.broadcast_to(chunk[None], (NP, NP, 128))
+    copies[1].wait()
     lane = iota((PIECE, 128), 1)
     for k in range(NP // 2):
         w = w_ref[:, 128 * k : 128 * (k + 1)].astype(F32)
@@ -124,10 +132,21 @@
     out_ref[...] = total
 
 
-def stats_cells_kernel(block_ref, out_ref):
+def strip_chunk(block_ref, j):
+    return block_ref[:, NP * j : NP * (j + 1), :].reshape(CELLS, 128)
+
+
+def stats_cells_kernel(block_ref, out_ref, leftmost_ref, rightmost_ref):
     firsts, seconds = [], []
+    row = iota((2 * LR, CELLS), 0)
+    wanted = jnp.where(row < LR, row * PC, (row - LR) * PC + PC - 1)
+    pick = one_hot(iota((2 * LR, CELLS), 1) == wanted, BF16)
     for j in range(C // 128):
-        x = block_ref[:, NP * j : NP * (j + 1), :].astype(F32).reshape(CELLS, 128)
+        x = strip_chunk(block_ref, j)
+        edges = nn(pick, x).astype(BF16)
+        leftmost_ref[:, 128 * j : 128 * (j + 1)] = edges[:LR]
+        rightmost_ref[:, 128 * j : 128 * (j + 1)] = edges[LR:]
+        x = x.astype(F32)
         firsts.append(jnp.sum(x, axis=0, keepdims=True))
         seconds.append(jnp.sum(x * x, axis=0, keepdims=True))
     first = jnp.concatenate(firsts, axis=1)
@@ -139,32 +158,46 @@
     out_ref[...] = jnp.broadcast_to(row[None], out_ref.shape)
 
 
-def conv_combine(products, mid_ref, to_left_ref, to_right_ref):
+def tap_sums(products, b):
+    row = iota((OC, products.shape[1]), 1) % LR
+    above, here, below = (
+        products[(3 * a + b) * OC : (3 * a + b + 1) * OC, :] for a in range(3)
+    )
+    above = jnp.where(row > 0, pltpu.roll(above, 1, 1), 0.0)
+    below = jnp.where(row < LR - 1, pltpu.roll(below, products.shape[1] - 1, 1), 0.0)
+    return here + above + below
+
+
+def tap_columns(products):
     lane = iota((OC, CELLS), 1)
-    row = lane % LR
-
-    def tap(a, b):
-        at = (3 * a + b) * OC
-        return products[at : at + OC, :]
-
-    def rows_summed(b):
-        above = jnp.where(row > 0, pltpu.roll(tap(0, b), 1, 1), 0.0)
-        below = jnp.where(row < LR - 1, pltpu.roll(tap(2, b), CELLS - 1, 1), 0.0)
-        return tap(1, b) + above + below
-
-    before = rows_summed(0)
-    after = rows_summed(2)
-    to_right_ref[...] = before[:, CELLS - LR :]
-    to_left_ref[...] = after[:, :LR]
-    mid_ref[...] = (
-        rows_summed(1)
+    before = tap_sums(products, 0)
+    after = tap_sums(products, 2)
+    mid = (
+        tap_sums(products, 1)
         + jnp.where(lane >= LR, pltpu.roll(before, LR, 1), 0.0)
         + jnp.where(lane < CELLS - LR, pltpu.roll(after, CELLS - LR, 1), 0.0)
     )
+    return before, mid, after
+
+
+def with_sides(mid, left, right):
+    blank = jnp.zeros((OC, CELLS - 2 * LR), F32)
+    return mid + jnp.concatenate([left, blank, right], axis=1)
 
 
 def conv_cells_kernel(
-    at_ref, block_ref, sums_ref, scale_ref, shift_ref, w_ref, mid_ref, left_ref, right_ref, own_ref
+    at_ref,
+    block_ref,
+    sums_ref,
+    scale_ref,
+    shift_ref,
+    w_ref,
+    left_ref,
+    right_ref,
+    cols_ref,
+    total_ref,
+    out_sums_ref,
+    own_ref,
 ):
     mean, rstd = moments(sums_ref)
     both = jnp.concatenate([mean, rstd, jnp.zeros((6, 128), F32)], axis=0)
@@ -172,36 +205,37 @@
     spread = nn(both, groups, lax.Precision.HIGHEST)
     gain = spread[1:2, :] * scale_ref[0:1, :]
     offset = shift_ref[0:1, :] - spread[0:1, :] * gain
-    chunks = [
-        block_ref[:, NP * j : NP * (j + 1), :].reshape(CELLS, 128) for j in range(C // 128)
-    ]
+    chunks = [strip_chunk(block_ref, j) for j in range(C // 128)]
     cells = nn(strip_order(), jnp.concatenate(chunks, axis=1))
     pick = one_hot(iota((OC, C), 1) == iota((OC, C), 0) + at_ref[0] * OC, BF16)
     own_ref[...] = nt(pick, cells.astype(BF16))
-    act = silu(cells * gain + offset).astype(BF16)
-    conv_combine(nt(w_ref[...], act), mid_ref, left_ref, right_ref)
-
-
-def conv_channels_kernel(x_ref, w_ref, mid_ref, left_ref, right_ref):
-    conv_combine(nn(w_ref[...], x_ref[...]), mid_ref, left_ref, right_ref)
+    _, mid, _ = tap_columns(nt(w_ref[...], silu(cells * gain + offset).astype(BF16)))
+    sides = jnp.concatenate([left_ref[...], right_ref[...]], axis=0).astype(F32)
+    sides = silu(sides * gain + offset)
+    row = iota((2 * LR, 1), 0)
+    first = jnp.where(at_ref[1] > 0, 0, LR)
+    last = jnp.where(at_ref[1] < NS - 1, 2 * LR, LR)
+    sides = jnp.where((row >= first) & (row < last), sides, 0.0).astype(BF16)
+    products = nt(w_ref[...], sides)
+    left = tap_sums(products, 0)[:, :LR]
+    right = tap_sums(products, 2)[:, LR:]
+    total = with_sides(mid, left, right) + cols_ref[:, 0:1]
+    total_ref[...] = total
+    own_sums(total, out_sums_ref)
+
+
+def conv_channels_kernel(x_ref, w_ref, mid_ref, to_left_ref, to_right_ref):
+    before, mid, after = tap_columns(nn(w_ref[...], x_ref[...]))
+    to_right_ref[...] = before[:, CELLS - LR :]
+    to_left_ref[...] = after[:, :LR]
+    mid_ref[...] = mid
 
 
 def whole(x):
     return jnp.sum(jnp.sum(x, axis=0, keepdims=True), axis=1, keepdims=True)
 
 
-def finish_kernel(which, mid_ref, from_left_ref, from_right_ref, cols_ref, *refs):
-    total_ref, sums_ref = refs[-2:]
-    sides = jnp.concatenate(
-        [from_left_ref[...], jnp.zeros((OC, CELLS - 2 * LR), F32), from_right_ref[...]], axis=1
-    )
-    total = mid_ref[...] + sides + cols_ref[:, 3 * which : 3 * which + 1]
-    if which == 1:
-        total = refs[0][...] + total
-        total_ref[...] = total.astype(BF16)
-        total = total.astype(BF16).astype(F32)
-    else:
-        total_ref[...] = total
+def own_sums(total, sums_ref):
     lane = iota((1, 128), 1)
     row = jnp.zeros((1, 128), F32)
     for k in range(2):
@@ -209,6 +243,13 @@
         row = jnp.where(lane == k, whole(half), row)
         row = jnp.where(lane == k + GROUPS, whole(half * half), row)
     sums_ref[...] = jnp.broadcast_to(row[None], sums_ref.shape)
+
+
+def finish_kernel(mid_ref, from_left_ref, from_right_ref, cols_ref, own_ref, total_ref, sums_ref):
+    total = with_sides(mid_ref[...], from_left_ref[...], from_right_ref[...])
+    total = (own_ref[...] + total + cols_ref[:, 3:4]).astype(BF16)
+    total_ref[...] = total
+    own_sums(total.astype(F32), sums_ref)
 
 
 def norm_kernel(which, total_ref, sums_ref, cols_ref, out_ref):
@@ -223,15 +264,37 @@
     out_ref[...] = jnp.broadcast_to(value.astype(BF16)[None], out_ref.shape)
 
 
-def join_kernel(left_ref, right_ref, out_ref):
+def join_kernel(left_ref, right_ref, out_ref, sems):
     count = left_ref.shape[0]
-    out_ref[:count] = left_ref[...]
-    out_ref[count:] = right_ref[...]
+    copies = [
+        pltpu.make_async_copy(left_ref, out_ref.at[pl.ds(0, count)], sems.at[0]),
+        pltpu.make_async_copy(right_ref, out_ref.at[pl.ds(count, count)], sems.at[1]),
+    ]
+    for copy in copies:
+        copy.start()
+    for copy in copies:
+        copy.wait()
 
 
 def attention_kernel(
-    at_ref, x_ref, w_ref, near_ref, far_ref, w_out_ref, own_ref, part_ref, fresh_ref
+    at_ref,
+    x_ref,
+    w_ref,
+    w_out_ref,
+    own_ref,
+    near_ref,
+    far_ref,
+    part_ref,
+    fresh_ref,
+    held_ref,
+    sems,
 ):
+    copies = [
+        pltpu.make_async_copy(half, held_ref.at[k], sems.at[k])
+        for k, half in enumerate((near_ref, far_ref))
+    ]
+    for copy in copies:
+        copy.start()
     mapped = nn(w_ref[...], x_ref[...])
     queries = jnp.transpose(mapped[:HEAD]).astype(BF16)
     fresh = jnp.transpose(mapped[HEAD:]).astype(BF16)
@@ -244,9 +307,10 @@
     denominator = jnp.zeros((CELLS, 1), F32)
     weighted = jnp.zeros((CELLS, 2 * HEAD), F32)
     for step in range(NS // chunk):
-        half = (near_ref, far_ref)[step // (NS // chunk // 2)]
-        start = chunk * step % (NS // 2)
-        pairs = half[start : start + chunk].reshape(chunk * CELLS, 2 * HEAD)
+        half, start = divmod(chunk * step, NS // 2)
+        if start == 0:
+            copies[half].wait()
+        pairs = held_ref[half, start : start + chunk].reshape(chunk * CELLS, 2 * HEAD)
         if step == 0:
             pairs = jnp.concatenate([fresh, pairs[CELLS:]], axis=0)
         scores = nt(queries, pairs)
@@ -269,15 +333,22 @@
         out_ref[r] = total[PC * r : PC * (r + 1), :].astype(BF16)
 
 
-def call(kernel, outs, scalars=0, mib=8):
+def call(kernel, outs, scalars=0, outer=0, mib=8, space=pltpu.VMEM, scratch=()):
     def run(*args):
+        args = list(args)
+        for k in range(len(args) - outer, len(args)):
+            args[k] = pltpu.with_memory_space_constraint(args[k], pltpu.HBM)
         specs = [pl.BlockSpec(memory_space=pltpu.SMEM)] * scalars
-        specs += [pl.BlockSpec(memory_space=pltpu.VMEM)] * (len(args) - scalars)
+        specs += [pl.BlockSpec(memory_space=pltpu.VMEM)] * (len(args) - scalars - outer)
+        specs += [pl.BlockSpec(memory_space=pltpu.HBM)] * outer
         return pl.pallas_call(
             kernel,
-            out_shape=[jax.ShapeDtypeStruct(*out) for out in outs],
+            out_shape=[
+                pltpu.HBM(*out) if space is pltpu.HBM else jax.ShapeDtypeStruct(*out) for out in outs
+            ],
             in_specs=specs,
-            out_specs=[pl.BlockSpec(memory_space=pltpu.VMEM)] * len(outs),
+            out_specs=[pl.BlockSpec(memory_space=space)] * len(outs),
+            scratch_shapes=list(scratch),
             compiler_params=pltpu.CompilerParams(vmem_limit_bytes=mib * 2**20),
         )(*args)
 
@@ -305,45 +376,77 @@
     w_out,
     stale_kv,
 ):
-    at = lax.axis_index(PROW).astype(jnp.int32).reshape(1)
+    at = jnp.stack([lax.axis_index(PROW), lax.axis_index(PCOL)]).astype(jnp.int32)
     near = stale_kv.reshape(1, CELLS, 2 * HEAD)
     for step, (axis, bit) in enumerate(HOPS):
         count = lax.axis_size(axis)
         far = lax.ppermute(near, axis, [(i, i ^ bit) for i in range(count)])
         if step < len(HOPS) - 1:
             out = ((2 * near.shape[0], CELLS, 2 * HEAD), BF16)
-            (near,) = call(join_kernel, [out])(near, far)
+            (near,) = call(
+                join_kernel,
+                [out],
+                outer=2,
+                space=pltpu.HBM,
+                scratch=[pltpu.SemaphoreType.DMA((2,))],
+            )(near, far)
     sums_out = ((NS, 1, 128), F32)
     every = ((NP, OC, CELLS), BF16)
-    conv_out = [((OC, CELLS), F32), ((OC, LR), F32), ((OC, LR), F32)]
+    tile = ((OC, CELLS), F32)
+    edge = ((LR, C), BF16)
     (cols,) = call(columns_kernel, [((OC, 128), F32)], scalars=1)(
         at, norm_scale, norm_shift, conv_bias, time_shift.reshape(1, C)
     )
 
-    def finish(which, mid, left, right, *more):
-        kind = (F32, BF16)[which]
-        total, sums = call(
-            functools.partial(finish_kernel, which), [((OC, CELLS), kind), sums_out]
-        )(mid, beside(right, 1), beside(left, -1), cols, *more)
-        (copies,) = call(functools.partial(norm_kernel, which), [every])(
-            total, to_every(sums, PCOL), cols
-        )
-        return total, to_every(copies, PROW).reshape(C, CELLS)
-
-    (block,) = call(pack_kernel, [((NP, BLOCK, 128), BF16)])(latent, w_out)
+    def gathered(which, total, sums):
+        sums = to_every(sums, PCOL)
+        (copies,) = call(functools.partial(norm_kernel, which), [every])(total, sums, cols)
+        return to_every(copies, PROW).reshape(C, CELLS)
+
+    (block,) = call(
+        pack_kernel,
+        [((NP, BLOCK, 128), BF16)],
+        outer=2,
+        scratch=[
+            pltpu.VMEM((PC, PC, C), BF16),
+            pltpu.VMEM(w_out.shape, BF16),
+            pltpu.SemaphoreType.DMA((2,)),
+        ],
+    )(latent, w_out)
     block = to_every(block, PROW)
-    (sums,) = call(stats_cells_kernel, [sums_out])(block)
+    sums, leftmost, rightmost = call(stats_cells_kernel, [sums_out, edge, edge])(block)
     sums = to_every(sums, PCOL)
+    left, right = beside(rightmost, 1), beside(leftmost, -1)
     (w_part,) = call(unpack_kernel, [((C, 128), BF16)])(block)
-    mid, left, right, own = call(
-        conv_cells_kernel, conv_out + [((OC, CELLS), F32)], scalars=1
-    )(at, block, sums, norm_scale, norm_shift, conv_one.reshape(9 * OC, C))
-    _, field = finish(0, mid, left, right)
-    mid, left, right = call(conv_channels_kernel, conv_out)(field, conv_two.reshape(9 * OC, C))
-    resnet, field = finish(1, mid, left, right, own)
+    total, sums, own = call(conv_cells_kernel, [tile, sums_out, tile], scalars=1)(
+        at,
+        block,
+        sums,
+        norm_scale,
+        norm_shift,
+        conv_one.reshape(9 * OC, C),
+        left,
+        right,
+        cols,
+    )
+    field = gathered(0, total, sums)
+    mid, left, right = call(
+        conv_channels_kernel, [tile, ((OC, LR), F32), ((OC, LR), F32)]
+    )(field, conv_two.reshape(9 * OC, C))
+    left, right = beside(right, 1), beside(left, -1)
+    resnet, sums = call(finish_kernel, [((OC, CELLS), BF16), sums_out])(mid, left, right, cols, own)
+    field = gathered(1, resnet, sums)
     parts, fresh = call(
-        attention_kernel, [((NP, NP, C), BF16), ((CELLS, 2 * HEAD), BF16)], scalars=1, mib=16
-    )(at, field, w_qkv, near, far, w_part, resnet)
+        attention_kernel,
+        [((NP, NP, C), BF16), ((CELLS, 2 * HEAD), BF16)],
+        scalars=1,
+        outer=2,
+        mib=16,
+        scratch=[
+            pltpu.VMEM((2, NS // 2, CELLS, 2 * HEAD), BF16),
+            pltpu.SemaphoreType.DMA((2,)),
+        ],
+    )(at, field, w_qkv, w_part, resnet, near, far)
     (out,) = call(output_kernel, [((PC, PC, C), BF16)])(to_every(parts, PROW))
     return out, fresh.reshape(LR, PC, 1, 2 * HEAD)
 

time: 229 us -> 281 us (1.23)
  Pallas kernels: 14.1 us -> 81.1 us
  waiting for transfers between devices: 51.2 us -> 29.8 us
  starting transfers between devices: 56.1 us -> 63.9 us
  local copies, waits for them, and re-layouts: 6.63 us -> 3 us
    pallas_call x16 -> x15, Pallas kernels: 14.1 us -> 81.1 us  [run(): pl.pallas_call(kernel, out_shape=[pltpu.HBM(*out) if space is pltpu.HBM e...]
    all_to_all x3, waiting for transfers between devices: 21 us -> 6.27 us  [to_every(): return lax.all_to_all(copies, axis, split_axis=0, concat_axis=0, tiled=True)]
    ppermute x4, starting transfers between devices: 13.5 us -> 20.7 us  [beside(): return lax.ppermute(value, PCOL, pairs)]
    ppermute x5, waiting for transfers between devices: 23.4 us -> 19.7 us  [shards(): far = lax.ppermute(near, axis, [(i, i ^ bit) for i in range(count)])]
    unnamed x24, local copies, waits for them, and re-layouts: 6.62 us -> 2.99 us
    ppermute x4, waiting for transfers between devices: 6.79 us -> 3.79 us  [beside(): return lax.ppermute(value, PCOL, pairs)]
  transfers between devices with their start and end apart: 12 -> 12, of which waited for: 8 -> 6; matrix products, arithmetic and copies ran while one was open for 0% -> 0% of each run, Pallas kernels for 2% -> 24%
where the time goes in v4:
time: 281 us; the launch traced here: 278 us
  blocking collectives  99.4 us (35%)
  Pallas kernels  81.1 us (29%)
  starting transfers between devices  63.9 us (23%)
  waiting for transfers between devices  29.8 us (11%)
  local copies, waits for them, and re-layouts  3 us (1%)
    all_to_all x4, blocking collectives, to_every(): return lax.all_to_all(copies, axis, split_axis=0, concat_axis=0, tiled=True)  99.4 us
    pallas_call x15, Pallas kernels, run(): pl.pallas_call(kernel, out_shape=[pltpu.HBM(*out) if space is pltpu.HBM e...  81.1 us
    all_to_all x3, starting transfers between devices, to_every(): return lax.all_to_all(copies, axis, split_axis=0, concat_axis=0, tiled=True)  30.7 us
    ppermute x4, starting transfers between devices, beside(): return lax.ppermute(value, PCOL, pairs)  20.7 us
    ppermute x5, waiting for transfers between devices, shards(): far = lax.ppermute(near, axis, [(i, i ^ bit) for i in range(count)])  19.7 us
    ppermute x5, starting transfers between devices, shards(): far = lax.ppermute(near, axis, [(i, i ^ bit) for i in range(count)])  12.5 us
    all_to_all x3, waiting for transfers between devices, to_every(): return lax.all_to_all(copies, axis, split_axis=0, concat_axis=0, tiled=True)  6.27 us
  transfers between devices with their start and end apart: 12, of which 6 were waited for; matrix products, arithmetic and copies ran while one was open for 0% of the time, Pallas kernels for 24%

profile of v4, /device:TPU:1, one launch (start us, length us, event | category | flops | bytes accessed | tf_op | source)
XLA Modules:
  0.0 278.2 jit_solution(1631093291218218255)
XLA Ops:
  1.9 41.6 %all_to_all.35.block_ref = bf16[16,208,128]{2,1,0:T(8,128)(2,1)S(1)} all-to-all(bf16[16,208,128]{2,1,0:T(8,128)(2,1)S(1)} %shard_map.113), channel_id=1, replica_groups=mesh['prow_0'=2,'prow_1'=8,'pcol_0'=4,'pcol_1'=4,'pcol_2'=2] {'prow_0','..., dimensions={0} | all-to-all | bytes 1703936 | tf_op jit(solution)/shard_map/all_to_all | solution.py:359
  44.9 5.0 %collective-permute-start = (bf16[64,1280]{1,0:T(8,128)(2,1)}, bf16[64,1280]{1,0:T(8,128)(2,1)S(1)}, u32[]{:S(2)}, u32[]{:S(2)}) collective-permute-start(bf16[64,1280]{1,0:T(8,128)(2,1)} %get-tuple-element.16), channel_id=1, source_target_pairs={{0,1},{1,2},{2,3},{3,4},{4,5},{5,6},{6,7},{7,8},{8,9},{9,10},{10,1... | collective-permute-start | bytes 491528 | tf_op jit(solution)/shard_map/ppermute | solution.py:364
  51.9 7.6 %all-to-all-start.1 = ((f32[32,1,128]{2,1,0:T(1,128)}), f32[32,1,128]{2,1,0:T(1,128)S(1)}, u32[]{:S(2)}, u32[]{:S(2)}) async-start(f32[32,1,128]{2,1,0:T(1,128)} %get-tuple-element.15), calls=%async_computation.1 | async-start | bytes 32768 | tf_op jit(solution)/shard_map/all_to_all | solution.py:359
  60.5 6.3 %all-to-all-done.1.sums_ref = f32[32,1,128]{2,1,0:T(1,128)S(1)} async-done(((f32[32,1,128]{2,1,0:T(1,128)}), f32[32,1,128]{2,1,0:T(1,128)S(1)}, u32[]{:S(2)}, u32[]{:S(2)}) %all-to-all-start.1) | async-done | bytes 16416 | tf_op jit(solution)/shard_map/all_to_all | solution.py:359
  66.8 2.7 shard_map.116
  69.5 10.8 %all_to_all.36.sums_ref = f32[32,1,128]{2,1,0:T(1,128)S(1)} all-to-all(f32[32,1,128]{2,1,0:T(1,128)S(1)} %get-tuple-element.19), channel_id=1, replica_groups=mesh['prow_0'=2,'prow_1'=8,'pcol_0'=4,'pcol_1'=4,'pcol_2'=2] {'pcol_0','..., dimensions={0} | all-to-all | bytes 32768 | tf_op jit(solution)/shard_map/all_to_all | solution.py:359
  81.5 4.5 %all-to-all-start.3 = ((bf16[16,80,256]{2,1,0:T(8,128)(2,1)}), bf16[16,80,256]{2,1,0:T(8,128)(2,1)S(1)}, u32[]{:S(2)}, u32[]{:S(2)}) async-start(bf16[16,80,256]{2,1,0:T(8,128)(2,1)} %shard_map.117), calls=%async_computation.3 | async-start | bytes 1310720 | tf_op jit(solution)/shard_map/all_to_all | solution.py:359
  88.3 4.2 %collective-permute-done.4.right_ref = bf16[1,256,128]{2,1,0:T(8,128)(2,1)S(1)} collective-permute-done((bf16[1,256,128]{2,1,0:T(8,128)(2,1)S(1)}, bf16[1,256,128]{2,1,0:T(8,128)(2,1)S(1)}, u32[]{:S(2)}, u32[]{:S(2)}) %collective-permute-start.4) | collective-permute-done | bytes 65568 | tf_op jit(solution)/shard_map/ppermute | solution.py:383
  93.1 5.1 %shard_map.122.left_ref = bf16[2,256,128]{2,1,0:T(8,128)(2,1)} custom-call(bf16[1,256,128]{2,1,0:T(8,128)(2,1)} %bitcast.14, bf16[1,256,128]{2,1,0:T(8,128)(2,1)} %copy-done.10), custom_call_target="tpu_custom_call" | custom-call | tf_op jit(solution)/shard_map/pallas_call | solution.py:344
  98.2 2.4 collective-permute-start.5
  100.6 8.1 %collective-permute-done.5.right_ref = bf16[2,256,128]{2,1,0:T(8,128)(2,1)S(1)} collective-permute-done((bf16[2,256,128]{2,1,0:T(8,128)(2,1)}, bf16[2,256,128]{2,1,0:T(8,128)(2,1)S(1)}, u32[]{:S(2)}, u32[]{:S(2)}) %collective-permute-start.5) | collective-permute-done | bytes 131104 | tf_op jit(solution)/shard_map/ppermute | solution.py:383
  109.4 9.1 %shard_map.123.left_ref = bf16[4,256,128]{2,1,0:T(8,128)(2,1)} custom-call(bf16[2,256,128]{2,1,0:T(8,128)(2,1)} %shard_map.122.left_ref, bf16[2,256,128]{2,1,0:T(8,128)(2,1)} %copy-done.8), custom_call_target="tpu_custom_call" | custom-call | tf_op jit(solution)/shard_map/pallas_call | solution.py:344
  120.6 5.1 %collective-permute-done.6.right_ref = bf16[4,256,128]{2,1,0:T(8,128)(2,1)S(1)} collective-permute-done((bf16[4,256,128]{2,1,0:T(8,128)(2,1)}, bf16[4,256,128]{2,1,0:T(8,128)(2,1)S(1)}, u32[]{:S(2)}, u32[]{:S(2)}) %collective-permute-start.6) | collective-permute-done | bytes 262176 | tf_op jit(solution)/shard_map/ppermute | solution.py:383
  126.5 17.0 %shard_map.124.left_ref = bf16[8,256,128]{2,1,0:T(8,128)(2,1)} custom-call(bf16[4,256,128]{2,1,0:T(8,128)(2,1)} %shard_map.123.left_ref, bf16[4,256,128]{2,1,0:T(8,128)(2,1)} %copy-done.7), custom_call_target="tpu_custom_call" | custom-call | tf_op jit(solution)/shard_map/pallas_call | solution.py:344
  143.5 2.8 %collective-permute-start.7 = (bf16[8,256,128]{2,1,0:T(8,128)(2,1)}, bf16[8,256,128]{2,1,0:T(8,128)(2,1)}, u32[]{:S(2)}, u32[]{:S(2)}) collective-permute-start(bf16[8,256,128]{2,1,0:T(8,128)(2,1)} %shard_map.124.left_ref), channel_id=1, source_target_pairs={{0,4},{2,6},{4,0},{6,2},{1,5},{3,7},{5,1},{7,3},{8,12},{10,14},{12... | collective-permute-start | bytes 1572872 | tf_op jit(solution)/shard_map/ppermute | solution.py:383
  147.1 11.8 %collective-permute-start.2 = (f32[80,64]{1,0:T(8,128)S(1)}, f32[80,64]{1,0:T(8,128)S(1)}, u32[]{:S(2)}, u32[]{:S(2)}) collective-permute-start(f32[80,64]{1,0:T(8,128)S(1)} %get-tuple-element.21), channel_id=1, source_target_pairs={{0,1},{1,2},{2,3},{3,4},{4,5},{5,6},{6,7},{7,8},{8,9},{9,10},{10,1... | collective-permute-start | bytes 61448 | tf_op jit(solution)/shard_map/ppermute | solution.py:364
  160.9 3.8 %collective-permute-done.3.from_right_ref = f32[80,64]{1,0:T(8,128)S(1)} collective-permute-done((f32[80,64]{1,0:T(8,128)S(1)}, f32[80,64]{1,0:T(8,128)S(1)}, u32[]{:S(2)}, u32[]{:S(2)}) %collective-permute-start.3) | collective-permute-done | bytes 20512 | tf_op jit(solution)/shard_map/ppermute | solution.py:364
  164.8 14.1 %all_to_all.37.sums_ref = f32[32,1,128]{2,1,0:T(1,128)S(1)} all-to-all(f32[32,1,128]{2,1,0:T(1,128)S(1)} %get-tuple-element.25), channel_id=1, replica_groups=mesh['prow_0'=2,'prow_1'=8,'pcol_0'=4,'pcol_1'=4,'pcol_2'=2] {'pcol_0','..., dimensions={0} | all-to-all | bytes 32768 | tf_op jit(solution)/shard_map/all_to_all | solution.py:359
  180.1 18.6 %all-to-all-start.5 = ((bf16[16,80,256]{2,1,0:T(8,128)(2,1)}), bf16[16,80,256]{2,1,0:T(8,128)(2,1)S(1)}, u32[]{:S(2)}, u32[]{:S(2)}) async-start(bf16[16,80,256]{2,1,0:T(8,128)(2,1)} %shard_map.120), calls=%async_computation.5 | async-start | bytes 1310720 | tf_op jit(solution)/shard_map/all_to_all | solution.py:359
  198.7 32.9 %shard_map.125.near_ref = bf16[16,256,128]{2,1,0:T(8,128)(2,1)} custom-call(bf16[8,256,128]{2,1,0:T(8,128)(2,1)} %shard_map.124.left_ref, bf16[8,256,128]{2,1,0:T(8,128)(2,1)} %collective-permute-done.7.right_ref), custom_call_target="tpu_custom_call" | custom-call | tf_op jit(solution)/shard_map/pallas_call | solution.py:344
  231.6 2.8 %collective-permute-start.8 = (bf16[16,256,128]{2,1,0:T(8,128)(2,1)}, bf16[16,256,128]{2,1,0:T(8,128)(2,1)S(1)}, u32[]{:S(2)}, u32[]{:S(2)}) collective-permute-start(bf16[16,256,128]{2,1,0:T(8,128)(2,1)} %shard_map.125.near_ref), channel_id=1, source_target_pairs={{0,1},{1,0},{2,3},{3,2},{4,5},{5,4},{6,7},{7,6},{8,9},{9,8},{10,11... | collective-permute-start | bytes 3145736 | tf_op jit(solution)/shard_map/ppermute | solution.py:383
  234.6 2.3 collective-permute-done.8.far_ref
  237.9 6.7 %shard_map.126 = (bf16[16,16,1280]{2,1,0:T(8,128)(2,1)S(1)}, bf16[256,128]{1,0:T(8,128)(2,1)}) custom-call(s32[2]{0:T(128)S(1)} %pad_add_fusion.at_ref, bf16[1280,256]{1,0:T(8,128)(2,1)S(1)} %bitcast.11, bf16[192,1280]{1,0:T(8,128)(2,1)S(1)} %copy-done.2, bf16[1280,128]{1,0:T(8,128)(2,1)S(1)} %shard_map.121.w_out_ref, ...), custom_call_target="tpu_custom_call" | custom-call | tf_op jit(solution)/shard_map/pallas_call | solution.py:344
  244.6 32.9 %all_to_all.38.parts_ref = bf16[16,16,1280]{2,1,0:T(8,128)(2,1)S(1)} all-to-all(bf16[16,16,1280]{2,1,0:T(8,128)(2,1)S(1)} %get-tuple-element.26), channel_id=1, replica_groups=mesh['prow_0'=2,'prow_1'=8,'pcol_0'=4,'pcol_1'=4,'pcol_2'=2] {'prow_0','..., dimensions={0} | all-to-all | bytes 1310720 | tf_op jit(solution)/shard_map/all_to_all | solution.py:359
  (45 shorter events, 19.1 us)
Async XLA Ops:
  0.6 59.0 %copy-start.11 = (f32[1280]{0:T(1024)S(1)}, f32[1280]{0:T(1024)}, u32[]{:S(2)}) copy-start(f32[1280]{0:T(1024)} %param.13) | copy-start | bytes 15364
  0.6 59.0 %copy-start.4 = (f32[3,1280]{1,0:T(4,128)S(1)}, f32[3,1280]{1,0:T(4,128)}, u32[]{:S(2)}) copy-start(f32[3,1280]{1,0:T(4,128)} %shift_ref.3) | copy-start | bytes 46084
  0.7 59.0 %copy-start.3 = (f32[3,1280]{1,0:T(4,128)S(1)}, f32[3,1280]{1,0:T(4,128)}, u32[]{:S(2)}) copy-start(f32[3,1280]{1,0:T(4,128)} %scale_ref.3) | copy-start | bytes 46084
  0.7 59.0 %copy-start.5 = (f32[2,1280]{1,0:T(2,128)S(1)}, f32[2,1280]{1,0:T(2,128)}, u32[]{:S(2)}) copy-start(f32[2,1280]{1,0:T(2,128)} %bias_ref.1) | copy-start | bytes 30724
  0.7 66.1 %copy-start.1 = (bf16[3,3,80,1280]{3,2,1,0:T(8,128)(2,1)S(1)}, bf16[3,3,80,1280]{3,2,1,0:T(8,128)(2,1)}, u32[]{:S(2)}) copy-start(bf16[3,3,80,1280]{3,2,1,0:T(8,128)(2,1)} %param.15) | copy-start | bytes 5529604
  44.9 21.9 %collective-permute-start = (bf16[64,1280]{1,0:T(8,128)(2,1)}, bf16[64,1280]{1,0:T(8,128)(2,1)S(1)}, u32[]{:S(2)}, u32[]{:S(2)}) collective-permute-start(bf16[64,1280]{1,0:T(8,128)(2,1)} %get-tuple-element.16), channel_id=1, source_target_pairs={{0,1},{1,2},{2,3},{3,4},{4,5},{5,6},{6,7},{7,8},{8,9},{9,10},{10,1... | collective-permute-start | bytes 491528 | tf_op jit(solution)/shard_map/ppermute | solution.py:364
  50.0 16.8 %collective-permute-start.1 = (bf16[64,1280]{1,0:T(8,128)(2,1)S(1)}, bf16[64,1280]{1,0:T(8,128)(2,1)S(1)}, u32[]{:S(2)}, u32[]{:S(2)}) collective-permute-start(bf16[64,1280]{1,0:T(8,128)(2,1)S(1)} %get-tuple-element.17), channel_id=1, source_target_pairs={{1,0},{2,1},{3,2},{4,3},{5,4},{6,5},{7,6},{8,7},{9,8},{10,9},{11,1... | collective-permute-start | bytes 491528 | tf_op jit(solution)/shard_map/ppermute | solution.py:364
  51.9 14.9 %all-to-all-start.1 = ((f32[32,1,128]{2,1,0:T(1,128)}), f32[32,1,128]{2,1,0:T(1,128)S(1)}, u32[]{:S(2)}, u32[]{:S(2)}) async-start(f32[32,1,128]{2,1,0:T(1,128)} %get-tuple-element.15), calls=%async_computation.1 | async-start | bytes 32768 | tf_op jit(solution)/shard_map/all_to_all | solution.py:359
  69.5 16.6 %copy-start.9 = (bf16[64,4,1,128]{3,1,2,0:T(4,128)(2,1)S(1)}, bf16[64,4,1,128]{3,1,2,0:T(4,128)(2,1)}, u32[]{:S(2)}) copy-start(bf16[64,4,1,128]{3,1,2,0:T(4,128)(2,1)} %param.19) | copy-start | bytes 196612
  80.3 66.0 %copy-start = (bf16[3,3,80,1280]{3,2,1,0:T(8,128)(2,1)S(1)}, bf16[3,3,80,1280]{3,2,1,0:T(8,128)(2,1)}, u32[]{:S(2)}) copy-start(bf16[3,3,80,1280]{3,2,1,0:T(8,128)(2,1)} %param.16) | copy-start | bytes 5529604
  81.5 64.8 %all-to-all-start.3 = ((bf16[16,80,256]{2,1,0:T(8,128)(2,1)}), bf16[16,80,256]{2,1,0:T(8,128)(2,1)S(1)}, u32[]{:S(2)}, u32[]{:S(2)}) async-start(bf16[16,80,256]{2,1,0:T(8,128)(2,1)} %shard_map.117), calls=%async_computation.3 | async-start | bytes 1310720 | tf_op jit(solution)/shard_map/all_to_all | solution.py:359
  86.1 6.4 %collective-permute-start.4 = (bf16[1,256,128]{2,1,0:T(8,128)(2,1)S(1)}, bf16[1,256,128]{2,1,0:T(8,128)(2,1)S(1)}, u32[]{:S(2)}, u32[]{:S(2)}) collective-permute-start(bf16[1,256,128]{2,1,0:T(8,128)(2,1)S(1)} %bitcast.15), channel_id=1, source_target_pairs={{0,8},{8,0},{16,24},{24,16},{1,9},{9,1},{17,25},{25,17},{2,10},{10... | collective-permute-start | bytes 196616 | tf_op jit(solution)/shard_map/ppermute | solution.py:383
  92.5 0.6 copy-start.10
  98.2 10.5 %collective-permute-start.5 = (bf16[2,256,128]{2,1,0:T(8,128)(2,1)}, bf16[2,256,128]{2,1,0:T(8,128)(2,1)S(1)}, u32[]{:S(2)}, u32[]{:S(2)}) collective-permute-start(bf16[2,256,128]{2,1,0:T(8,128)(2,1)} %shard_map.122.left_ref), channel_id=1, source_target_pairs={{0,16},{8,24},{16,0},{24,8},{1,17},{9,25},{17,1},{25,9},{2,18},{10... | collective-permute-start | bytes 393224 | tf_op jit(solution)/shard_map/ppermute | solution.py:383
  108.7 0.6 copy-start.8
  118.4 7.3 %collective-permute-start.6 = (bf16[4,256,128]{2,1,0:T(8,128)(2,1)}, bf16[4,256,128]{2,1,0:T(8,128)(2,1)S(1)}, u32[]{:S(2)}, u32[]{:S(2)}) collective-permute-start(bf16[4,256,128]{2,1,0:T(8,128)(2,1)} %shard_map.123.left_ref), channel_id=1, source_target_pairs={{0,2},{2,0},{4,6},{6,4},{1,3},{3,1},{5,7},{7,5},{8,10},{10,8},{12,... | collective-permute-start | bytes 786440 | tf_op jit(solution)/shard_map/ppermute | solution.py:383
  125.7 0.7 copy-start.7
  143.5 55.3 %collective-permute-start.7 = (bf16[8,256,128]{2,1,0:T(8,128)(2,1)}, bf16[8,256,128]{2,1,0:T(8,128)(2,1)}, u32[]{:S(2)}, u32[]{:S(2)}) collective-permute-start(bf16[8,256,128]{2,1,0:T(8,128)(2,1)} %shard_map.124.left_ref), channel_id=1, source_target_pairs={{0,4},{2,6},{4,0},{6,2},{1,5},{3,7},{5,1},{7,3},{8,12},{10,14},{12... | collective-permute-start | bytes 1572872 | tf_op jit(solution)/shard_map/ppermute | solution.py:383
  147.1 13.8 %collective-permute-start.2 = (f32[80,64]{1,0:T(8,128)S(1)}, f32[80,64]{1,0:T(8,128)S(1)}, u32[]{:S(2)}, u32[]{:S(2)}) collective-permute-start(f32[80,64]{1,0:T(8,128)S(1)} %get-tuple-element.21), channel_id=1, source_target_pairs={{0,1},{1,2},{2,3},{3,4},{4,5},{5,6},{6,7},{7,8},{8,9},{9,10},{10,1... | collective-permute-start | bytes 61448 | tf_op jit(solution)/shard_map/ppermute | solution.py:364
  158.9 5.7 %collective-permute-start.3 = (f32[80,64]{1,0:T(8,128)S(1)}, f32[80,64]{1,0:T(8,128)S(1)}, u32[]{:S(2)}, u32[]{:S(2)}) collective-permute-start(f32[80,64]{1,0:T(8,128)S(1)} %get-tuple-element.22), channel_id=1, source_target_pairs={{1,0},{2,1},{3,2},{4,3},{5,4},{6,5},{7,6},{8,7},{9,8},{10,9},{11,1... | collective-permute-start | bytes 61448 | tf_op jit(solution)/shard_map/ppermute | solution.py:364
  180.1 56.8 %all-to-all-start.5 = ((bf16[16,80,256]{2,1,0:T(8,128)(2,1)}), bf16[16,80,256]{2,1,0:T(8,128)(2,1)S(1)}, u32[]{:S(2)}, u32[]{:S(2)}) async-start(bf16[16,80,256]{2,1,0:T(8,128)(2,1)} %shard_map.120), calls=%async_computation.5 | async-start | bytes 1310720 | tf_op jit(solution)/shard_map/all_to_all | solution.py:359
  198.7 39.2 %copy-start.2 = (bf16[192,1280]{1,0:T(8,128)(2,1)S(1)}, bf16[192,1280]{1,0:T(8,128)(2,1)}, u32[]{:S(2)}) copy-start(bf16[192,1280]{1,0:T(8,128)(2,1)} %w_ref.1) | copy-start | bytes 1474564
  231.6 5.3 %collective-permute-start.8 = (bf16[16,256,128]{2,1,0:T(8,128)(2,1)}, bf16[16,256,128]{2,1,0:T(8,128)(2,1)S(1)}, u32[]{:S(2)}, u32[]{:S(2)}) collective-permute-start(bf16[16,256,128]{2,1,0:T(8,128)(2,1)} %shard_map.125.near_ref), channel_id=1, source_target_pairs={{0,1},{1,0},{2,3},{3,2},{4,5},{5,4},{6,7},{7,6},{8,9},{9,8},{10,11... | collective-permute-start | bytes 3145736 | tf_op jit(solution)/shard_map/ppermute | solution.py:383
  236.9 1.0 copy-start.6

commit v5 on v4

--- a/solution.py
+++ b/solution.py
@@ -289,10 +289,15 @@
     held_ref,
     sems,
 ):
-    copies = [
-        pltpu.make_async_copy(half, held_ref.at[k], sems.at[k])
-        for k, half in enumerate((near_ref, far_ref))
-    ]
+    chunk = 4
+    copies = []
+    for step in range(NS // chunk):
+        half, start = divmod(chunk * step, NS // 2)
+        strips = pl.ds(start, chunk)
+        source = (near_ref, far_ref)[half].at[strips]
+        copies.append(
+            pltpu.make_async_copy(source, held_ref.at[half, strips], sems.at[step])
+        )
     for copy in copies:
         copy.start()
     mapped = nn(w_ref[...], x_ref[...])
@@ -302,14 +307,12 @@
     queries = jnp.concatenate([queries, jnp.zeros((CELLS, HEAD), BF16)], axis=1)
     order = cell_order()
     fresh_ref[...] = nn(order, fresh).astype(BF16)
-    chunk = 4
     highest = jnp.full((CELLS, 1), -jnp.inf, F32)
     denominator = jnp.zeros((CELLS, 1), F32)
     weighted = jnp.zeros((CELLS, 2 * HEAD), F32)
     for step in range(NS // chunk):
         half, start = divmod(chunk * step, NS // 2)
-        if start == 0:
-            copies[half].wait()
+        copies[step].wait()
         pairs = held_ref[half, start : start + chunk].reshape(chunk * CELLS, 2 * HEAD)
         if step == 0:
             pairs = jnp.concatenate([fresh, pairs[CELLS:]], axis=0)
@@ -384,11 +387,7 @@
         if step < len(HOPS) - 1:
             out = ((2 * near.shape[0], CELLS, 2 * HEAD), BF16)
             (near,) = call(
-                join_kernel,
-                [out],
-                outer=2,
-                space=pltpu.HBM,
-                scratch=[pltpu.SemaphoreType.DMA((2,))],
+                join_kernel, [out], space=pltpu.HBM, scratch=[pltpu.SemaphoreType.DMA((2,))]
             )(near, far)
     sums_out = ((NS, 1, 128), F32)
     every = ((NP, OC, CELLS), BF16)
@@ -444,7 +443,7 @@
         mib=16,
         scratch=[
             pltpu.VMEM((2, NS // 2, CELLS, 2 * HEAD), BF16),
-            pltpu.SemaphoreType.DMA((2,)),
+            pltpu.SemaphoreType.DMA((NS // 4,)),
         ],
     )(at, field, w_qkv, w_part, resnet, near, far)
     (out,) = call(output_kernel, [((PC, PC, C), BF16)])(to_every(parts, PROW))

time: 281 us -> 228 us (0.81)
  Pallas kernels: 81.1 us -> 21.3 us
  waiting for transfers between devices: 29.8 us -> 49.5 us
  blocking collectives: 99.4 us -> 92.6 us
  starting transfers between devices: 63.9 us -> 58.1 us
    pallas_call x15, Pallas kernels: 81.1 us -> 21.3 us  [run(): pl.pallas_call(kernel, out_shape=[pltpu.HBM(*out) if space is pltpu.HBM e...]
    all_to_all x3, waiting for transfers between devices: 6.27 us -> 20.8 us  [to_every(): return lax.all_to_all(copies, axis, split_axis=0, concat_axis=0, tiled=True)]
    all_to_all x4, blocking collectives: 99.4 us -> 92.6 us  [to_every(): return lax.all_to_all(copies, axis, split_axis=0, concat_axis=0, tiled=True)]
    ppermute x5, waiting for transfers between devices: 19.7 us -> 25.4 us  [shards(): far = lax.ppermute(near, axis, [(i, i ^ bit) for i in range(count)])]
    ppermute x4, starting transfers between devices: 20.7 us -> 16.7 us  [beside(): return lax.ppermute(value, PCOL, pairs)]
  transfers between devices with their start and end apart: 12 -> 12, of which waited for: 6 -> 7; matrix products, arithmetic and copies ran while one was open for 0% -> 0% of each run, Pallas kernels for 24% -> 3%
where the time goes in v5:
time: 228 us; the launch traced here: 226 us
  blocking collectives  92.6 us (41%)
  starting transfers between devices  58.1 us (25%)
  waiting for transfers between devices  49.5 us (22%)
  Pallas kernels  21.3 us (9%)
  local copies, waits for them, and re-layouts  3.39 us (1%)
    all_to_all x4, blocking collectives, to_every(): return lax.all_to_all(copies, axis, split_axis=0, concat_axis=0, tiled=True)  92.6 us
    all_to_all x3, starting transfers between devices, to_every(): return lax.all_to_all(copies, axis, split_axis=0, concat_axis=0, tiled=True)  28.8 us
    ppermute x5, waiting for transfers between devices, shards(): far = lax.ppermute(near, axis, [(i, i ^ bit) for i in range(count)])  25.4 us
    pallas_call x15, Pallas kernels, run(): pl.pallas_call(kernel, out_shape=[pltpu.HBM(*out) if space is pltpu.HBM e...  21.3 us
    all_to_all x3, waiting for transfers between devices, to_every(): return lax.all_to_all(copies, axis, split_axis=0, concat_axis=0, tiled=True)  20.8 us
    ppermute x4, starting transfers between devices, beside(): return lax.ppermute(value, PCOL, pairs)  16.7 us
    ppermute x5, starting transfers between devices, shards(): far = lax.ppermute(near, axis, [(i, i ^ bit) for i in range(count)])  12.6 us
  transfers between devices with their start and end apart: 12, of which 7 were waited for; matrix products, arithmetic and copies ran while one was open for 0% of the time, Pallas kernels for 3%

profile of v5, /device:TPU:1, one launch (start us, length us, event | category | flops | bytes accessed | tf_op | source)
XLA Modules:
  0.0 226.0 jit_solution(4346510206929367498)
XLA Ops:
  1.9 41.6 %all_to_all.35.block_ref = bf16[16,208,128]{2,1,0:T(8,128)(2,1)S(1)} all-to-all(bf16[16,208,128]{2,1,0:T(8,128)(2,1)S(1)} %shard_map.113), channel_id=1, replica_groups=mesh['prow_0'=2,'prow_1'=8,'pcol_0'=4,'pcol_1'=4,'pcol_2'=2] {'prow_0','..., dimensions={0} | all-to-all | bytes 1703936 | tf_op jit(solution)/shard_map/all_to_all | solution.py:362
  44.9 5.0 %collective-permute-start = (bf16[64,1280]{1,0:T(8,128)(2,1)S(1)}, bf16[64,1280]{1,0:T(8,128)(2,1)S(1)}, u32[]{:S(2)}, u32[]{:S(2)}) collective-permute-start(bf16[64,1280]{1,0:T(8,128)(2,1)S(1)} %get-tuple-element.16), channel_id=1, source_target_pairs={{0,1},{1,2},{2,3},{3,4},{4,5},{5,6},{6,7},{7,8},{8,9},{9,10},{10,1... | collective-permute-start | bytes 491528 | tf_op jit(solution)/shard_map/ppermute | solution.py:367
  50.0 1.9 collective-permute-start.1
  51.9 7.6 %all-to-all-start.1 = ((f32[32,1,128]{2,1,0:T(1,128)}), f32[32,1,128]{2,1,0:T(1,128)S(1)}, u32[]{:S(2)}, u32[]{:S(2)}) async-start(f32[32,1,128]{2,1,0:T(1,128)} %get-tuple-element.15), calls=%async_computation.1 | async-start | bytes 32768 | tf_op jit(solution)/shard_map/all_to_all | solution.py:362
  60.5 6.3 %all-to-all-done.1.sums_ref = f32[32,1,128]{2,1,0:T(1,128)S(1)} async-done(((f32[32,1,128]{2,1,0:T(1,128)}), f32[32,1,128]{2,1,0:T(1,128)S(1)}, u32[]{:S(2)}, u32[]{:S(2)}) %all-to-all-start.1) | async-done | bytes 16416 | tf_op jit(solution)/shard_map/all_to_all | solution.py:362
  66.8 2.7 %shard_map.116 = (f32[80,256]{1,0:T(8,128)S(1)}, f32[32,1,128]{2,1,0:T(1,128)S(1)}, f32[80,256]{1,0:T(8,128)S(1)}) custom-call(s32[2]{0:T(128)S(1)} %pad_add_fusion.at_ref, bf16[16,208,128]{2,1,0:T(8,128)(2,1)S(1)} %all_to_all.35.block_ref, f32[32,1,128]{2,1,0:T(1,128)S(1)} %all-to-all-done.1.sums_ref, f32[3,1280]{1,0:T(4,128)S(1)} %copy-done.6, ...), custom_call_target="tpu_custom_call" | custom-call | tf_op jit(solution)/shard_map/pallas_call | solution.py:347
  69.5 10.8 %all_to_all.36.sums_ref = f32[32,1,128]{2,1,0:T(1,128)S(1)} all-to-all(f32[32,1,128]{2,1,0:T(1,128)S(1)} %get-tuple-element.19), channel_id=1, replica_groups=mesh['prow_0'=2,'prow_1'=8,'pcol_0'=4,'pcol_1'=4,'pcol_2'=2] {'pcol_0','..., dimensions={0} | all-to-all | bytes 32768 | tf_op jit(solution)/shard_map/all_to_all | solution.py:362
  81.6 4.5 %all-to-all-start.3 = ((bf16[16,80,256]{2,1,0:T(8,128)(2,1)}), bf16[16,80,256]{2,1,0:T(8,128)(2,1)S(1)}, u32[]{:S(2)}, u32[]{:S(2)}) async-start(bf16[16,80,256]{2,1,0:T(8,128)(2,1)} %shard_map.117), calls=%async_computation.3 | async-start | bytes 1310720 | tf_op jit(solution)/shard_map/all_to_all | solution.py:362
  86.1 2.2 collective-permute-start.4
  88.3 4.2 %collective-permute-done.4.right_ref = bf16[1,256,128]{2,1,0:T(8,128)(2,1)S(1)} collective-permute-done((bf16[1,256,128]{2,1,0:T(8,128)(2,1)S(1)}, bf16[1,256,128]{2,1,0:T(8,128)(2,1)S(1)}, u32[]{:S(2)}, u32[]{:S(2)}) %collective-permute-start.4) | collective-permute-done | bytes 65568 | tf_op jit(solution)/shard_map/ppermute | solution.py:386
  93.2 2.4 %collective-permute-start.5 = (bf16[2,256,128]{2,1,0:T(8,128)(2,1)}, bf16[2,256,128]{2,1,0:T(8,128)(2,1)S(1)}, u32[]{:S(2)}, u32[]{:S(2)}) collective-permute-start(bf16[2,256,128]{2,1,0:T(8,128)(2,1)} %shard_map.122.left_ref), channel_id=1, source_target_pairs={{0,16},{8,24},{16,0},{24,8},{1,17},{9,25},{17,1},{25,9},{2,18},{10... | collective-permute-start | bytes 393224 | tf_op jit(solution)/shard_map/ppermute | solution.py:386
  95.6 13.8 %collective-permute-done.5.right_ref = bf16[2,256,128]{2,1,0:T(8,128)(2,1)S(1)} collective-permute-done((bf16[2,256,128]{2,1,0:T(8,128)(2,1)}, bf16[2,256,128]{2,1,0:T(8,128)(2,1)S(1)}, u32[]{:S(2)}, u32[]{:S(2)}) %collective-permute-start.5) | collective-permute-done | bytes 131104 | tf_op jit(solution)/shard_map/ppermute | solution.py:386
  111.0 2.2 collective-permute-start.6
  113.3 5.1 %collective-permute-done.6.right_ref = bf16[4,256,128]{2,1,0:T(8,128)(2,1)S(1)} collective-permute-done((bf16[4,256,128]{2,1,0:T(8,128)(2,1)}, bf16[4,256,128]{2,1,0:T(8,128)(2,1)S(1)}, u32[]{:S(2)}, u32[]{:S(2)}) %collective-permute-start.6) | collective-permute-done | bytes 262176 | tf_op jit(solution)/shard_map/ppermute | solution.py:386
  120.2 2.8 %collective-permute-start.7 = (bf16[8,256,128]{2,1,0:T(8,128)(2,1)}, bf16[8,256,128]{2,1,0:T(8,128)(2,1)S(1)}, u32[]{:S(2)}, u32[]{:S(2)}) collective-permute-start(bf16[8,256,128]{2,1,0:T(8,128)(2,1)} %shard_map.124.left_ref), channel_id=1, source_target_pairs={{0,4},{2,6},{4,0},{6,2},{1,5},{3,7},{5,1},{7,3},{8,12},{10,14},{12... | collective-permute-start | bytes 1572872 | tf_op jit(solution)/shard_map/ppermute | solution.py:386
  125.2 7.8 %collective-permute-start.2 = (f32[80,64]{1,0:T(8,128)S(1)}, f32[80,64]{1,0:T(8,128)S(1)}, u32[]{:S(2)}, u32[]{:S(2)}) collective-permute-start(f32[80,64]{1,0:T(8,128)S(1)} %get-tuple-element.21), channel_id=1, source_target_pairs={{0,1},{1,2},{2,3},{3,4},{4,5},{5,6},{6,7},{7,8},{8,9},{9,10},{10,1... | collective-permute-start | bytes 61448 | tf_op jit(solution)/shard_map/ppermute | solution.py:367
  135.0 3.4 %collective-permute-done.3.from_right_ref = f32[80,64]{1,0:T(8,128)S(1)} collective-permute-done((f32[80,64]{1,0:T(8,128)S(1)}, f32[80,64]{1,0:T(8,128)S(1)}, u32[]{:S(2)}, u32[]{:S(2)}) %collective-permute-start.3) | collective-permute-done | bytes 20512 | tf_op jit(solution)/shard_map/ppermute | solution.py:367
  138.5 13.2 %all_to_all.37.sums_ref = f32[32,1,128]{2,1,0:T(1,128)S(1)} all-to-all(f32[32,1,128]{2,1,0:T(1,128)S(1)} %get-tuple-element.25), channel_id=1, replica_groups=mesh['prow_0'=2,'prow_1'=8,'pcol_0'=4,'pcol_1'=4,'pcol_2'=2] {'pcol_0','..., dimensions={0} | all-to-all | bytes 32768 | tf_op jit(solution)/shard_map/all_to_all | solution.py:362
  152.9 16.7 %all-to-all-start.5 = ((bf16[16,80,256]{2,1,0:T(8,128)(2,1)}), bf16[16,80,256]{2,1,0:T(8,128)(2,1)S(1)}, u32[]{:S(2)}, u32[]{:S(2)}) async-start(bf16[16,80,256]{2,1,0:T(8,128)(2,1)} %shard_map.120), calls=%async_computation.5 | async-start | bytes 1310720 | tf_op jit(solution)/shard_map/all_to_all | solution.py:362
  170.6 3.0 %collective-permute-start.8 = (bf16[16,256,128]{2,1,0:T(8,128)(2,1)}, bf16[16,256,128]{2,1,0:T(8,128)(2,1)}, u32[]{:S(2)}, u32[]{:S(2)}) collective-permute-start(bf16[16,256,128]{2,1,0:T(8,128)(2,1)} %shard_map.125.near_ref), channel_id=1, source_target_pairs={{0,1},{1,0},{2,3},{3,2},{4,5},{5,4},{6,7},{7,6},{8,9},{9,8},{10,11... | collective-permute-start | bytes 3145736 | tf_op jit(solution)/shard_map/ppermute | solution.py:386
  173.8 2.3 %collective-permute-done.8.far_ref = bf16[16,256,128]{2,1,0:T(8,128)(2,1)} collective-permute-done((bf16[16,256,128]{2,1,0:T(8,128)(2,1)}, bf16[16,256,128]{2,1,0:T(8,128)(2,1)}, u32[]{:S(2)}, u32[]{:S(2)}) %collective-permute-start.8) | collective-permute-done | bytes 1048608 | tf_op jit(solution)/shard_map/ppermute | solution.py:386
  176.1 14.5 %all-to-all-done.5 = bf16[16,80,256]{2,1,0:T(8,128)(2,1)S(1)} async-done(((bf16[16,80,256]{2,1,0:T(8,128)(2,1)}), bf16[16,80,256]{2,1,0:T(8,128)(2,1)S(1)}, u32[]{:S(2)}, u32[]{:S(2)}) %all-to-all-start.5) | async-done | bytes 655392 | tf_op jit(solution)/shard_map/all_to_all | solution.py:362
  190.6 7.7 %shard_map.126 = (bf16[16,16,1280]{2,1,0:T(8,128)(2,1)S(1)}, bf16[256,128]{1,0:T(8,128)(2,1)}) custom-call(s32[2]{0:T(128)S(1)} %pad_add_fusion.at_ref, bf16[1280,256]{1,0:T(8,128)(2,1)S(1)} %bitcast.11, bf16[192,1280]{1,0:T(8,128)(2,1)S(1)} %copy-done.5, bf16[1280,128]{1,0:T(8,128)(2,1)S(1)} %shard_map.121.w_out_ref, ...), custom_call_target="tpu_custom_call" | custom-call | tf_op jit(solution)/shard_map/pallas_call | solution.py:347
  198.3 27.0 %all_to_all.38.parts_ref = bf16[16,16,1280]{2,1,0:T(8,128)(2,1)S(1)} all-to-all(bf16[16,16,1280]{2,1,0:T(8,128)(2,1)S(1)} %get-tuple-element.26), channel_id=1, replica_groups=mesh['prow_0'=2,'prow_1'=8,'pcol_0'=4,'pcol_1'=4,'pcol_2'=2] {'prow_0','..., dimensions={0} | all-to-all | bytes 1310720 | tf_op jit(solution)/shard_map/all_to_all | solution.py:362
  (43 shorter events, 16.4 us)
Async XLA Ops:
  0.6 59.0 %copy-start.10 = (f32[1280]{0:T(1024)S(1)}, f32[1280]{0:T(1024)}, u32[]{:S(2)}) copy-start(f32[1280]{0:T(1024)} %param.13) | copy-start | bytes 15364
  0.6 59.0 %copy-start.7 = (f32[3,1280]{1,0:T(4,128)S(1)}, f32[3,1280]{1,0:T(4,128)}, u32[]{:S(2)}) copy-start(f32[3,1280]{1,0:T(4,128)} %shift_ref.3) | copy-start | bytes 46084
  0.7 59.0 %copy-start.6 = (f32[3,1280]{1,0:T(4,128)S(1)}, f32[3,1280]{1,0:T(4,128)}, u32[]{:S(2)}) copy-start(f32[3,1280]{1,0:T(4,128)} %scale_ref.3) | copy-start | bytes 46084
  0.7 59.0 %copy-start.9 = (f32[2,1280]{1,0:T(2,128)S(1)}, f32[2,1280]{1,0:T(2,128)}, u32[]{:S(2)}) copy-start(f32[2,1280]{1,0:T(2,128)} %bias_ref.1) | copy-start | bytes 30724
  0.7 66.1 %copy-start.2 = (bf16[3,3,80,1280]{3,2,1,0:T(8,128)(2,1)S(1)}, bf16[3,3,80,1280]{3,2,1,0:T(8,128)(2,1)}, u32[]{:S(2)}) copy-start(bf16[3,3,80,1280]{3,2,1,0:T(8,128)(2,1)} %param.15) | copy-start | bytes 5529604
  44.9 21.9 %collective-permute-start = (bf16[64,1280]{1,0:T(8,128)(2,1)S(1)}, bf16[64,1280]{1,0:T(8,128)(2,1)S(1)}, u32[]{:S(2)}, u32[]{:S(2)}) collective-permute-start(bf16[64,1280]{1,0:T(8,128)(2,1)S(1)} %get-tuple-element.16), channel_id=1, source_target_pairs={{0,1},{1,2},{2,3},{3,4},{4,5},{5,6},{6,7},{7,8},{8,9},{9,10},{10,1... | collective-permute-start | bytes 491528 | tf_op jit(solution)/shard_map/ppermute | solution.py:367
  50.0 16.8 %collective-permute-start.1 = (bf16[64,1280]{1,0:T(8,128)(2,1)S(1)}, bf16[64,1280]{1,0:T(8,128)(2,1)S(1)}, u32[]{:S(2)}, u32[]{:S(2)}) collective-permute-start(bf16[64,1280]{1,0:T(8,128)(2,1)S(1)} %get-tuple-element.17), channel_id=1, source_target_pairs={{1,0},{2,1},{3,2},{4,3},{5,4},{6,5},{7,6},{8,7},{9,8},{10,9},{11,1... | collective-permute-start | bytes 491528 | tf_op jit(solution)/shard_map/ppermute | solution.py:367
  51.9 14.9 %all-to-all-start.1 = ((f32[32,1,128]{2,1,0:T(1,128)}), f32[32,1,128]{2,1,0:T(1,128)S(1)}, u32[]{:S(2)}, u32[]{:S(2)}) async-start(f32[32,1,128]{2,1,0:T(1,128)} %get-tuple-element.15), calls=%async_computation.1 | async-start | bytes 32768 | tf_op jit(solution)/shard_map/all_to_all | solution.py:362
  69.5 16.6 %copy-start.8 = (bf16[64,4,1,128]{3,1,2,0:T(4,128)(2,1)S(1)}, bf16[64,4,1,128]{3,1,2,0:T(4,128)(2,1)}, u32[]{:S(2)}) copy-start(bf16[64,4,1,128]{3,1,2,0:T(4,128)(2,1)} %param.19) | copy-start | bytes 196612
  81.6 41.4 %all-to-all-start.3 = ((bf16[16,80,256]{2,1,0:T(8,128)(2,1)}), bf16[16,80,256]{2,1,0:T(8,128)(2,1)S(1)}, u32[]{:S(2)}, u32[]{:S(2)}) async-start(bf16[16,80,256]{2,1,0:T(8,128)(2,1)} %shard_map.117), calls=%async_computation.3 | async-start | bytes 1310720 | tf_op jit(solution)/shard_map/all_to_all | solution.py:362
  86.1 6.4 %collective-permute-start.4 = (bf16[1,256,128]{2,1,0:T(8,128)(2,1)S(1)}, bf16[1,256,128]{2,1,0:T(8,128)(2,1)S(1)}, u32[]{:S(2)}, u32[]{:S(2)}) collective-permute-start(bf16[1,256,128]{2,1,0:T(8,128)(2,1)S(1)} %bitcast.14), channel_id=1, source_target_pairs={{0,8},{8,0},{16,24},{24,16},{1,9},{9,1},{17,25},{25,17},{2,10},{10... | collective-permute-start | bytes 196616 | tf_op jit(solution)/shard_map/ppermute | solution.py:386
  93.2 16.2 %collective-permute-start.5 = (bf16[2,256,128]{2,1,0:T(8,128)(2,1)}, bf16[2,256,128]{2,1,0:T(8,128)(2,1)S(1)}, u32[]{:S(2)}, u32[]{:S(2)}) collective-permute-start(bf16[2,256,128]{2,1,0:T(8,128)(2,1)} %shard_map.122.left_ref), channel_id=1, source_target_pairs={{0,16},{8,24},{16,0},{24,8},{1,17},{9,25},{17,1},{25,9},{2,18},{10... | collective-permute-start | bytes 393224 | tf_op jit(solution)/shard_map/ppermute | solution.py:386
  109.4 0.9 copy-start.4
  111.0 7.3 %collective-permute-start.6 = (bf16[4,256,128]{2,1,0:T(8,128)(2,1)}, bf16[4,256,128]{2,1,0:T(8,128)(2,1)S(1)}, u32[]{:S(2)}, u32[]{:S(2)}) collective-permute-start(bf16[4,256,128]{2,1,0:T(8,128)(2,1)} %shard_map.123.left_ref), channel_id=1, source_target_pairs={{0,2},{2,0},{4,6},{6,4},{1,3},{3,1},{5,7},{7,5},{8,10},{10,8},{12,... | collective-permute-start | bytes 786440 | tf_op jit(solution)/shard_map/ppermute | solution.py:386
  118.4 1.0 copy-start.3
  120.2 49.4 %collective-permute-start.7 = (bf16[8,256,128]{2,1,0:T(8,128)(2,1)}, bf16[8,256,128]{2,1,0:T(8,128)(2,1)S(1)}, u32[]{:S(2)}, u32[]{:S(2)}) collective-permute-start(bf16[8,256,128]{2,1,0:T(8,128)(2,1)} %shard_map.124.left_ref), channel_id=1, source_target_pairs={{0,4},{2,6},{4,0},{6,2},{1,5},{3,7},{5,1},{7,3},{8,12},{10,14},{12... | collective-permute-start | bytes 1572872 | tf_op jit(solution)/shard_map/ppermute | solution.py:386
  122.9 1.5 copy-start.1
  124.4 45.2 %copy-start = (bf16[8,256,128]{2,1,0:T(8,128)(2,1)S(1)}, bf16[8,256,128]{2,1,0:T(8,128)(2,1)}, u32[]{:S(2)}) copy-start(bf16[8,256,128]{2,1,0:T(8,128)(2,1)} %shard_map.124.left_ref) | copy-start | bytes 1572868
  125.2 9.7 %collective-permute-start.2 = (f32[80,64]{1,0:T(8,128)S(1)}, f32[80,64]{1,0:T(8,128)S(1)}, u32[]{:S(2)}, u32[]{:S(2)}) collective-permute-start(f32[80,64]{1,0:T(8,128)S(1)} %get-tuple-element.21), channel_id=1, source_target_pairs={{0,1},{1,2},{2,3},{3,4},{4,5},{5,6},{6,7},{7,8},{8,9},{9,10},{10,1... | collective-permute-start | bytes 61448 | tf_op jit(solution)/shard_map/ppermute | solution.py:367
  133.0 5.3 %collective-permute-start.3 = (f32[80,64]{1,0:T(8,128)S(1)}, f32[80,64]{1,0:T(8,128)S(1)}, u32[]{:S(2)}, u32[]{:S(2)}) collective-permute-start(f32[80,64]{1,0:T(8,128)S(1)} %get-tuple-element.22), channel_id=1, source_target_pairs={{1,0},{2,1},{3,2},{4,3},{5,4},{6,5},{7,6},{8,7},{9,8},{10,9},{11,1... | collective-permute-start | bytes 61448 | tf_op jit(solution)/shard_map/ppermute | solution.py:367
  152.9 37.7 %all-to-all-start.5 = ((bf16[16,80,256]{2,1,0:T(8,128)(2,1)}), bf16[16,80,256]{2,1,0:T(8,128)(2,1)S(1)}, u32[]{:S(2)}, u32[]{:S(2)}) async-start(bf16[16,80,256]{2,1,0:T(8,128)(2,1)} %shard_map.120), calls=%async_computation.5 | async-start | bytes 1310720 | tf_op jit(solution)/shard_map/all_to_all | solution.py:362
  169.6 21.0 %copy-start.5 = (bf16[192,1280]{1,0:T(8,128)(2,1)S(1)}, bf16[192,1280]{1,0:T(8,128)(2,1)}, u32[]{:S(2)}) copy-start(bf16[192,1280]{1,0:T(8,128)(2,1)} %w_ref.1) | copy-start | bytes 1474564
  170.6 5.4 %collective-permute-start.8 = (bf16[16,256,128]{2,1,0:T(8,128)(2,1)}, bf16[16,256,128]{2,1,0:T(8,128)(2,1)}, u32[]{:S(2)}, u32[]{:S(2)}) collective-permute-start(bf16[16,256,128]{2,1,0:T(8,128)(2,1)} %shard_map.125.near_ref), channel_id=1, source_target_pairs={{0,1},{1,0},{2,3},{3,2},{4,5},{5,4},{6,7},{7,6},{8,9},{9,8},{10,11... | collective-permute-start | bytes 3145736 | tf_op jit(solution)/shard_map/ppermute | solution.py:386

commit v6 on v5

--- a/solution.py
+++ b/solution.py
@@ -104,7 +104,7 @@
         out_ref[2 * k + 1, ROWS:, :] = halves(turned, w)
 
 
-def unpack_kernel(block_ref, out_ref):
+def unpack_kernel(block_ref, out_hbm, out_ref, sem):
     lane = iota((PIECE, 128), 1)
     for p in range(NP):
         piece = block_ref[p, ROWS:, :].astype(F32)
@@ -112,6 +112,9 @@
         low = jnp.where(lane >= HEAD, piece, 0.0)
         both = jnp.concatenate([high, low[: OC - PIECE]], axis=0)
         out_ref[OC * p : OC * (p + 1), :] = both.astype(BF16)
+    copy = pltpu.make_async_copy(out_ref, out_hbm, sem)
+    copy.start()
+    copy.wait()
 
 
 def columns_kernel(at_ref, scale_ref, shift_ref, bias_ref, time_ref, out_ref):
@@ -132,20 +135,26 @@
     out_ref[...] = total
 
 
+def by_parity(at_ref, one, other):
+    even = at_ref[1] % 2 == 0
+    return jnp.where(even, one, other), jnp.where(even, other, one)
+
+
 def strip_chunk(block_ref, j):
     return block_ref[:, NP * j : NP * (j + 1), :].reshape(CELLS, 128)
 
 
-def stats_cells_kernel(block_ref, out_ref, leftmost_ref, rightmost_ref):
+def stats_cells_kernel(at_ref, block_ref, out_ref, inner_ref, outer_ref):
     firsts, seconds = [], []
     row = iota((2 * LR, CELLS), 0)
-    wanted = jnp.where(row < LR, row * PC, (row - LR) * PC + PC - 1)
+    inner, outer = by_parity(at_ref, PC - 1, 0)
+    wanted = jnp.where(row < LR, row * PC + inner, (row - LR) * PC + outer)
     pick = one_hot(iota((2 * LR, CELLS), 1) == wanted, BF16)
     for j in range(C // 128):
         x = strip_chunk(block_ref, j)
         edges = nn(pick, x).astype(BF16)
-        leftmost_ref[:, 128 * j : 128 * (j + 1)] = edges[:LR]
-        rightmost_ref[:, 128 * j : 128 * (j + 1)] = edges[LR:]
+        inner_ref[:, 128 * j : 128 * (j + 1)] = edges[:LR]
+        outer_ref[:, 128 * j : 128 * (j + 1)] = edges[LR:]
         x = x.astype(F32)
         firsts.append(jnp.sum(x, axis=0, keepdims=True))
         seconds.append(jnp.sum(x * x, axis=0, keepdims=True))
@@ -192,8 +201,8 @@
     scale_ref,
     shift_ref,
     w_ref,
-    left_ref,
-    right_ref,
+    inner_ref,
+    outer_ref,
     cols_ref,
     total_ref,
     out_sums_ref,
@@ -208,9 +217,10 @@
     chunks = [strip_chunk(block_ref, j) for j in range(C // 128)]
     cells = nn(strip_order(), jnp.concatenate(chunks, axis=1))
     pick = one_hot(iota((OC, C), 1) == iota((OC, C), 0) + at_ref[0] * OC, BF16)
-    own_ref[...] = nt(pick, cells.astype(BF16))
+    own_ref[...] = nt(pick, cells.astype(BF16)).astype(BF16)
     _, mid, _ = tap_columns(nt(w_ref[...], silu(cells * gain + offset).astype(BF16)))
-    sides = jnp.concatenate([left_ref[...], right_ref[...]], axis=0).astype(F32)
+    right, left = by_parity(at_ref, inner_ref[...].astype(F32), outer_ref[...].astype(F32))
+    sides = jnp.concatenate([left, right], axis=0)
     sides = silu(sides * gain + offset)
     row = iota((2 * LR, 1), 0)
     first = jnp.where(at_ref[1] > 0, 0, LR)
@@ -224,10 +234,11 @@
     own_sums(total, out_sums_ref)
 
 
-def conv_channels_kernel(x_ref, w_ref, mid_ref, to_left_ref, to_right_ref):
+def conv_channels_kernel(at_ref, x_ref, w_ref, mid_ref, inner_ref, outer_ref):
     before, mid, after = tap_columns(nn(w_ref[...], x_ref[...]))
-    to_right_ref[...] = before[:, CELLS - LR :]
-    to_left_ref[...] = after[:, :LR]
+    inner, outer = by_parity(at_ref, before[:, CELLS - LR :], after[:, :LR])
+    inner_ref[...] = inner
+    outer_ref[...] = outer
     mid_ref[...] = mid
 
 
@@ -245,9 +256,10 @@
     sums_ref[...] = jnp.broadcast_to(row[None], sums_ref.shape)
 
 
-def finish_kernel(mid_ref, from_left_ref, from_right_ref, cols_ref, own_ref, total_ref, sums_ref):
-    total = with_sides(mid_ref[...], from_left_ref[...], from_right_ref[...])
-    total = (own_ref[...] + total + cols_ref[:, 3:4]).astype(BF16)
+def finish_kernel(at_ref, mid_ref, inner_ref, outer_ref, cols_ref, own_ref, total_ref, sums_ref):
+    right, left = by_parity(at_ref, inner_ref[...], outer_ref[...])
+    total = with_sides(mid_ref[...], left, right)
+    total = (own_ref[...].astype(F32) + total + cols_ref[:, 3:4]).astype(BF16)
     total_ref[...] = total
     own_sums(total.astype(F32), sums_ref)
 
@@ -282,24 +294,16 @@
     w_ref,
     w_out_ref,
     own_ref,
-    near_ref,
     far_ref,
+    near_hbm,
     part_ref,
     fresh_ref,
-    held_ref,
-    sems,
+    near_ref,
+    sem,
 ):
     chunk = 4
-    copies = []
-    for step in range(NS // chunk):
-        half, start = divmod(chunk * step, NS // 2)
-        strips = pl.ds(start, chunk)
-        source = (near_ref, far_ref)[half].at[strips]
-        copies.append(
-            pltpu.make_async_copy(source, held_ref.at[half, strips], sems.at[step])
-        )
-    for copy in copies:
-        copy.start()
+    copy = pltpu.make_async_copy(near_hbm, near_ref, sem)
+    copy.start()
     mapped = nn(w_ref[...], x_ref[...])
     queries = jnp.transpose(mapped[:HEAD]).astype(BF16)
     fresh = jnp.transpose(mapped[HEAD:]).astype(BF16)
@@ -312,9 +316,11 @@
     weighted = jnp.zeros((CELLS, 2 * HEAD), F32)
     for step in range(NS // chunk):
         half, start = divmod(chunk * step, NS // 2)
-        copies[step].wait()
-        pairs = held_ref[half, start : start + chunk].reshape(chunk * CELLS, 2 * HEAD)
-        if step == 0:
+        if half == 1 and start == 0:
+            copy.wait()
+        pairs = (far_ref, near_ref)[half][start : start + chunk]
+        pairs = pairs.reshape(chunk * CELLS, 2 * HEAD)
+        if half == 1 and start == 0:
             pairs = jnp.concatenate([fresh, pairs[CELLS:]], axis=0)
         scores = nt(queries, pairs)
         raised = jnp.maximum(highest, jnp.max(scores, axis=1, keepdims=True))
@@ -362,9 +368,10 @@
     return lax.all_to_all(copies, axis, split_axis=0, concat_axis=0, tiled=True)
 
 
-def beside(value, step):
-    pairs = [(i, i + step) for i in range(NS) if 0 <= i + step < NS]
-    return lax.ppermute(value, PCOL, pairs)
+def swapped(inner, outer):
+    pairs = [(i, j) for i in range(NS) if 0 <= (j := i + 1 if i % 2 else i - 1) < NS]
+    outer = lax.ppermute(outer, PCOL, pairs)
+    return lax.ppermute(inner, PCOL[-1], [(0, 1), (1, 0)]), outer
 
 
 def shards(
@@ -413,39 +420,43 @@
         ],
     )(latent, w_out)
     block = to_every(block, PROW)
-    sums, leftmost, rightmost = call(stats_cells_kernel, [sums_out, edge, edge])(block)
+    sums, inner, outer = call(stats_cells_kernel, [sums_out, edge, edge], scalars=1)(at, block)
     sums = to_every(sums, PCOL)
-    left, right = beside(rightmost, 1), beside(leftmost, -1)
-    (w_part,) = call(unpack_kernel, [((C, 128), BF16)])(block)
-    total, sums, own = call(conv_cells_kernel, [tile, sums_out, tile], scalars=1)(
+    inner, outer = swapped(inner, outer)
+    (w_part,) = call(
+        unpack_kernel,
+        [((C, 128), BF16)],
+        space=pltpu.HBM,
+        scratch=[pltpu.VMEM((C, 128), BF16), pltpu.SemaphoreType.DMA],
+    )(block)
+    total, sums, own = call(conv_cells_kernel, [tile, sums_out, ((OC, CELLS), BF16)], scalars=1)(
         at,
         block,
         sums,
         norm_scale,
         norm_shift,
         conv_one.reshape(9 * OC, C),
-        left,
-        right,
+        inner,
+        outer,
         cols,
     )
     field = gathered(0, total, sums)
-    mid, left, right = call(
-        conv_channels_kernel, [tile, ((OC, LR), F32), ((OC, LR), F32)]
-    )(field, conv_two.reshape(9 * OC, C))
-    left, right = beside(right, 1), beside(left, -1)
-    resnet, sums = call(finish_kernel, [((OC, CELLS), BF16), sums_out])(mid, left, right, cols, own)
+    mid, inner, outer = call(
+        conv_channels_kernel, [tile, ((OC, LR), F32), ((OC, LR), F32)], scalars=1
+    )(at, field, conv_two.reshape(9 * OC, C))
+    inner, outer = swapped(inner, outer)
+    resnet, sums = call(finish_kernel, [((OC, CELLS), BF16), sums_out], scalars=1)(
+        at, mid, inner, outer, cols, own
+    )
     field = gathered(1, resnet, sums)
     parts, fresh = call(
         attention_kernel,
         [((NP, NP, C), BF16), ((CELLS, 2 * HEAD), BF16)],
         scalars=1,
-        outer=2,
+        outer=1,
         mib=16,
-        scratch=[
-            pltpu.VMEM((2, NS // 2, CELLS, 2 * HEAD), BF16),
-            pltpu.SemaphoreType.DMA((NS // 4,)),
-        ],
-    )(at, field, w_qkv, w_part, resnet, near, far)
+        scratch=[pltpu.VMEM((NS // 2, CELLS, 2 * HEAD), BF16), pltpu.SemaphoreType.DMA],
+    )(at, field, w_qkv, w_part, resnet, far, near)
     (out,) = call(output_kernel, [((PC, PC, C), BF16)])(to_every(parts, PROW))
     return out, fresh.reshape(LR, PC, 1, 2 * HEAD)
 

time: 228 us -> 232 us (1.018)
  blocking collectives: 92.6 us -> 49.6 us
  waiting for transfers between devices: 49.5 us -> 72.6 us
  starting transfers between devices: 58.1 us -> 76.7 us
  Pallas kernels: 21.3 us -> 23.7 us
    all_to_all x4 -> x3, blocking collectives: 92.6 us -> 49.6 us  [to_every(): return lax.all_to_all(copies, axis, split_axis=0, concat_axis=0, tiled=True)]
    all_to_all x3 -> x4, waiting for transfers between devices: 20.8 us -> 45.5 us  [to_every(): return lax.all_to_all(copies, axis, split_axis=0, concat_axis=0, tiled=True)]
    all_to_all x3 -> x4, starting transfers between devices: 28.8 us -> 46.3 us  [to_every(): return lax.all_to_all(copies, axis, split_axis=0, concat_axis=0, tiled=True)]
    pallas_call x15, Pallas kernels: 21.3 us -> 23.7 us  [run(): pl.pallas_call(kernel, out_shape=[pltpu.HBM(*out) if space is pltpu.HBM e...]
    unnamed x22 -> x24, local copies, waits for them, and re-layouts: 3.39 us -> 5.38 us
  transfers between devices with their start and end apart: 12 -> 13, of which waited for: 7 -> 8; matrix products, arithmetic and copies ran while one was open for 0% -> 0% of each run, Pallas kernels for 3% -> 4%
where the time goes in v6:
time: 232 us; the launch traced here: 229 us
  starting transfers between devices  76.7 us (33%)
  waiting for transfers between devices  72.6 us (31%)
  blocking collectives  49.6 us (21%)
  Pallas kernels  23.7 us (10%)
  local copies, waits for them, and re-layouts  5.39 us (2%)
    all_to_all x3, blocking collectives, to_every(): return lax.all_to_all(copies, axis, split_axis=0, concat_axis=0, tiled=True)  49.6 us
    all_to_all x4, starting transfers between devices, to_every(): return lax.all_to_all(copies, axis, split_axis=0, concat_axis=0, tiled=True)  46.3 us
    all_to_all x4, waiting for transfers between devices, to_every(): return lax.all_to_all(copies, axis, split_axis=0, concat_axis=0, tiled=True)  45.5 us
    ppermute x5, waiting for transfers between devices, shards(): far = lax.ppermute(near, axis, [(i, i ^ bit) for i in range(count)])  24.7 us
    pallas_call x15, Pallas kernels, run(): pl.pallas_call(kernel, out_shape=[pltpu.HBM(*out) if space is pltpu.HBM e...  23.7 us
    ppermute x5, starting transfers between devices, shards(): far = lax.ppermute(near, axis, [(i, i ^ bit) for i in range(count)])  12.4 us
    ppermute x2, starting transfers between devices, swapped(): return (lax.ppermute(inner, PCOL[-1], [(0, 1), (1, 0)]), outer)  12 us
    ppermute x2, starting transfers between devices, swapped(): outer = lax.ppermute(outer, PCOL, pairs)  5.87 us
  transfers between devices with their start and end apart: 13, of which 8 were waited for; matrix products, arithmetic and copies ran while one was open for 0% of the time, Pallas kernels for 4%

profile of v6, /device:TPU:1, one launch (start us, length us, event | category | flops | bytes accessed | tf_op | source)
XLA Modules:
  0.0 229.0 jit_solution(6632841476394341283)
XLA Ops:
  2.8 16.2 %all-to-all-start = ((bf16[16,208,128]{2,1,0:T(8,128)(2,1)}), bf16[16,208,128]{2,1,0:T(8,128)(2,1)S(1)}, u32[]{:S(2)}, u32[]{:S(2)}) async-start(bf16[16,208,128]{2,1,0:T(8,128)(2,1)} %shard_map.113), calls=%async_computation | async-start | bytes 1703936 | tf_op jit(solution)/shard_map/all_to_all | solution.py:368
  19.1 24.5 %all-to-all-done.block_ref = bf16[16,208,128]{2,1,0:T(8,128)(2,1)S(1)} async-done(((bf16[16,208,128]{2,1,0:T(8,128)(2,1)}), bf16[16,208,128]{2,1,0:T(8,128)(2,1)S(1)}, u32[]{:S(2)}, u32[]{:S(2)}) %all-to-all-start) | async-done | bytes 852000 | tf_op jit(solution)/shard_map/all_to_all | solution.py:368
  45.6 5.2 %collective-permute-start = (bf16[64,1280]{1,0:T(8,128)(2,1)S(1)}, bf16[64,1280]{1,0:T(8,128)(2,1)S(1)}, u32[]{:S(2)}, u32[]{:S(2)}) collective-permute-start(bf16[64,1280]{1,0:T(8,128)(2,1)S(1)} %get-tuple-element.16), channel_id=1, source_target_pairs={{0,1},{1,0},{2,3},{3,2},{4,5},{5,4},{6,7},{7,6},{8,9},{9,8},{10,11... | collective-permute-start | bytes 491528 | tf_op jit(solution)/shard_map/ppermute | solution.py:374
  50.8 3.0 %collective-permute-start.1 = (bf16[64,1280]{1,0:T(8,128)(2,1)S(1)}, bf16[64,1280]{1,0:T(8,128)(2,1)S(1)}, u32[]{:S(2)}, u32[]{:S(2)}) collective-permute-start(bf16[64,1280]{1,0:T(8,128)(2,1)S(1)} %get-tuple-element.17), channel_id=1, source_target_pairs={{1,2},{2,1},{3,4},{4,3},{5,6},{6,5},{7,8},{8,7},{9,10},{10,9},{11,... | collective-permute-start | bytes 491528 | tf_op jit(solution)/shard_map/ppermute | solution.py:373
  53.8 6.8 %all-to-all-start.1 = ((f32[32,1,128]{2,1,0:T(1,128)}), f32[32,1,128]{2,1,0:T(1,128)S(1)}, u32[]{:S(2)}, u32[]{:S(2)}) async-start(f32[32,1,128]{2,1,0:T(1,128)} %get-tuple-element.15), calls=%async_computation.1 | async-start | bytes 32768 | tf_op jit(solution)/shard_map/all_to_all | solution.py:368
  61.6 6.3 %all-to-all-done.1.sums_ref = f32[32,1,128]{2,1,0:T(1,128)S(1)} async-done(((f32[32,1,128]{2,1,0:T(1,128)}), f32[32,1,128]{2,1,0:T(1,128)S(1)}, u32[]{:S(2)}, u32[]{:S(2)}) %all-to-all-start.1) | async-done | bytes 16416 | tf_op jit(solution)/shard_map/all_to_all | solution.py:368
  68.0 2.7 %shard_map.116 = (f32[80,256]{1,0:T(8,128)S(1)}, f32[32,1,128]{2,1,0:T(1,128)S(1)}, bf16[80,256]{1,0:T(8,128)(2,1)S(1)}) custom-call(s32[2]{0:T(128)S(1)} %pad_add_fusion.at_ref, bf16[16,208,128]{2,1,0:T(8,128)(2,1)S(1)} %all-to-all-done.block_ref, f32[32,1,128]{2,1,0:T(1,128)S(1)} %all-to-all-done.1.sums_ref, f32[3,1280]{1,0:T(4,128)S(1)} %copy-done.7, ...), custom_call_target="tpu_custom_call" | custom-call | tf_op jit(solution)/shard_map/pallas_call | solution.py:353
  70.7 10.8 %all_to_all.35.sums_ref = f32[32,1,128]{2,1,0:T(1,128)S(1)} all-to-all(f32[32,1,128]{2,1,0:T(1,128)S(1)} %get-tuple-element.19), channel_id=1, replica_groups=mesh['prow_0'=2,'prow_1'=8,'pcol_0'=4,'pcol_1'=4,'pcol_2'=2] {'pcol_0','..., dimensions={0} | all-to-all | bytes 32768 | tf_op jit(solution)/shard_map/all_to_all | solution.py:368
  82.7 5.1 %all-to-all-start.3 = ((bf16[16,80,256]{2,1,0:T(8,128)(2,1)}), bf16[16,80,256]{2,1,0:T(8,128)(2,1)S(1)}, u32[]{:S(2)}, u32[]{:S(2)}) async-start(bf16[16,80,256]{2,1,0:T(8,128)(2,1)} %shard_map.117), calls=%async_computation.3 | async-start | bytes 1310720 | tf_op jit(solution)/shard_map/all_to_all | solution.py:368
  87.8 2.2 collective-permute-start.4
  90.0 4.2 %collective-permute-done.4.right_ref = bf16[1,256,128]{2,1,0:T(8,128)(2,1)S(1)} collective-permute-done((bf16[1,256,128]{2,1,0:T(8,128)(2,1)S(1)}, bf16[1,256,128]{2,1,0:T(8,128)(2,1)S(1)}, u32[]{:S(2)}, u32[]{:S(2)}) %collective-permute-start.4) | collective-permute-done | bytes 65568 | tf_op jit(solution)/shard_map/ppermute | solution.py:393
  94.9 2.4 %collective-permute-start.5 = (bf16[2,256,128]{2,1,0:T(8,128)(2,1)}, bf16[2,256,128]{2,1,0:T(8,128)(2,1)S(1)}, u32[]{:S(2)}, u32[]{:S(2)}) collective-permute-start(bf16[2,256,128]{2,1,0:T(8,128)(2,1)} %shard_map.122.left_ref), channel_id=1, source_target_pairs={{0,16},{8,24},{16,0},{24,8},{1,17},{9,25},{17,1},{25,9},{2,18},{10... | collective-permute-start | bytes 393224 | tf_op jit(solution)/shard_map/ppermute | solution.py:393
  97.3 13.8 %collective-permute-done.5.right_ref = bf16[2,256,128]{2,1,0:T(8,128)(2,1)S(1)} collective-permute-done((bf16[2,256,128]{2,1,0:T(8,128)(2,1)}, bf16[2,256,128]{2,1,0:T(8,128)(2,1)S(1)}, u32[]{:S(2)}, u32[]{:S(2)}) %collective-permute-start.5) | collective-permute-done | bytes 131104 | tf_op jit(solution)/shard_map/ppermute | solution.py:393
  115.0 5.1 %collective-permute-done.6.right_ref = bf16[4,256,128]{2,1,0:T(8,128)(2,1)S(1)} collective-permute-done((bf16[4,256,128]{2,1,0:T(8,128)(2,1)}, bf16[4,256,128]{2,1,0:T(8,128)(2,1)S(1)}, u32[]{:S(2)}, u32[]{:S(2)}) %collective-permute-start.6) | collective-permute-done | bytes 262176 | tf_op jit(solution)/shard_map/ppermute | solution.py:393
  121.9 2.8 %collective-permute-start.7 = (bf16[8,256,128]{2,1,0:T(8,128)(2,1)}, bf16[8,256,128]{2,1,0:T(8,128)(2,1)S(1)}, u32[]{:S(2)}, u32[]{:S(2)}) collective-permute-start(bf16[8,256,128]{2,1,0:T(8,128)(2,1)} %shard_map.124.left_ref), channel_id=1, source_target_pairs={{0,4},{2,6},{4,0},{6,2},{1,5},{3,7},{5,1},{7,3},{8,12},{10,14},{12... | collective-permute-start | bytes 1572872 | tf_op jit(solution)/shard_map/ppermute | solution.py:393
  127.6 6.8 %collective-permute-start.2 = (f32[80,64]{1,0:T(8,128)S(1)}, f32[80,64]{1,0:T(8,128)S(1)}, u32[]{:S(2)}, u32[]{:S(2)}) collective-permute-start(f32[80,64]{1,0:T(8,128)S(1)} %get-tuple-element.21), channel_id=1, source_target_pairs={{0,1},{1,0},{2,3},{3,2},{4,5},{5,4},{6,7},{7,6},{8,9},{9,8},{10,11... | collective-permute-start | bytes 61448 | tf_op jit(solution)/shard_map/ppermute | solution.py:374
  134.4 2.9 %collective-permute-start.3 = (f32[80,64]{1,0:T(8,128)S(1)}, f32[80,64]{1,0:T(8,128)S(1)}, u32[]{:S(2)}, u32[]{:S(2)}) collective-permute-start(f32[80,64]{1,0:T(8,128)S(1)} %get-tuple-element.22), channel_id=1, source_target_pairs={{1,2},{2,1},{3,4},{4,3},{5,6},{6,5},{7,8},{8,7},{9,10},{10,9},{11,... | collective-permute-start | bytes 61448 | tf_op jit(solution)/shard_map/ppermute | solution.py:373
  137.3 2.5 %collective-permute-done.3.outer_ref = f32[80,64]{1,0:T(8,128)S(1)} collective-permute-done((f32[80,64]{1,0:T(8,128)S(1)}, f32[80,64]{1,0:T(8,128)S(1)}, u32[]{:S(2)}, u32[]{:S(2)}) %collective-permute-start.3) | collective-permute-done | bytes 20512 | tf_op jit(solution)/shard_map/ppermute | solution.py:373
  140.5 12.0 %all_to_all.36.sums_ref = f32[32,1,128]{2,1,0:T(1,128)S(1)} all-to-all(f32[32,1,128]{2,1,0:T(1,128)S(1)} %get-tuple-element.25), channel_id=1, replica_groups=mesh['prow_0'=2,'prow_1'=8,'pcol_0'=4,'pcol_1'=4,'pcol_2'=2] {'pcol_0','..., dimensions={0} | all-to-all | bytes 32768 | tf_op jit(solution)/shard_map/all_to_all | solution.py:368
  153.6 18.2 %all-to-all-start.5 = ((bf16[16,80,256]{2,1,0:T(8,128)(2,1)}), bf16[16,80,256]{2,1,0:T(8,128)(2,1)S(1)}, u32[]{:S(2)}, u32[]{:S(2)}) async-start(bf16[16,80,256]{2,1,0:T(8,128)(2,1)} %shard_map.120), calls=%async_computation.5 | async-start | bytes 1310720 | tf_op jit(solution)/shard_map/all_to_all | solution.py:368
  172.9 2.8 %collective-permute-start.8 = (bf16[16,256,128]{2,1,0:T(8,128)(2,1)}, bf16[16,256,128]{2,1,0:T(8,128)(2,1)S(1)}, u32[]{:S(2)}, u32[]{:S(2)}) collective-permute-start(bf16[16,256,128]{2,1,0:T(8,128)(2,1)} %shard_map.125.near_hbm), channel_id=1, source_target_pairs={{0,1},{1,0},{2,3},{3,2},{4,5},{5,4},{6,7},{7,6},{8,9},{9,8},{10,11... | collective-permute-start | bytes 3145736 | tf_op jit(solution)/shard_map/ppermute | solution.py:393
  178.2 14.6 %all-to-all-done.5 = bf16[16,80,256]{2,1,0:T(8,128)(2,1)S(1)} async-done(((bf16[16,80,256]{2,1,0:T(8,128)(2,1)}), bf16[16,80,256]{2,1,0:T(8,128)(2,1)S(1)}, u32[]{:S(2)}, u32[]{:S(2)}) %all-to-all-start.5) | async-done | bytes 655392 | tf_op jit(solution)/shard_map/all_to_all | solution.py:368
  194.8 6.7 %shard_map.126 = (bf16[16,16,1280]{2,1,0:T(8,128)(2,1)S(1)}, bf16[256,128]{1,0:T(8,128)(2,1)}) custom-call(s32[2]{0:T(128)S(1)} %pad_add_fusion.at_ref, bf16[1280,256]{1,0:T(8,128)(2,1)S(1)} %bitcast.11, bf16[192,1280]{1,0:T(8,128)(2,1)S(1)} %copy-done.6, bf16[1280,128]{1,0:T(8,128)(2,1)S(1)} %copy-done.3, ...), custom_call_target="tpu_custom_call" | custom-call | tf_op jit(solution)/shard_map/pallas_call | solution.py:353
  201.5 26.8 %all_to_all.37.parts_ref = bf16[16,16,1280]{2,1,0:T(8,128)(2,1)S(1)} all-to-all(bf16[16,16,1280]{2,1,0:T(8,128)(2,1)S(1)} %get-tuple-element.26), channel_id=1, replica_groups=mesh['prow_0'=2,'prow_1'=8,'pcol_0'=4,'pcol_1'=4,'pcol_2'=2] {'prow_0','..., dimensions={0} | all-to-all | bytes 1310720 | tf_op jit(solution)/shard_map/all_to_all | solution.py:368
  (46 shorter events, 23.6 us)
Async XLA Ops:
  0.6 60.0 %copy-start.11 = (f32[1280]{0:T(1024)S(1)}, f32[1280]{0:T(1024)}, u32[]{:S(2)}) copy-start(f32[1280]{0:T(1024)} %param.13) | copy-start | bytes 15364
  0.6 60.1 %copy-start.8 = (f32[3,1280]{1,0:T(4,128)S(1)}, f32[3,1280]{1,0:T(4,128)}, u32[]{:S(2)}) copy-start(f32[3,1280]{1,0:T(4,128)} %shift_ref.3) | copy-start | bytes 46084
  0.7 60.1 %copy-start.7 = (f32[3,1280]{1,0:T(4,128)S(1)}, f32[3,1280]{1,0:T(4,128)}, u32[]{:S(2)}) copy-start(f32[3,1280]{1,0:T(4,128)} %scale_ref.3) | copy-start | bytes 46084
  0.7 60.1 %copy-start.10 = (f32[2,1280]{1,0:T(2,128)S(1)}, f32[2,1280]{1,0:T(2,128)}, u32[]{:S(2)}) copy-start(f32[2,1280]{1,0:T(2,128)} %bias_ref.1) | copy-start | bytes 30724
  0.7 67.3 %copy-start.1 = (bf16[3,3,80,1280]{3,2,1,0:T(8,128)(2,1)S(1)}, bf16[3,3,80,1280]{3,2,1,0:T(8,128)(2,1)}, u32[]{:S(2)}) copy-start(bf16[3,3,80,1280]{3,2,1,0:T(8,128)(2,1)} %param.15) | copy-start | bytes 5529604
  2.8 40.8 %all-to-all-start = ((bf16[16,208,128]{2,1,0:T(8,128)(2,1)}), bf16[16,208,128]{2,1,0:T(8,128)(2,1)S(1)}, u32[]{:S(2)}, u32[]{:S(2)}) async-start(bf16[16,208,128]{2,1,0:T(8,128)(2,1)} %shard_map.113), calls=%async_computation | async-start | bytes 1703936 | tf_op jit(solution)/shard_map/all_to_all | solution.py:368
  45.6 22.3 %collective-permute-start = (bf16[64,1280]{1,0:T(8,128)(2,1)S(1)}, bf16[64,1280]{1,0:T(8,128)(2,1)S(1)}, u32[]{:S(2)}, u32[]{:S(2)}) collective-permute-start(bf16[64,1280]{1,0:T(8,128)(2,1)S(1)} %get-tuple-element.16), channel_id=1, source_target_pairs={{0,1},{1,0},{2,3},{3,2},{4,5},{5,4},{6,7},{7,6},{8,9},{9,8},{10,11... | collective-permute-start | bytes 491528 | tf_op jit(solution)/shard_map/ppermute | solution.py:374
  50.8 17.2 %collective-permute-start.1 = (bf16[64,1280]{1,0:T(8,128)(2,1)S(1)}, bf16[64,1280]{1,0:T(8,128)(2,1)S(1)}, u32[]{:S(2)}, u32[]{:S(2)}) collective-permute-start(bf16[64,1280]{1,0:T(8,128)(2,1)S(1)} %get-tuple-element.17), channel_id=1, source_target_pairs={{1,2},{2,1},{3,4},{4,3},{5,6},{6,5},{7,8},{8,7},{9,10},{10,9},{11,... | collective-permute-start | bytes 491528 | tf_op jit(solution)/shard_map/ppermute | solution.py:373
  53.8 14.1 %all-to-all-start.1 = ((f32[32,1,128]{2,1,0:T(1,128)}), f32[32,1,128]{2,1,0:T(1,128)S(1)}, u32[]{:S(2)}, u32[]{:S(2)}) async-start(f32[32,1,128]{2,1,0:T(1,128)} %get-tuple-element.15), calls=%async_computation.1 | async-start | bytes 32768 | tf_op jit(solution)/shard_map/all_to_all | solution.py:368
  70.7 17.2 %copy-start.9 = (bf16[64,4,1,128]{3,1,2,0:T(4,128)(2,1)S(1)}, bf16[64,4,1,128]{3,1,2,0:T(4,128)(2,1)}, u32[]{:S(2)}) copy-start(bf16[64,4,1,128]{3,1,2,0:T(4,128)(2,1)} %param.19) | copy-start | bytes 196612
  82.7 41.9 %all-to-all-start.3 = ((bf16[16,80,256]{2,1,0:T(8,128)(2,1)}), bf16[16,80,256]{2,1,0:T(8,128)(2,1)S(1)}, u32[]{:S(2)}, u32[]{:S(2)}) async-start(bf16[16,80,256]{2,1,0:T(8,128)(2,1)} %shard_map.117), calls=%async_computation.3 | async-start | bytes 1310720 | tf_op jit(solution)/shard_map/all_to_all | solution.py:368
  87.8 6.4 %collective-permute-start.4 = (bf16[1,256,128]{2,1,0:T(8,128)(2,1)S(1)}, bf16[1,256,128]{2,1,0:T(8,128)(2,1)S(1)}, u32[]{:S(2)}, u32[]{:S(2)}) collective-permute-start(bf16[1,256,128]{2,1,0:T(8,128)(2,1)S(1)} %bitcast.14), channel_id=1, source_target_pairs={{0,8},{8,0},{16,24},{24,16},{1,9},{9,1},{17,25},{25,17},{2,10},{10... | collective-permute-start | bytes 196616 | tf_op jit(solution)/shard_map/ppermute | solution.py:393
  94.9 16.2 %collective-permute-start.5 = (bf16[2,256,128]{2,1,0:T(8,128)(2,1)}, bf16[2,256,128]{2,1,0:T(8,128)(2,1)S(1)}, u32[]{:S(2)}, u32[]{:S(2)}) collective-permute-start(bf16[2,256,128]{2,1,0:T(8,128)(2,1)} %shard_map.122.left_ref), channel_id=1, source_target_pairs={{0,16},{8,24},{16,0},{24,8},{1,17},{9,25},{17,1},{25,9},{2,18},{10... | collective-permute-start | bytes 393224 | tf_op jit(solution)/shard_map/ppermute | solution.py:393
  112.8 7.3 %collective-permute-start.6 = (bf16[4,256,128]{2,1,0:T(8,128)(2,1)}, bf16[4,256,128]{2,1,0:T(8,128)(2,1)S(1)}, u32[]{:S(2)}, u32[]{:S(2)}) collective-permute-start(bf16[4,256,128]{2,1,0:T(8,128)(2,1)} %shard_map.123.left_ref), channel_id=1, source_target_pairs={{0,2},{2,0},{4,6},{6,4},{1,3},{3,1},{5,7},{7,5},{8,10},{10,8},{12,... | collective-permute-start | bytes 786440 | tf_op jit(solution)/shard_map/ppermute | solution.py:393
  120.1 1.0 copy-start.4
  121.9 50.0 %collective-permute-start.7 = (bf16[8,256,128]{2,1,0:T(8,128)(2,1)}, bf16[8,256,128]{2,1,0:T(8,128)(2,1)S(1)}, u32[]{:S(2)}, u32[]{:S(2)}) collective-permute-start(bf16[8,256,128]{2,1,0:T(8,128)(2,1)} %shard_map.124.left_ref), channel_id=1, source_target_pairs={{0,4},{2,6},{4,0},{6,2},{1,5},{3,7},{5,1},{7,3},{8,12},{10,14},{12... | collective-permute-start | bytes 1572872 | tf_op jit(solution)/shard_map/ppermute | solution.py:393
  124.7 1.5 copy-start.2
  126.2 45.7 %copy-start = (bf16[8,256,128]{2,1,0:T(8,128)(2,1)S(1)}, bf16[8,256,128]{2,1,0:T(8,128)(2,1)}, u32[]{:S(2)}) copy-start(bf16[8,256,128]{2,1,0:T(8,128)(2,1)} %shard_map.124.left_ref) | copy-start | bytes 1572868
  127.6 9.7 %collective-permute-start.2 = (f32[80,64]{1,0:T(8,128)S(1)}, f32[80,64]{1,0:T(8,128)S(1)}, u32[]{:S(2)}, u32[]{:S(2)}) collective-permute-start(f32[80,64]{1,0:T(8,128)S(1)} %get-tuple-element.21), channel_id=1, source_target_pairs={{0,1},{1,0},{2,3},{3,2},{4,5},{5,4},{6,7},{7,6},{8,9},{9,8},{10,11... | collective-permute-start | bytes 61448 | tf_op jit(solution)/shard_map/ppermute | solution.py:374
  134.4 5.3 %collective-permute-start.3 = (f32[80,64]{1,0:T(8,128)S(1)}, f32[80,64]{1,0:T(8,128)S(1)}, u32[]{:S(2)}, u32[]{:S(2)}) collective-permute-start(f32[80,64]{1,0:T(8,128)S(1)} %get-tuple-element.22), channel_id=1, source_target_pairs={{1,2},{2,1},{3,4},{4,3},{5,6},{6,5},{7,8},{8,7},{9,10},{10,9},{11,... | collective-permute-start | bytes 61448 | tf_op jit(solution)/shard_map/ppermute | solution.py:373
  153.6 39.2 %all-to-all-start.5 = ((bf16[16,80,256]{2,1,0:T(8,128)(2,1)}), bf16[16,80,256]{2,1,0:T(8,128)(2,1)S(1)}, u32[]{:S(2)}, u32[]{:S(2)}) async-start(bf16[16,80,256]{2,1,0:T(8,128)(2,1)} %shard_map.120), calls=%async_computation.5 | async-start | bytes 1310720 | tf_op jit(solution)/shard_map/all_to_all | solution.py:368
  172.9 5.3 %collective-permute-start.8 = (bf16[16,256,128]{2,1,0:T(8,128)(2,1)}, bf16[16,256,128]{2,1,0:T(8,128)(2,1)S(1)}, u32[]{:S(2)}, u32[]{:S(2)}) collective-permute-start(bf16[16,256,128]{2,1,0:T(8,128)(2,1)} %shard_map.125.near_hbm), channel_id=1, source_target_pairs={{0,1},{1,0},{2,3},{3,2},{4,5},{5,4},{6,7},{7,6},{8,9},{9,8},{10,11... | collective-permute-start | bytes 3145736 | tf_op jit(solution)/shard_map/ppermute | solution.py:393
  192.8 1.0 copy-start.3
  193.8 1.0 copy-start.6
  (1 other events, 0.9 us)

commit v7 on v6

--- a/solution.py
+++ b/solution.py
@@ -117,8 +117,8 @@
     copy.wait()
 
 
-def columns_kernel(at_ref, scale_ref, shift_ref, bias_ref, time_ref, out_ref):
-    pick = iota((OC, C), 1) == iota((OC, C), 0) + at_ref[0] * OC
+def columns_kernel(scale_ref, shift_ref, bias_ref, time_ref, out_ref):
+    pick = iota((OC, C), 1) == iota((OC, C), 0) + lax.axis_index(PROW) * OC
     lane = iota((OC, 128), 1)
     total = jnp.zeros((OC, 128), F32)
     rows = [
@@ -135,8 +135,8 @@
     out_ref[...] = total
 
 
-def by_parity(at_ref, one, other):
-    even = at_ref[1] % 2 == 0
+def by_parity(one, other):
+    even = lax.axis_index(PCOL) % 2 == 0
     return jnp.where(even, one, other), jnp.where(even, other, one)
 
 
@@ -144,10 +144,10 @@
     return block_ref[:, NP * j : NP * (j + 1), :].reshape(CELLS, 128)
 
 
-def stats_cells_kernel(at_ref, block_ref, out_ref, inner_ref, outer_ref):
+def stats_cells_kernel(block_ref, out_ref, inner_ref, outer_ref):
     firsts, seconds = [], []
     row = iota((2 * LR, CELLS), 0)
-    inner, outer = by_parity(at_ref, PC - 1, 0)
+    inner, outer = by_parity(PC - 1, 0)
     wanted = jnp.where(row < LR, row * PC + inner, (row - LR) * PC + outer)
     pick = one_hot(iota((2 * LR, CELLS), 1) == wanted, BF16)
     for j in range(C // 128):
@@ -195,7 +195,6 @@
 
 
 def conv_cells_kernel(
-    at_ref,
     block_ref,
     sums_ref,
     scale_ref,
@@ -216,15 +215,15 @@
     offset = shift_ref[0:1, :] - spread[0:1, :] * gain
     chunks = [strip_chunk(block_ref, j) for j in range(C // 128)]
     cells = nn(strip_order(), jnp.concatenate(chunks, axis=1))
-    pick = one_hot(iota((OC, C), 1) == iota((OC, C), 0) + at_ref[0] * OC, BF16)
+    pick = one_hot(iota((OC, C), 1) == iota((OC, C), 0) + lax.axis_index(PROW) * OC, BF16)
     own_ref[...] = nt(pick, cells.astype(BF16)).astype(BF16)
     _, mid, _ = tap_columns(nt(w_ref[...], silu(cells * gain + offset).astype(BF16)))
-    right, left = by_parity(at_ref, inner_ref[...].astype(F32), outer_ref[...].astype(F32))
+    right, left = by_parity(inner_ref[...].astype(F32), outer_ref[...].astype(F32))
     sides = jnp.concatenate([left, right], axis=0)
     sides = silu(sides * gain + offset)
     row = iota((2 * LR, 1), 0)
-    first = jnp.where(at_ref[1] > 0, 0, LR)
-    last = jnp.where(at_ref[1] < NS - 1, 2 * LR, LR)
+    first = jnp.where(lax.axis_index(PCOL) > 0, 0, LR)
+    last = jnp.where(lax.axis_index(PCOL) < NS - 1, 2 * LR, LR)
     sides = jnp.where((row >= first) & (row < last), sides, 0.0).astype(BF16)
     products = nt(w_ref[...], sides)
     left = tap_sums(products, 0)[:, :LR]
@@ -234,9 +233,9 @@
     own_sums(total, out_sums_ref)
 
 
-def conv_channels_kernel(at_ref, x_ref, w_ref, mid_ref, inner_ref, outer_ref):
+def conv_channels_kernel(x_ref, w_ref, mid_ref, inner_ref, outer_ref):
     before, mid, after = tap_columns(nn(w_ref[...], x_ref[...]))
-    inner, outer = by_parity(at_ref, before[:, CELLS - LR :], after[:, :LR])
+    inner, outer = by_parity(before[:, CELLS - LR :], after[:, :LR])
     inner_ref[...] = inner
     outer_ref[...] = outer
     mid_ref[...] = mid
@@ -256,8 +255,8 @@
     sums_ref[...] = jnp.broadcast_to(row[None], sums_ref.shape)
 
 
-def finish_kernel(at_ref, mid_ref, inner_ref, outer_ref, cols_ref, own_ref, total_ref, sums_ref):
-    right, left = by_parity(at_ref, inner_ref[...], outer_ref[...])
+def finish_kernel(mid_ref, inner_ref, outer_ref, cols_ref, own_ref, total_ref, sums_ref):
+    right, left = by_parity(inner_ref[...], outer_ref[...])
     total = with_sides(mid_ref[...], left, right)
     total = (own_ref[...].astype(F32) + total + cols_ref[:, 3:4]).astype(BF16)
     total_ref[...] = total
@@ -289,7 +288,6 @@
 
 
 def attention_kernel(
-    at_ref,
     x_ref,
     w_ref,
     w_out_ref,
@@ -331,7 +329,7 @@
         highest = raised
     attended = nn(order, (weighted / denominator).astype(BF16)).astype(BF16)
     own = nt(order, own_ref[...]).astype(BF16)
-    pick = one_hot(iota((OC, C), 1) == iota((OC, C), 0) + at_ref[0] * OC, BF16)
+    pick = one_hot(iota((OC, C), 1) == iota((OC, C), 0) + lax.axis_index(PROW) * OC, BF16)
     part = nt(attended, w_out_ref[...]) + nn(own, pick)
     part_ref[...] = part.astype(BF16).reshape(part_ref.shape)
 
@@ -342,13 +340,12 @@
         out_ref[r] = total[PC * r : PC * (r + 1), :].astype(BF16)
 
 
-def call(kernel, outs, scalars=0, outer=0, mib=8, space=pltpu.VMEM, scratch=()):
+def call(kernel, outs, outer=0, mib=8, space=pltpu.VMEM, scratch=()):
     def run(*args):
         args = list(args)
         for k in range(len(args) - outer, len(args)):
             args[k] = pltpu.with_memory_space_constraint(args[k], pltpu.HBM)
-        specs = [pl.BlockSpec(memory_space=pltpu.SMEM)] * scalars
-        specs += [pl.BlockSpec(memory_space=pltpu.VMEM)] * (len(args) - scalars - outer)
+        specs = [pl.BlockSpec(memory_space=pltpu.VMEM)] * (len(args) - outer)
         specs += [pl.BlockSpec(memory_space=pltpu.HBM)] * outer
         return pl.pallas_call(
             kernel,
@@ -386,7 +383,6 @@
     w_out,
     stale_kv,
 ):
-    at = jnp.stack([lax.axis_index(PROW), lax.axis_index(PCOL)]).astype(jnp.int32)
     near = stale_kv.reshape(1, CELLS, 2 * HEAD)
     for step, (axis, bit) in enumerate(HOPS):
         count = lax.axis_size(axis)
@@ -400,8 +396,8 @@
     every = ((NP, OC, CELLS), BF16)
     tile = ((OC, CELLS), F32)
     edge = ((LR, C), BF16)
-    (cols,) = call(columns_kernel, [((OC, 128), F32)], scalars=1)(
-        at, norm_scale, norm_shift, conv_bias, time_shift.reshape(1, C)
+    (cols,) = call(columns_kernel, [((OC, 128), F32)])(
+        norm_scale, norm_shift, conv_bias, time_shift.reshape(1, C)
     )
 
     def gathered(which, total, sums):
@@ -420,7 +416,7 @@
         ],
     )(latent, w_out)
     block = to_every(block, PROW)
-    sums, inner, outer = call(stats_cells_kernel, [sums_out, edge, edge], scalars=1)(at, block)
+    sums, inner, outer = call(stats_cells_kernel, [sums_out, edge, edge])(block)
     sums = to_every(sums, PCOL)
     inner, outer = swapped(inner, outer)
     (w_part,) = call(
@@ -429,8 +425,7 @@
         space=pltpu.HBM,
         scratch=[pltpu.VMEM((C, 128), BF16), pltpu.SemaphoreType.DMA],
     )(block)
-    total, sums, own = call(conv_cells_kernel, [tile, sums_out, ((OC, CELLS), BF16)], scalars=1)(
-        at,
+    total, sums, own = call(conv_cells_kernel, [tile, sums_out, ((OC, CELLS), BF16)])(
         block,
         sums,
         norm_scale,
@@ -442,21 +437,20 @@
     )
     field = gathered(0, total, sums)
     mid, inner, outer = call(
-        conv_channels_kernel, [tile, ((OC, LR), F32), ((OC, LR), F32)], scalars=1
-    )(at, field, conv_two.reshape(9 * OC, C))
+        conv_channels_kernel, [tile, ((OC, LR), F32), ((OC, LR), F32)]
+    )(field, conv_two.reshape(9 * OC, C))
     inner, outer = swapped(inner, outer)
-    resnet, sums = call(finish_kernel, [((OC, CELLS), BF16), sums_out], scalars=1)(
-        at, mid, inner, outer, cols, own
+    resnet, sums = call(finish_kernel, [((OC, CELLS), BF16), sums_out])(
+        mid, inner, outer, cols, own
     )
     field = gathered(1, resnet, sums)
     parts, fresh = call(
         attention_kernel,
         [((NP, NP, C), BF16), ((CELLS, 2 * HEAD), BF16)],
-        scalars=1,
         outer=1,
         mib=16,
         scratch=[pltpu.VMEM((NS // 2, CELLS, 2 * HEAD), BF16), pltpu.SemaphoreType.DMA],
-    )(at, field, w_qkv, w_part, resnet, far, near)
+    )(field, w_qkv, w_part, resnet, far, near)
     (out,) = call(output_kernel, [((PC, PC, C), BF16)])(to_every(parts, PROW))
     return out, fresh.reshape(LR, PC, 1, 2 * HEAD)
 

time: 232 us -> 228 us (0.983)
  blocking collectives: 49.6 us -> 91 us
  waiting for transfers between devices: 72.6 us -> 49 us
  starting transfers between devices: 76.7 us -> 59.1 us
  Pallas kernels: 23.7 us -> 19.5 us
    all_to_all x3 -> x4, blocking collectives: 49.6 us -> 91 us  [to_every(): return lax.all_to_all(copies, axis, split_axis=0, concat_axis=0, tiled=True)]
    all_to_all x4 -> x3, waiting for transfers between devices: 45.5 us -> 21.5 us  [to_every(): return lax.all_to_all(copies, axis, split_axis=0, concat_axis=0, tiled=True)]
    all_to_all x4 -> x3, starting transfers between devices: 46.3 us -> 30 us  [to_every(): return lax.all_to_all(copies, axis, split_axis=0, concat_axis=0, tiled=True)]
    pallas_call x15, Pallas kernels: 23.7 us -> 19.5 us  [run(): pl.pallas_call(kernel, out_shape=[pltpu.HBM(*out) if space is pltpu.HBM e...]
  transfers between devices with their start and end apart: 13 -> 12, of which waited for: 8 -> 7; matrix products, arithmetic and copies ran while one was open for 0% -> 0% of each run, Pallas kernels for 4% -> 3%
where the time goes in v7:
time: 228 us; the launch traced here: 225 us
  blocking collectives  91 us (40%)
  starting transfers between devices  59.1 us (26%)
  waiting for transfers between devices  49 us (21%)
  Pallas kernels  19.5 us (9%)
  local copies, waits for them, and re-layouts  5.39 us (2%)
    all_to_all x4, blocking collectives, to_every(): return lax.all_to_all(copies, axis, split_axis=0, concat_axis=0, tiled=True)  91 us
    all_to_all x3, starting transfers between devices, to_every(): return lax.all_to_all(copies, axis, split_axis=0, concat_axis=0, tiled=True)  30 us
    ppermute x5, waiting for transfers between devices, shards(): far = lax.ppermute(near, axis, [(i, i ^ bit) for i in range(count)])  24.7 us
    all_to_all x3, waiting for transfers between devices, to_every(): return lax.all_to_all(copies, axis, split_axis=0, concat_axis=0, tiled=True)  21.5 us
    pallas_call x15, Pallas kernels, run(): pl.pallas_call(kernel, out_shape=[pltpu.HBM(*out) if space is pltpu.HBM e...  19.5 us
    ppermute x5, starting transfers between devices, shards(): far = lax.ppermute(near, axis, [(i, i ^ bit) for i in range(count)])  12.4 us
    ppermute x2, starting transfers between devices, swapped(): return (lax.ppermute(inner, PCOL[-1], [(0, 1), (1, 0)]), outer)  10.8 us
    ppermute x2, starting transfers between devices, swapped(): outer = lax.ppermute(outer, PCOL, pairs)  5.87 us
  transfers between devices with their start and end apart: 12, of which 7 were waited for; matrix products, arithmetic and copies ran while one was open for 0% of the time, Pallas kernels for 3%

profile of v7, /device:TPU:1, one launch (start us, length us, event | category | flops | bytes accessed | tf_op | source)
XLA Modules:
  0.0 225.0 jit_solution(12636090370914580577)
XLA Ops:
  1.9 41.6 %all_to_all.35.block_ref = bf16[16,208,128]{2,1,0:T(8,128)(2,1)S(1)} all-to-all(bf16[16,208,128]{2,1,0:T(8,128)(2,1)S(1)} %shard_map.113), channel_id=1, replica_groups=mesh['prow_0'=2,'prow_1'=8,'pcol_0'=4,'pcol_1'=4,'pcol_2'=2] {'prow_0','..., dimensions={0} | all-to-all | bytes 1703936 | tf_op jit(solution)/shard_map/all_to_all | solution.py:365
  44.9 3.9 %collective-permute-start = (bf16[64,1280]{1,0:T(8,128)(2,1)S(1)}, bf16[64,1280]{1,0:T(8,128)(2,1)S(1)}, u32[]{:S(2)}, u32[]{:S(2)}) collective-permute-start(bf16[64,1280]{1,0:T(8,128)(2,1)S(1)} %get-tuple-element.16), channel_id=1, source_target_pairs={{0,1},{1,0},{2,3},{3,2},{4,5},{5,4},{6,7},{7,6},{8,9},{9,8},{10,11... | collective-permute-start | bytes 491528 | tf_op jit(solution)/shard_map/ppermute | solution.py:371
  48.9 3.0 %collective-permute-start.1 = (bf16[64,1280]{1,0:T(8,128)(2,1)S(1)}, bf16[64,1280]{1,0:T(8,128)(2,1)S(1)}, u32[]{:S(2)}, u32[]{:S(2)}) collective-permute-start(bf16[64,1280]{1,0:T(8,128)(2,1)S(1)} %get-tuple-element.17), channel_id=1, source_target_pairs={{1,2},{2,1},{3,4},{4,3},{5,6},{6,5},{7,8},{8,7},{9,10},{10,9},{11,... | collective-permute-start | bytes 491528 | tf_op jit(solution)/shard_map/ppermute | solution.py:370
  51.9 6.8 %all-to-all-start.1 = ((f32[32,1,128]{2,1,0:T(1,128)}), f32[32,1,128]{2,1,0:T(1,128)S(1)}, u32[]{:S(2)}, u32[]{:S(2)}) async-start(f32[32,1,128]{2,1,0:T(1,128)} %get-tuple-element.15), calls=%async_computation.1 | async-start | bytes 32768 | tf_op jit(solution)/shard_map/all_to_all | solution.py:365
  59.1 6.9 %all-to-all-done.1.sums_ref = f32[32,1,128]{2,1,0:T(1,128)S(1)} async-done(((f32[32,1,128]{2,1,0:T(1,128)}), f32[32,1,128]{2,1,0:T(1,128)S(1)}, u32[]{:S(2)}, u32[]{:S(2)}) %all-to-all-start.1) | async-done | bytes 16416 | tf_op jit(solution)/shard_map/all_to_all | solution.py:365
  66.0 2.2 shard_map.116
  68.2 10.8 %all_to_all.36.sums_ref = f32[32,1,128]{2,1,0:T(1,128)S(1)} all-to-all(f32[32,1,128]{2,1,0:T(1,128)S(1)} %get-tuple-element.19), channel_id=1, replica_groups=mesh['prow_0'=2,'prow_1'=8,'pcol_0'=4,'pcol_1'=4,'pcol_2'=2] {'pcol_0','..., dimensions={0} | all-to-all | bytes 32768 | tf_op jit(solution)/shard_map/all_to_all | solution.py:365
  80.2 4.5 %all-to-all-start.3 = ((bf16[16,80,256]{2,1,0:T(8,128)(2,1)}), bf16[16,80,256]{2,1,0:T(8,128)(2,1)S(1)}, u32[]{:S(2)}, u32[]{:S(2)}) async-start(bf16[16,80,256]{2,1,0:T(8,128)(2,1)} %shard_map.117), calls=%async_computation.3 | async-start | bytes 1310720 | tf_op jit(solution)/shard_map/all_to_all | solution.py:365
  84.8 2.2 collective-permute-start.4
  87.0 4.2 %collective-permute-done.4.right_ref = bf16[1,256,128]{2,1,0:T(8,128)(2,1)S(1)} collective-permute-done((bf16[1,256,128]{2,1,0:T(8,128)(2,1)S(1)}, bf16[1,256,128]{2,1,0:T(8,128)(2,1)S(1)}, u32[]{:S(2)}, u32[]{:S(2)}) %collective-permute-start.4) | collective-permute-done | bytes 65568 | tf_op jit(solution)/shard_map/ppermute | solution.py:389
  91.8 2.4 %collective-permute-start.5 = (bf16[2,256,128]{2,1,0:T(8,128)(2,1)}, bf16[2,256,128]{2,1,0:T(8,128)(2,1)S(1)}, u32[]{:S(2)}, u32[]{:S(2)}) collective-permute-start(bf16[2,256,128]{2,1,0:T(8,128)(2,1)} %shard_map.122.left_ref), channel_id=1, source_target_pairs={{0,16},{8,24},{16,0},{24,8},{1,17},{9,25},{17,1},{25,9},{2,18},{10... | collective-permute-start | bytes 393224 | tf_op jit(solution)/shard_map/ppermute | solution.py:389
  94.3 13.8 %collective-permute-done.5.right_ref = bf16[2,256,128]{2,1,0:T(8,128)(2,1)S(1)} collective-permute-done((bf16[2,256,128]{2,1,0:T(8,128)(2,1)}, bf16[2,256,128]{2,1,0:T(8,128)(2,1)S(1)}, u32[]{:S(2)}, u32[]{:S(2)}) %collective-permute-start.5) | collective-permute-done | bytes 131104 | tf_op jit(solution)/shard_map/ppermute | solution.py:389
  109.7 2.2 collective-permute-start.6
  111.9 5.1 %collective-permute-done.6.right_ref = bf16[4,256,128]{2,1,0:T(8,128)(2,1)S(1)} collective-permute-done((bf16[4,256,128]{2,1,0:T(8,128)(2,1)}, bf16[4,256,128]{2,1,0:T(8,128)(2,1)S(1)}, u32[]{:S(2)}, u32[]{:S(2)}) %collective-permute-start.6) | collective-permute-done | bytes 262176 | tf_op jit(solution)/shard_map/ppermute | solution.py:389
  118.8 2.8 %collective-permute-start.7 = (bf16[8,256,128]{2,1,0:T(8,128)(2,1)}, bf16[8,256,128]{2,1,0:T(8,128)(2,1)S(1)}, u32[]{:S(2)}, u32[]{:S(2)}) collective-permute-start(bf16[8,256,128]{2,1,0:T(8,128)(2,1)} %shard_map.124.left_ref), channel_id=1, source_target_pairs={{0,4},{2,6},{4,0},{6,2},{1,5},{3,7},{5,1},{7,3},{8,12},{10,14},{12... | collective-permute-start | bytes 1572872 | tf_op jit(solution)/shard_map/ppermute | solution.py:389
  123.9 6.8 %collective-permute-start.2 = (f32[80,64]{1,0:T(8,128)S(1)}, f32[80,64]{1,0:T(8,128)S(1)}, u32[]{:S(2)}, u32[]{:S(2)}) collective-permute-start(f32[80,64]{1,0:T(8,128)S(1)} %get-tuple-element.21), channel_id=1, source_target_pairs={{0,1},{1,0},{2,3},{3,2},{4,5},{5,4},{6,7},{7,6},{8,9},{9,8},{10,11... | collective-permute-start | bytes 61448 | tf_op jit(solution)/shard_map/ppermute | solution.py:371
  130.8 2.9 %collective-permute-start.3 = (f32[80,64]{1,0:T(8,128)S(1)}, f32[80,64]{1,0:T(8,128)S(1)}, u32[]{:S(2)}, u32[]{:S(2)}) collective-permute-start(f32[80,64]{1,0:T(8,128)S(1)} %get-tuple-element.22), channel_id=1, source_target_pairs={{1,2},{2,1},{3,4},{4,3},{5,6},{6,5},{7,8},{8,7},{9,10},{10,9},{11,... | collective-permute-start | bytes 61448 | tf_op jit(solution)/shard_map/ppermute | solution.py:370
  133.7 2.7 %collective-permute-done.3.outer_ref = f32[80,64]{1,0:T(8,128)S(1)} collective-permute-done((f32[80,64]{1,0:T(8,128)S(1)}, f32[80,64]{1,0:T(8,128)S(1)}, u32[]{:S(2)}, u32[]{:S(2)}) %collective-permute-start.3) | collective-permute-done | bytes 20512 | tf_op jit(solution)/shard_map/ppermute | solution.py:370
  136.6 11.7 %all_to_all.37.sums_ref = f32[32,1,128]{2,1,0:T(1,128)S(1)} all-to-all(f32[32,1,128]{2,1,0:T(1,128)S(1)} %get-tuple-element.25), channel_id=1, replica_groups=mesh['prow_0'=2,'prow_1'=8,'pcol_0'=4,'pcol_1'=4,'pcol_2'=2] {'pcol_0','..., dimensions={0} | all-to-all | bytes 32768 | tf_op jit(solution)/shard_map/all_to_all | solution.py:365
  149.5 18.7 %all-to-all-start.5 = ((bf16[16,80,256]{2,1,0:T(8,128)(2,1)}), bf16[16,80,256]{2,1,0:T(8,128)(2,1)S(1)}, u32[]{:S(2)}, u32[]{:S(2)}) async-start(bf16[16,80,256]{2,1,0:T(8,128)(2,1)} %shard_map.120), calls=%async_computation.5 | async-start | bytes 1310720 | tf_op jit(solution)/shard_map/all_to_all | solution.py:365
  169.3 2.8 %collective-permute-start.8 = (bf16[16,256,128]{2,1,0:T(8,128)(2,1)}, bf16[16,256,128]{2,1,0:T(8,128)(2,1)S(1)}, u32[]{:S(2)}, u32[]{:S(2)}) collective-permute-start(bf16[16,256,128]{2,1,0:T(8,128)(2,1)} %shard_map.125.near_hbm), channel_id=1, source_target_pairs={{0,1},{1,0},{2,3},{3,2},{4,5},{5,4},{6,7},{7,6},{8,9},{9,8},{10,11... | collective-permute-start | bytes 3145736 | tf_op jit(solution)/shard_map/ppermute | solution.py:389
  174.6 14.6 %all-to-all-done.5 = bf16[16,80,256]{2,1,0:T(8,128)(2,1)S(1)} async-done(((bf16[16,80,256]{2,1,0:T(8,128)(2,1)}), bf16[16,80,256]{2,1,0:T(8,128)(2,1)S(1)}, u32[]{:S(2)}, u32[]{:S(2)}) %all-to-all-start.5) | async-done | bytes 655392 | tf_op jit(solution)/shard_map/all_to_all | solution.py:365
  191.2 6.1 %shard_map.126 = (bf16[16,16,1280]{2,1,0:T(8,128)(2,1)S(1)}, bf16[256,128]{1,0:T(8,128)(2,1)}) custom-call(bf16[1280,256]{1,0:T(8,128)(2,1)S(1)} %bitcast.8, bf16[192,1280]{1,0:T(8,128)(2,1)S(1)} %copy-done.6, bf16[1280,128]{1,0:T(8,128)(2,1)S(1)} %copy-done.3, bf16[80,256]{1,0:T(8,128)(2,1)S(1)} %get-tuple-element.24.total_ref.own_ref, ...), custom_call_target="tpu_custom_call" | custom-call | tf_op jit(solution)/shard_map/pallas_call | solution.py:350
  197.4 26.9 %all_to_all.38.parts_ref = bf16[16,16,1280]{2,1,0:T(8,128)(2,1)S(1)} all-to-all(bf16[16,16,1280]{2,1,0:T(8,128)(2,1)S(1)} %get-tuple-element.26), channel_id=1, replica_groups=mesh['prow_0'=2,'prow_1'=8,'pcol_0'=4,'pcol_1'=4,'pcol_2'=2] {'prow_0','..., dimensions={0} | all-to-all | bytes 1310720 | tf_op jit(solution)/shard_map/all_to_all | solution.py:365
  (44 shorter events, 18.2 us)
Async XLA Ops:
  0.6 58.1 %copy-start.11 = (f32[1280]{0:T(1024)S(1)}, f32[1280]{0:T(1024)}, u32[]{:S(2)}) copy-start(f32[1280]{0:T(1024)} %param.13) | copy-start | bytes 15364
  0.6 58.1 %copy-start.8 = (f32[3,1280]{1,0:T(4,128)S(1)}, f32[3,1280]{1,0:T(4,128)}, u32[]{:S(2)}) copy-start(f32[3,1280]{1,0:T(4,128)} %shift_ref.3) | copy-start | bytes 46084
  0.7 58.1 %copy-start.7 = (f32[3,1280]{1,0:T(4,128)S(1)}, f32[3,1280]{1,0:T(4,128)}, u32[]{:S(2)}) copy-start(f32[3,1280]{1,0:T(4,128)} %scale_ref.3) | copy-start | bytes 46084
  0.7 58.1 %copy-start.10 = (f32[2,1280]{1,0:T(2,128)S(1)}, f32[2,1280]{1,0:T(2,128)}, u32[]{:S(2)}) copy-start(f32[2,1280]{1,0:T(2,128)} %bias_ref.1) | copy-start | bytes 30724
  0.7 65.3 %copy-start.2 = (bf16[3,3,80,1280]{3,2,1,0:T(8,128)(2,1)S(1)}, bf16[3,3,80,1280]{3,2,1,0:T(8,128)(2,1)}, u32[]{:S(2)}) copy-start(bf16[3,3,80,1280]{3,2,1,0:T(8,128)(2,1)} %param.15) | copy-start | bytes 5529604
  44.9 21.0 %collective-permute-start = (bf16[64,1280]{1,0:T(8,128)(2,1)S(1)}, bf16[64,1280]{1,0:T(8,128)(2,1)S(1)}, u32[]{:S(2)}, u32[]{:S(2)}) collective-permute-start(bf16[64,1280]{1,0:T(8,128)(2,1)S(1)} %get-tuple-element.16), channel_id=1, source_target_pairs={{0,1},{1,0},{2,3},{3,2},{4,5},{5,4},{6,7},{7,6},{8,9},{9,8},{10,11... | collective-permute-start | bytes 491528 | tf_op jit(solution)/shard_map/ppermute | solution.py:371
  48.9 17.1 %collective-permute-start.1 = (bf16[64,1280]{1,0:T(8,128)(2,1)S(1)}, bf16[64,1280]{1,0:T(8,128)(2,1)S(1)}, u32[]{:S(2)}, u32[]{:S(2)}) collective-permute-start(bf16[64,1280]{1,0:T(8,128)(2,1)S(1)} %get-tuple-element.17), channel_id=1, source_target_pairs={{1,2},{2,1},{3,4},{4,3},{5,6},{6,5},{7,8},{8,7},{9,10},{10,9},{11,... | collective-permute-start | bytes 491528 | tf_op jit(solution)/shard_map/ppermute | solution.py:370
  51.9 14.1 %all-to-all-start.1 = ((f32[32,1,128]{2,1,0:T(1,128)}), f32[32,1,128]{2,1,0:T(1,128)S(1)}, u32[]{:S(2)}, u32[]{:S(2)}) async-start(f32[32,1,128]{2,1,0:T(1,128)} %get-tuple-element.15), calls=%async_computation.1 | async-start | bytes 32768 | tf_op jit(solution)/shard_map/all_to_all | solution.py:365
  68.2 16.6 %copy-start.9 = (bf16[64,4,1,128]{3,1,2,0:T(4,128)(2,1)S(1)}, bf16[64,4,1,128]{3,1,2,0:T(4,128)(2,1)}, u32[]{:S(2)}) copy-start(bf16[64,4,1,128]{3,1,2,0:T(4,128)(2,1)} %param.19) | copy-start | bytes 196612
  80.2 41.4 %all-to-all-start.3 = ((bf16[16,80,256]{2,1,0:T(8,128)(2,1)}), bf16[16,80,256]{2,1,0:T(8,128)(2,1)S(1)}, u32[]{:S(2)}, u32[]{:S(2)}) async-start(bf16[16,80,256]{2,1,0:T(8,128)(2,1)} %shard_map.117), calls=%async_computation.3 | async-start | bytes 1310720 | tf_op jit(solution)/shard_map/all_to_all | solution.py:365
  84.8 6.4 %collective-permute-start.4 = (bf16[1,256,128]{2,1,0:T(8,128)(2,1)S(1)}, bf16[1,256,128]{2,1,0:T(8,128)(2,1)S(1)}, u32[]{:S(2)}, u32[]{:S(2)}) collective-permute-start(bf16[1,256,128]{2,1,0:T(8,128)(2,1)S(1)} %bitcast.12), channel_id=1, source_target_pairs={{0,8},{8,0},{16,24},{24,16},{1,9},{9,1},{17,25},{25,17},{2,10},{10... | collective-permute-start | bytes 196616 | tf_op jit(solution)/shard_map/ppermute | solution.py:389
  91.8 16.2 %collective-permute-start.5 = (bf16[2,256,128]{2,1,0:T(8,128)(2,1)}, bf16[2,256,128]{2,1,0:T(8,128)(2,1)S(1)}, u32[]{:S(2)}, u32[]{:S(2)}) collective-permute-start(bf16[2,256,128]{2,1,0:T(8,128)(2,1)} %shard_map.122.left_ref), channel_id=1, source_target_pairs={{0,16},{8,24},{16,0},{24,8},{1,17},{9,25},{17,1},{25,9},{2,18},{10... | collective-permute-start | bytes 393224 | tf_op jit(solution)/shard_map/ppermute | solution.py:389
  108.1 0.9 copy-start.5
  109.7 7.3 %collective-permute-start.6 = (bf16[4,256,128]{2,1,0:T(8,128)(2,1)}, bf16[4,256,128]{2,1,0:T(8,128)(2,1)S(1)}, u32[]{:S(2)}, u32[]{:S(2)}) collective-permute-start(bf16[4,256,128]{2,1,0:T(8,128)(2,1)} %shard_map.123.left_ref), channel_id=1, source_target_pairs={{0,2},{2,0},{4,6},{6,4},{1,3},{3,1},{5,7},{7,5},{8,10},{10,8},{12,... | collective-permute-start | bytes 786440 | tf_op jit(solution)/shard_map/ppermute | solution.py:389
  117.0 1.0 copy-start.4
  118.8 49.4 %collective-permute-start.7 = (bf16[8,256,128]{2,1,0:T(8,128)(2,1)}, bf16[8,256,128]{2,1,0:T(8,128)(2,1)S(1)}, u32[]{:S(2)}, u32[]{:S(2)}) collective-permute-start(bf16[8,256,128]{2,1,0:T(8,128)(2,1)} %shard_map.124.left_ref), channel_id=1, source_target_pairs={{0,4},{2,6},{4,0},{6,2},{1,5},{3,7},{5,1},{7,3},{8,12},{10,14},{12... | collective-permute-start | bytes 1572872 | tf_op jit(solution)/shard_map/ppermute | solution.py:389
  121.6 1.5 copy-start.1
  123.1 45.2 %copy-start = (bf16[8,256,128]{2,1,0:T(8,128)(2,1)S(1)}, bf16[8,256,128]{2,1,0:T(8,128)(2,1)}, u32[]{:S(2)}) copy-start(bf16[8,256,128]{2,1,0:T(8,128)(2,1)} %shard_map.124.left_ref) | copy-start | bytes 1572868
  123.9 9.7 %collective-permute-start.2 = (f32[80,64]{1,0:T(8,128)S(1)}, f32[80,64]{1,0:T(8,128)S(1)}, u32[]{:S(2)}, u32[]{:S(2)}) collective-permute-start(f32[80,64]{1,0:T(8,128)S(1)} %get-tuple-element.21), channel_id=1, source_target_pairs={{0,1},{1,0},{2,3},{3,2},{4,5},{5,4},{6,7},{7,6},{8,9},{9,8},{10,11... | collective-permute-start | bytes 61448 | tf_op jit(solution)/shard_map/ppermute | solution.py:371
  130.8 5.6 %collective-permute-start.3 = (f32[80,64]{1,0:T(8,128)S(1)}, f32[80,64]{1,0:T(8,128)S(1)}, u32[]{:S(2)}, u32[]{:S(2)}) collective-permute-start(f32[80,64]{1,0:T(8,128)S(1)} %get-tuple-element.22), channel_id=1, source_target_pairs={{1,2},{2,1},{3,4},{4,3},{5,6},{6,5},{7,8},{8,7},{9,10},{10,9},{11,... | collective-permute-start | bytes 61448 | tf_op jit(solution)/shard_map/ppermute | solution.py:370
  149.5 39.7 %all-to-all-start.5 = ((bf16[16,80,256]{2,1,0:T(8,128)(2,1)}), bf16[16,80,256]{2,1,0:T(8,128)(2,1)S(1)}, u32[]{:S(2)}, u32[]{:S(2)}) async-start(bf16[16,80,256]{2,1,0:T(8,128)(2,1)} %shard_map.120), calls=%async_computation.5 | async-start | bytes 1310720 | tf_op jit(solution)/shard_map/all_to_all | solution.py:365
  169.3 5.3 %collective-permute-start.8 = (bf16[16,256,128]{2,1,0:T(8,128)(2,1)}, bf16[16,256,128]{2,1,0:T(8,128)(2,1)S(1)}, u32[]{:S(2)}, u32[]{:S(2)}) collective-permute-start(bf16[16,256,128]{2,1,0:T(8,128)(2,1)} %shard_map.125.near_hbm), channel_id=1, source_target_pairs={{0,1},{1,0},{2,3},{3,2},{4,5},{5,4},{6,7},{7,6},{8,9},{9,8},{10,11... | collective-permute-start | bytes 3145736 | tf_op jit(solution)/shard_map/ppermute | solution.py:389
  189.2 1.0 copy-start.3
  190.2 1.0 copy-start.6

commit v8 on v7

--- a/solution.py
+++ b/solution.py
@@ -76,7 +76,7 @@
     return v / (1.0 + jnp.exp(-v))
 
 
-def pack_kernel(latent_hbm, w_hbm, out_ref, latent_ref, w_ref, sems):
+def pack_kernel(latent_hbm, w_hbm, out_hbm, latent_ref, w_ref, patch_ref, piece_ref, sems):
     copies = [
         pltpu.make_async_copy(latent_hbm, latent_ref, sems.at[0]),
         pltpu.make_async_copy(w_hbm, w_ref, sems.at[1]),
@@ -87,8 +87,12 @@
     rows = [latent_ref[r].astype(F32) for r in range(PC)]
     patch = jnp.concatenate(rows, axis=0).astype(BF16)
     for j in range(C // 128):
-        chunk = patch[:, 128 * j : 128 * (j + 1)]
-        out_ref[:, NP * j : NP * (j + 1), :] = jnp.broadcast_to(chunk[None], (NP, NP, 128))
+        patch_ref[NP * j : NP * (j + 1), :] = patch[:, 128 * j : 128 * (j + 1)]
+    for k in range(NP):
+        copies.append(
+            pltpu.make_async_copy(patch_ref, out_hbm.at[k, pl.ds(0, ROWS)], sems.at[2 + k])
+        )
+        copies[-1].start()
     copies[1].wait()
     lane = iota((PIECE, 128), 1)
     for k in range(NP // 2):
@@ -100,8 +104,17 @@
             low = jnp.concatenate([right[PIECE:], blank], axis=0)
             return jnp.where(lane < HEAD, left[:PIECE], low).astype(BF16)
 
-        out_ref[2 * k, ROWS:, :] = halves(w, turned)
-        out_ref[2 * k + 1, ROWS:, :] = halves(turned, w)
+        piece_ref[2 * k] = halves(w, turned)
+        piece_ref[2 * k + 1] = halves(turned, w)
+    for k in range(NP):
+        copies.append(
+            pltpu.make_async_copy(
+                piece_ref.at[k], out_hbm.at[k, pl.ds(ROWS, PIECE)], sems.at[2 + NP + k]
+            )
+        )
+        copies[-1].start()
+    for copy in copies[2:]:
+        copy.wait()
 
 
 def unpack_kernel(block_ref, out_hbm, out_ref, sem):
@@ -263,7 +276,7 @@
     own_sums(total.astype(F32), sums_ref)
 
 
-def norm_kernel(which, total_ref, sums_ref, cols_ref, out_ref):
+def norm_kernel(which, total_ref, sums_ref, cols_ref, out_hbm, out_ref, sems):
     mean, rstd = moments(sums_ref)
     upper = iota((OC, 1), 0) < GC
     gain = jnp.where(upper, rstd[:, 0:1], rstd[:, 1:2]) * cols_ref[:, 3 * which + 1 : 3 * which + 2]
@@ -272,7 +285,12 @@
     value = total_ref[...].astype(F32) * gain + offset
     if which == 0:
         value = silu(value)
-    out_ref[...] = jnp.broadcast_to(value.astype(BF16)[None], out_ref.shape)
+    out_ref[...] = value.astype(BF16)
+    copies = [pltpu.make_async_copy(out_ref, out_hbm.at[k], sems.at[k]) for k in range(NP)]
+    for copy in copies:
+        copy.start()
+    for copy in copies:
+        copy.wait()
 
 
 def join_kernel(left_ref, right_ref, out_ref, sems):
@@ -299,7 +317,7 @@
     near_ref,
     sem,
 ):
-    chunk = 4
+    chunk = 8
     copy = pltpu.make_async_copy(near_hbm, near_ref, sem)
     copy.start()
     mapped = nn(w_ref[...], x_ref[...])
@@ -402,7 +420,14 @@
 
     def gathered(which, total, sums):
         sums = to_every(sums, PCOL)
-        (copies,) = call(functools.partial(norm_kernel, which), [every])(total, sums, cols)
+        (copies,) = call(
+            functools.partial(norm_kernel, which),
+            [every],
+            space=pltpu.HBM,
+            scratch=[pltpu.VMEM((OC, CELLS), BF16), pltpu.SemaphoreType.DMA((NP,))],
+        )(
+            total, sums, cols
+        )
         return to_every(copies, PROW).reshape(C, CELLS)
 
     (block,) = call(
@@ -412,8 +437,11 @@
         scratch=[
             pltpu.VMEM((PC, PC, C), BF16),
             pltpu.VMEM(w_out.shape, BF16),
-            pltpu.SemaphoreType.DMA((2,)),
+            pltpu.VMEM((ROWS, 128), BF16),
+            pltpu.VMEM((NP, PIECE, 128), BF16),
+            pltpu.SemaphoreType.DMA((2 + 2 * NP,)),
         ],
+        space=pltpu.HBM,
     )(latent, w_out)
     block = to_every(block, PROW)
     sums, inner, outer = call(stats_cells_kernel, [sums_out, edge, edge])(block)

time: 228 us -> 229 us (level)
  no operation moved by 1% of the time
where the time goes in v8:
time: 229 us; the launch traced here: 226 us
  blocking collectives  91.3 us (40%)
  starting transfers between devices  59.2 us (26%)
  waiting for transfers between devices  49 us (21%)
  Pallas kernels  20.4 us (9%)
  local copies, waits for them, and re-layouts  5.39 us (2%)
    all_to_all x4, blocking collectives, to_every(): return lax.all_to_all(copies, axis, split_axis=0, concat_axis=0, tiled=True)  91.3 us
    all_to_all x3, starting transfers between devices, to_every(): return lax.all_to_all(copies, axis, split_axis=0, concat_axis=0, tiled=True)  30.1 us
    ppermute x5, waiting for transfers between devices, shards(): far = lax.ppermute(near, axis, [(i, i ^ bit) for i in range(count)])  24.7 us
    all_to_all x3, waiting for transfers between devices, to_every(): return lax.all_to_all(copies, axis, split_axis=0, concat_axis=0, tiled=True)  21.5 us
    pallas_call x15, Pallas kernels, run(): pl.pallas_call(kernel, out_shape=[pltpu.HBM(*out) if space is pltpu.HBM e...  20.4 us
    ppermute x5, starting transfers between devices, shards(): far = lax.ppermute(near, axis, [(i, i ^ bit) for i in range(count)])  12.4 us
    ppermute x2, starting transfers between devices, swapped(): return (lax.ppermute(inner, PCOL[-1], [(0, 1), (1, 0)]), outer)  10.8 us
    ppermute x2, starting transfers between devices, swapped(): outer = lax.ppermute(outer, PCOL, pairs)  5.87 us
  transfers between devices with their start and end apart: 12, of which 7 were waited for; matrix products, arithmetic and copies ran while one was open for 0% of the time, Pallas kernels for 3%

profile of v8, /device:TPU:1, one launch (start us, length us, event | category | flops | bytes accessed | tf_op | source)
XLA Modules:
  0.0 226.2 jit_solution(1871599225445203546)
XLA Ops:
  0.7 2.2 shard_map.113
  2.9 41.8 %all_to_all.35.block_ref = bf16[16,208,128]{2,1,0:T(8,128)(2,1)S(1)} all-to-all(bf16[16,208,128]{2,1,0:T(8,128)(2,1)} %shard_map.113), channel_id=1, replica_groups=mesh['prow_0'=2,'prow_1'=8,'pcol_0'=4,'pcol_1'=4,'pcol_2'=2] {'prow_0','..., dimensions={0} | all-to-all | bytes 1703936 | tf_op jit(solution)/shard_map/all_to_all | solution.py:383
  46.1 3.9 %collective-permute-start = (bf16[64,1280]{1,0:T(8,128)(2,1)S(1)}, bf16[64,1280]{1,0:T(8,128)(2,1)S(1)}, u32[]{:S(2)}, u32[]{:S(2)}) collective-permute-start(bf16[64,1280]{1,0:T(8,128)(2,1)S(1)} %get-tuple-element.16), channel_id=1, source_target_pairs={{0,1},{1,0},{2,3},{3,2},{4,5},{5,4},{6,7},{7,6},{8,9},{9,8},{10,11... | collective-permute-start | bytes 491528 | tf_op jit(solution)/shard_map/ppermute | solution.py:389
  50.1 3.0 %collective-permute-start.1 = (bf16[64,1280]{1,0:T(8,128)(2,1)S(1)}, bf16[64,1280]{1,0:T(8,128)(2,1)S(1)}, u32[]{:S(2)}, u32[]{:S(2)}) collective-permute-start(bf16[64,1280]{1,0:T(8,128)(2,1)S(1)} %get-tuple-element.17), channel_id=1, source_target_pairs={{1,2},{2,1},{3,4},{4,3},{5,6},{6,5},{7,8},{8,7},{9,10},{10,9},{11,... | collective-permute-start | bytes 491528 | tf_op jit(solution)/shard_map/ppermute | solution.py:388
  53.1 6.8 %all-to-all-start.1 = ((f32[32,1,128]{2,1,0:T(1,128)}), f32[32,1,128]{2,1,0:T(1,128)S(1)}, u32[]{:S(2)}, u32[]{:S(2)}) async-start(f32[32,1,128]{2,1,0:T(1,128)} %get-tuple-element.15), calls=%async_computation.1 | async-start | bytes 32768 | tf_op jit(solution)/shard_map/all_to_all | solution.py:383
  60.3 6.9 %all-to-all-done.1.sums_ref = f32[32,1,128]{2,1,0:T(1,128)S(1)} async-done(((f32[32,1,128]{2,1,0:T(1,128)}), f32[32,1,128]{2,1,0:T(1,128)S(1)}, u32[]{:S(2)}, u32[]{:S(2)}) %all-to-all-start.1) | async-done | bytes 16416 | tf_op jit(solution)/shard_map/all_to_all | solution.py:383
  69.4 10.8 %all_to_all.36.sums_ref = f32[32,1,128]{2,1,0:T(1,128)S(1)} all-to-all(f32[32,1,128]{2,1,0:T(1,128)S(1)} %get-tuple-element.19), channel_id=1, replica_groups=mesh['prow_0'=2,'prow_1'=8,'pcol_0'=4,'pcol_1'=4,'pcol_2'=2] {'pcol_0','..., dimensions={0} | all-to-all | bytes 32768 | tf_op jit(solution)/shard_map/all_to_all | solution.py:383
  81.5 4.6 %all-to-all-start.3 = ((bf16[16,80,256]{2,1,0:T(8,128)(2,1)}), bf16[16,80,256]{2,1,0:T(8,128)(2,1)S(1)}, u32[]{:S(2)}, u32[]{:S(2)}) async-start(bf16[16,80,256]{2,1,0:T(8,128)(2,1)} %shard_map.117), calls=%async_computation.3 | async-start | bytes 1310720 | tf_op jit(solution)/shard_map/all_to_all | solution.py:383
  86.1 2.2 collective-permute-start.4
  88.3 4.2 %collective-permute-done.4.right_ref = bf16[1,256,128]{2,1,0:T(8,128)(2,1)S(1)} collective-permute-done((bf16[1,256,128]{2,1,0:T(8,128)(2,1)S(1)}, bf16[1,256,128]{2,1,0:T(8,128)(2,1)S(1)}, u32[]{:S(2)}, u32[]{:S(2)}) %collective-permute-start.4) | collective-permute-done | bytes 65568 | tf_op jit(solution)/shard_map/ppermute | solution.py:407
  93.2 2.4 %collective-permute-start.5 = (bf16[2,256,128]{2,1,0:T(8,128)(2,1)}, bf16[2,256,128]{2,1,0:T(8,128)(2,1)S(1)}, u32[]{:S(2)}, u32[]{:S(2)}) collective-permute-start(bf16[2,256,128]{2,1,0:T(8,128)(2,1)} %shard_map.122.left_ref), channel_id=1, source_target_pairs={{0,16},{8,24},{16,0},{24,8},{1,17},{9,25},{17,1},{25,9},{2,18},{10... | collective-permute-start | bytes 393224 | tf_op jit(solution)/shard_map/ppermute | solution.py:407
  95.6 13.8 %collective-permute-done.5.right_ref = bf16[2,256,128]{2,1,0:T(8,128)(2,1)S(1)} collective-permute-done((bf16[2,256,128]{2,1,0:T(8,128)(2,1)}, bf16[2,256,128]{2,1,0:T(8,128)(2,1)S(1)}, u32[]{:S(2)}, u32[]{:S(2)}) %collective-permute-start.5) | collective-permute-done | bytes 131104 | tf_op jit(solution)/shard_map/ppermute | solution.py:407
  111.0 2.2 collective-permute-start.6
  113.2 5.1 %collective-permute-done.6.right_ref = bf16[4,256,128]{2,1,0:T(8,128)(2,1)S(1)} collective-permute-done((bf16[4,256,128]{2,1,0:T(8,128)(2,1)}, bf16[4,256,128]{2,1,0:T(8,128)(2,1)S(1)}, u32[]{:S(2)}, u32[]{:S(2)}) %collective-permute-start.6) | collective-permute-done | bytes 262176 | tf_op jit(solution)/shard_map/ppermute | solution.py:407
  120.1 2.8 %collective-permute-start.7 = (bf16[8,256,128]{2,1,0:T(8,128)(2,1)}, bf16[8,256,128]{2,1,0:T(8,128)(2,1)S(1)}, u32[]{:S(2)}, u32[]{:S(2)}) collective-permute-start(bf16[8,256,128]{2,1,0:T(8,128)(2,1)} %shard_map.124.left_ref), channel_id=1, source_target_pairs={{0,4},{2,6},{4,0},{6,2},{1,5},{3,7},{5,1},{7,3},{8,12},{10,14},{12... | collective-permute-start | bytes 1572872 | tf_op jit(solution)/shard_map/ppermute | solution.py:407
  125.3 6.8 %collective-permute-start.2 = (f32[80,64]{1,0:T(8,128)S(1)}, f32[80,64]{1,0:T(8,128)S(1)}, u32[]{:S(2)}, u32[]{:S(2)}) collective-permute-start(f32[80,64]{1,0:T(8,128)S(1)} %get-tuple-element.21), channel_id=1, source_target_pairs={{0,1},{1,0},{2,3},{3,2},{4,5},{5,4},{6,7},{7,6},{8,9},{9,8},{10,11... | collective-permute-start | bytes 61448 | tf_op jit(solution)/shard_map/ppermute | solution.py:389
  132.1 2.9 %collective-permute-start.3 = (f32[80,64]{1,0:T(8,128)S(1)}, f32[80,64]{1,0:T(8,128)S(1)}, u32[]{:S(2)}, u32[]{:S(2)}) collective-permute-start(f32[80,64]{1,0:T(8,128)S(1)} %get-tuple-element.22), channel_id=1, source_target_pairs={{1,2},{2,1},{3,4},{4,3},{5,6},{6,5},{7,8},{8,7},{9,10},{10,9},{11,... | collective-permute-start | bytes 61448 | tf_op jit(solution)/shard_map/ppermute | solution.py:388
  135.0 2.7 %collective-permute-done.3.outer_ref = f32[80,64]{1,0:T(8,128)S(1)} collective-permute-done((f32[80,64]{1,0:T(8,128)S(1)}, f32[80,64]{1,0:T(8,128)S(1)}, u32[]{:S(2)}, u32[]{:S(2)}) %collective-permute-start.3) | collective-permute-done | bytes 20512 | tf_op jit(solution)/shard_map/ppermute | solution.py:388
  138.0 11.7 %all_to_all.37.sums_ref = f32[32,1,128]{2,1,0:T(1,128)S(1)} all-to-all(f32[32,1,128]{2,1,0:T(1,128)S(1)} %get-tuple-element.25), channel_id=1, replica_groups=mesh['prow_0'=2,'prow_1'=8,'pcol_0'=4,'pcol_1'=4,'pcol_2'=2] {'pcol_0','..., dimensions={0} | all-to-all | bytes 32768 | tf_op jit(solution)/shard_map/all_to_all | solution.py:383
  151.0 18.7 %all-to-all-start.5 = ((bf16[16,80,256]{2,1,0:T(8,128)(2,1)}), bf16[16,80,256]{2,1,0:T(8,128)(2,1)S(1)}, u32[]{:S(2)}, u32[]{:S(2)}) async-start(bf16[16,80,256]{2,1,0:T(8,128)(2,1)} %shard_map.120), calls=%async_computation.5 | async-start | bytes 1310720 | tf_op jit(solution)/shard_map/all_to_all | solution.py:383
  170.8 2.8 %collective-permute-start.8 = (bf16[16,256,128]{2,1,0:T(8,128)(2,1)}, bf16[16,256,128]{2,1,0:T(8,128)(2,1)S(1)}, u32[]{:S(2)}, u32[]{:S(2)}) collective-permute-start(bf16[16,256,128]{2,1,0:T(8,128)(2,1)} %shard_map.125.near_hbm), channel_id=1, source_target_pairs={{0,1},{1,0},{2,3},{3,2},{4,5},{5,4},{6,7},{7,6},{8,9},{9,8},{10,11... | collective-permute-start | bytes 3145736 | tf_op jit(solution)/shard_map/ppermute | solution.py:407
  176.1 14.6 %all-to-all-done.5 = bf16[16,80,256]{2,1,0:T(8,128)(2,1)S(1)} async-done(((bf16[16,80,256]{2,1,0:T(8,128)(2,1)}), bf16[16,80,256]{2,1,0:T(8,128)(2,1)S(1)}, u32[]{:S(2)}, u32[]{:S(2)}) %all-to-all-start.5) | async-done | bytes 655392 | tf_op jit(solution)/shard_map/all_to_all | solution.py:383
  192.7 5.8 %shard_map.126 = (bf16[16,16,1280]{2,1,0:T(8,128)(2,1)S(1)}, bf16[256,128]{1,0:T(8,128)(2,1)}) custom-call(bf16[1280,256]{1,0:T(8,128)(2,1)S(1)} %bitcast.8, bf16[192,1280]{1,0:T(8,128)(2,1)S(1)} %copy-done.6, bf16[1280,128]{1,0:T(8,128)(2,1)S(1)} %copy-done.3, bf16[80,256]{1,0:T(8,128)(2,1)S(1)} %get-tuple-element.24.total_ref.own_ref, ...), custom_call_target="tpu_custom_call" | custom-call | tf_op jit(solution)/shard_map/pallas_call | solution.py:368
  198.5 26.9 %all_to_all.38.parts_ref = bf16[16,16,1280]{2,1,0:T(8,128)(2,1)S(1)} all-to-all(bf16[16,16,1280]{2,1,0:T(8,128)(2,1)S(1)} %get-tuple-element.26), channel_id=1, replica_groups=mesh['prow_0'=2,'prow_1'=8,'pcol_0'=4,'pcol_1'=4,'pcol_2'=2] {'prow_0','..., dimensions={0} | all-to-all | bytes 1310720 | tf_op jit(solution)/shard_map/all_to_all | solution.py:383
  (44 shorter events, 19.4 us)
Async XLA Ops:
  0.6 59.3 %copy-start.11 = (f32[1280]{0:T(1024)S(1)}, f32[1280]{0:T(1024)}, u32[]{:S(2)}) copy-start(f32[1280]{0:T(1024)} %param.13) | copy-start | bytes 15364
  0.6 59.3 %copy-start.8 = (f32[3,1280]{1,0:T(4,128)S(1)}, f32[3,1280]{1,0:T(4,128)}, u32[]{:S(2)}) copy-start(f32[3,1280]{1,0:T(4,128)} %shift_ref.3) | copy-start | bytes 46084
  0.7 59.3 %copy-start.7 = (f32[3,1280]{1,0:T(4,128)S(1)}, f32[3,1280]{1,0:T(4,128)}, u32[]{:S(2)}) copy-start(f32[3,1280]{1,0:T(4,128)} %scale_ref.3) | copy-start | bytes 46084
  0.7 59.3 %copy-start.10 = (f32[2,1280]{1,0:T(2,128)S(1)}, f32[2,1280]{1,0:T(2,128)}, u32[]{:S(2)}) copy-start(f32[2,1280]{1,0:T(2,128)} %bias_ref.1) | copy-start | bytes 30724
  0.7 66.5 %copy-start.2 = (bf16[3,3,80,1280]{3,2,1,0:T(8,128)(2,1)S(1)}, bf16[3,3,80,1280]{3,2,1,0:T(8,128)(2,1)}, u32[]{:S(2)}) copy-start(bf16[3,3,80,1280]{3,2,1,0:T(8,128)(2,1)} %param.15) | copy-start | bytes 5529604
  46.1 21.0 %collective-permute-start = (bf16[64,1280]{1,0:T(8,128)(2,1)S(1)}, bf16[64,1280]{1,0:T(8,128)(2,1)S(1)}, u32[]{:S(2)}, u32[]{:S(2)}) collective-permute-start(bf16[64,1280]{1,0:T(8,128)(2,1)S(1)} %get-tuple-element.16), channel_id=1, source_target_pairs={{0,1},{1,0},{2,3},{3,2},{4,5},{5,4},{6,7},{7,6},{8,9},{9,8},{10,11... | collective-permute-start | bytes 491528 | tf_op jit(solution)/shard_map/ppermute | solution.py:389
  50.1 17.1 %collective-permute-start.1 = (bf16[64,1280]{1,0:T(8,128)(2,1)S(1)}, bf16[64,1280]{1,0:T(8,128)(2,1)S(1)}, u32[]{:S(2)}, u32[]{:S(2)}) collective-permute-start(bf16[64,1280]{1,0:T(8,128)(2,1)S(1)} %get-tuple-element.17), channel_id=1, source_target_pairs={{1,2},{2,1},{3,4},{4,3},{5,6},{6,5},{7,8},{8,7},{9,10},{10,9},{11,... | collective-permute-start | bytes 491528 | tf_op jit(solution)/shard_map/ppermute | solution.py:388
  53.1 14.1 %all-to-all-start.1 = ((f32[32,1,128]{2,1,0:T(1,128)}), f32[32,1,128]{2,1,0:T(1,128)S(1)}, u32[]{:S(2)}, u32[]{:S(2)}) async-start(f32[32,1,128]{2,1,0:T(1,128)} %get-tuple-element.15), calls=%async_computation.1 | async-start | bytes 32768 | tf_op jit(solution)/shard_map/all_to_all | solution.py:383
  69.4 16.8 %copy-start.9 = (bf16[64,4,1,128]{3,1,2,0:T(4,128)(2,1)S(1)}, bf16[64,4,1,128]{3,1,2,0:T(4,128)(2,1)}, u32[]{:S(2)}) copy-start(bf16[64,4,1,128]{3,1,2,0:T(4,128)(2,1)} %param.19) | copy-start | bytes 196612
  81.5 41.4 %all-to-all-start.3 = ((bf16[16,80,256]{2,1,0:T(8,128)(2,1)}), bf16[16,80,256]{2,1,0:T(8,128)(2,1)S(1)}, u32[]{:S(2)}, u32[]{:S(2)}) async-start(bf16[16,80,256]{2,1,0:T(8,128)(2,1)} %shard_map.117), calls=%async_computation.3 | async-start | bytes 1310720 | tf_op jit(solution)/shard_map/all_to_all | solution.py:383
  86.1 6.4 %collective-permute-start.4 = (bf16[1,256,128]{2,1,0:T(8,128)(2,1)S(1)}, bf16[1,256,128]{2,1,0:T(8,128)(2,1)S(1)}, u32[]{:S(2)}, u32[]{:S(2)}) collective-permute-start(bf16[1,256,128]{2,1,0:T(8,128)(2,1)S(1)} %bitcast.12), channel_id=1, source_target_pairs={{0,8},{8,0},{16,24},{24,16},{1,9},{9,1},{17,25},{25,17},{2,10},{10... | collective-permute-start | bytes 196616 | tf_op jit(solution)/shard_map/ppermute | solution.py:407
  93.2 16.2 %collective-permute-start.5 = (bf16[2,256,128]{2,1,0:T(8,128)(2,1)}, bf16[2,256,128]{2,1,0:T(8,128)(2,1)S(1)}, u32[]{:S(2)}, u32[]{:S(2)}) collective-permute-start(bf16[2,256,128]{2,1,0:T(8,128)(2,1)} %shard_map.122.left_ref), channel_id=1, source_target_pairs={{0,16},{8,24},{16,0},{24,8},{1,17},{9,25},{17,1},{25,9},{2,18},{10... | collective-permute-start | bytes 393224 | tf_op jit(solution)/shard_map/ppermute | solution.py:407
  109.4 0.9 copy-start.5
  111.0 7.3 %collective-permute-start.6 = (bf16[4,256,128]{2,1,0:T(8,128)(2,1)}, bf16[4,256,128]{2,1,0:T(8,128)(2,1)S(1)}, u32[]{:S(2)}, u32[]{:S(2)}) collective-permute-start(bf16[4,256,128]{2,1,0:T(8,128)(2,1)} %shard_map.123.left_ref), channel_id=1, source_target_pairs={{0,2},{2,0},{4,6},{6,4},{1,3},{3,1},{5,7},{7,5},{8,10},{10,8},{12,... | collective-permute-start | bytes 786440 | tf_op jit(solution)/shard_map/ppermute | solution.py:407
  118.4 1.0 copy-start.4
  120.1 49.6 %collective-permute-start.7 = (bf16[8,256,128]{2,1,0:T(8,128)(2,1)}, bf16[8,256,128]{2,1,0:T(8,128)(2,1)S(1)}, u32[]{:S(2)}, u32[]{:S(2)}) collective-permute-start(bf16[8,256,128]{2,1,0:T(8,128)(2,1)} %shard_map.124.left_ref), channel_id=1, source_target_pairs={{0,4},{2,6},{4,0},{6,2},{1,5},{3,7},{5,1},{7,3},{8,12},{10,14},{12... | collective-permute-start | bytes 1572872 | tf_op jit(solution)/shard_map/ppermute | solution.py:407
  122.9 1.5 copy-start.1
  124.4 45.3 %copy-start = (bf16[8,256,128]{2,1,0:T(8,128)(2,1)S(1)}, bf16[8,256,128]{2,1,0:T(8,128)(2,1)}, u32[]{:S(2)}) copy-start(bf16[8,256,128]{2,1,0:T(8,128)(2,1)} %shard_map.124.left_ref) | copy-start | bytes 1572868
  125.3 9.7 %collective-permute-start.2 = (f32[80,64]{1,0:T(8,128)S(1)}, f32[80,64]{1,0:T(8,128)S(1)}, u32[]{:S(2)}, u32[]{:S(2)}) collective-permute-start(f32[80,64]{1,0:T(8,128)S(1)} %get-tuple-element.21), channel_id=1, source_target_pairs={{0,1},{1,0},{2,3},{3,2},{4,5},{5,4},{6,7},{7,6},{8,9},{9,8},{10,11... | collective-permute-start | bytes 61448 | tf_op jit(solution)/shard_map/ppermute | solution.py:389
  132.1 5.6 %collective-permute-start.3 = (f32[80,64]{1,0:T(8,128)S(1)}, f32[80,64]{1,0:T(8,128)S(1)}, u32[]{:S(2)}, u32[]{:S(2)}) collective-permute-start(f32[80,64]{1,0:T(8,128)S(1)} %get-tuple-element.22), channel_id=1, source_target_pairs={{1,2},{2,1},{3,4},{4,3},{5,6},{6,5},{7,8},{8,7},{9,10},{10,9},{11,... | collective-permute-start | bytes 61448 | tf_op jit(solution)/shard_map/ppermute | solution.py:388
  151.0 39.7 %all-to-all-start.5 = ((bf16[16,80,256]{2,1,0:T(8,128)(2,1)}), bf16[16,80,256]{2,1,0:T(8,128)(2,1)S(1)}, u32[]{:S(2)}, u32[]{:S(2)}) async-start(bf16[16,80,256]{2,1,0:T(8,128)(2,1)} %shard_map.120), calls=%async_computation.5 | async-start | bytes 1310720 | tf_op jit(solution)/shard_map/all_to_all | solution.py:383
  170.8 5.3 %collective-permute-start.8 = (bf16[16,256,128]{2,1,0:T(8,128)(2,1)}, bf16[16,256,128]{2,1,0:T(8,128)(2,1)S(1)}, u32[]{:S(2)}, u32[]{:S(2)}) collective-permute-start(bf16[16,256,128]{2,1,0:T(8,128)(2,1)} %shard_map.125.near_hbm), channel_id=1, source_target_pairs={{0,1},{1,0},{2,3},{3,2},{4,5},{5,4},{6,7},{7,6},{8,9},{9,8},{10,11... | collective-permute-start | bytes 3145736 | tf_op jit(solution)/shard_map/ppermute | solution.py:407
  190.7 1.0 copy-start.3
  191.7 1.0 copy-start.6

commit v9 on v7

--- a/solution.py
+++ b/solution.py
@@ -61,7 +61,7 @@
 
 
 ROWS = OC // 5 * C // 128
-PIECE = 48
+PIECE = 40
 BLOCK = ROWS + PIECE
 
 
@@ -94,11 +94,9 @@
     for k in range(NP // 2):
         w = w_ref[:, 128 * k : 128 * (k + 1)].astype(F32)
         turned = pltpu.roll(w, HEAD, 1)
-        blank = jnp.zeros((2 * PIECE - OC, 128), F32)
 
         def halves(left, right):
-            low = jnp.concatenate([right[PIECE:], blank], axis=0)
-            return jnp.where(lane < HEAD, left[:PIECE], low).astype(BF16)
+            return jnp.where(lane < HEAD, left[:PIECE], right[PIECE:]).astype(BF16)
 
         out_ref[2 * k, ROWS:, :] = halves(w, turned)
         out_ref[2 * k + 1, ROWS:, :] = halves(turned, w)
@@ -110,7 +108,7 @@
         piece = block_ref[p, ROWS:, :].astype(F32)
         high = jnp.where(lane >= HEAD, pltpu.roll(piece, HEAD, 1), 0.0)
         low = jnp.where(lane >= HEAD, piece, 0.0)
-        both = jnp.concatenate([high, low[: OC - PIECE]], axis=0)
+        both = jnp.concatenate([high, low], axis=0)
         out_ref[OC * p : OC * (p + 1), :] = both.astype(BF16)
     copy = pltpu.make_async_copy(out_ref, out_hbm, sem)
     copy.start()
@@ -299,7 +297,7 @@
     near_ref,
     sem,
 ):
-    chunk = 4
+    chunk = 8
     copy = pltpu.make_async_copy(near_hbm, near_ref, sem)
     copy.start()
     mapped = nn(w_ref[...], x_ref[...])

time: 228 us -> 227 us (level)
  no operation moved by 1% of the time
where the time goes in v9:
time: 227 us; the launch traced here: 224 us
  blocking collectives  90.4 us (40%)
  starting transfers between devices  58.9 us (26%)
  waiting for transfers between devices  49 us (22%)
  Pallas kernels  19.2 us (8%)
  local copies, waits for them, and re-layouts  5.39 us (2%)
    all_to_all x4, blocking collectives, to_every(): return lax.all_to_all(copies, axis, split_axis=0, concat_axis=0, tiled=True)  90.4 us
    all_to_all x3, starting transfers between devices, to_every(): return lax.all_to_all(copies, axis, split_axis=0, concat_axis=0, tiled=True)  29.9 us
    ppermute x5, waiting for transfers between devices, shards(): far = lax.ppermute(near, axis, [(i, i ^ bit) for i in range(count)])  24.7 us
    all_to_all x3, waiting for transfers between devices, to_every(): return lax.all_to_all(copies, axis, split_axis=0, concat_axis=0, tiled=True)  21.5 us
    pallas_call x15, Pallas kernels, run(): pl.pallas_call(kernel, out_shape=[pltpu.HBM(*out) if space is pltpu.HBM e...  19.2 us
    ppermute x5, starting transfers between devices, shards(): far = lax.ppermute(near, axis, [(i, i ^ bit) for i in range(count)])  12.4 us
    ppermute x2, starting transfers between devices, swapped(): return (lax.ppermute(inner, PCOL[-1], [(0, 1), (1, 0)]), outer)  10.7 us
    ppermute x2, starting transfers between devices, swapped(): outer = lax.ppermute(outer, PCOL, pairs)  5.88 us
  transfers between devices with their start and end apart: 12, of which 7 were waited for; matrix products, arithmetic and copies ran while one was open for 0% of the time, Pallas kernels for 3%

profile of v9, /device:TPU:1, one launch (start us, length us, event | category | flops | bytes accessed | tf_op | source)
XLA Modules:
  0.0 223.8 jit_solution(14622823226862336559)
XLA Ops:
  1.9 41.0 %all_to_all.35.block_ref = bf16[16,200,128]{2,1,0:T(8,128)(2,1)S(1)} all-to-all(bf16[16,200,128]{2,1,0:T(8,128)(2,1)S(1)} %shard_map.113), channel_id=1, replica_groups=mesh['prow_0'=2,'prow_1'=8,'pcol_0'=4,'pcol_1'=4,'pcol_2'=2] {'prow_0','..., dimensions={0} | all-to-all | bytes 1638400 | tf_op jit(solution)/shard_map/all_to_all | solution.py:363
  44.4 3.9 %collective-permute-start = (bf16[64,1280]{1,0:T(8,128)(2,1)S(1)}, bf16[64,1280]{1,0:T(8,128)(2,1)S(1)}, u32[]{:S(2)}, u32[]{:S(2)}) collective-permute-start(bf16[64,1280]{1,0:T(8,128)(2,1)S(1)} %get-tuple-element.16), channel_id=1, source_target_pairs={{0,1},{1,0},{2,3},{3,2},{4,5},{5,4},{6,7},{7,6},{8,9},{9,8},{10,11... | collective-permute-start | bytes 491528 | tf_op jit(solution)/shard_map/ppermute | solution.py:369
  48.3 3.0 %collective-permute-start.1 = (bf16[64,1280]{1,0:T(8,128)(2,1)S(1)}, bf16[64,1280]{1,0:T(8,128)(2,1)S(1)}, u32[]{:S(2)}, u32[]{:S(2)}) collective-permute-start(bf16[64,1280]{1,0:T(8,128)(2,1)S(1)} %get-tuple-element.17), channel_id=1, source_target_pairs={{1,2},{2,1},{3,4},{4,3},{5,6},{6,5},{7,8},{8,7},{9,10},{10,9},{11,... | collective-permute-start | bytes 491528 | tf_op jit(solution)/shard_map/ppermute | solution.py:368
  51.3 6.8 %all-to-all-start.1 = ((f32[32,1,128]{2,1,0:T(1,128)}), f32[32,1,128]{2,1,0:T(1,128)S(1)}, u32[]{:S(2)}, u32[]{:S(2)}) async-start(f32[32,1,128]{2,1,0:T(1,128)} %get-tuple-element.15), calls=%async_computation.1 | async-start | bytes 32768 | tf_op jit(solution)/shard_map/all_to_all | solution.py:363
  58.5 6.9 %all-to-all-done.1.sums_ref = f32[32,1,128]{2,1,0:T(1,128)S(1)} async-done(((f32[32,1,128]{2,1,0:T(1,128)}), f32[32,1,128]{2,1,0:T(1,128)S(1)}, u32[]{:S(2)}, u32[]{:S(2)}) %all-to-all-start.1) | async-done | bytes 16416 | tf_op jit(solution)/shard_map/all_to_all | solution.py:363
  65.4 2.2 shard_map.116
  67.6 10.8 %all_to_all.36.sums_ref = f32[32,1,128]{2,1,0:T(1,128)S(1)} all-to-all(f32[32,1,128]{2,1,0:T(1,128)S(1)} %get-tuple-element.19), channel_id=1, replica_groups=mesh['prow_0'=2,'prow_1'=8,'pcol_0'=4,'pcol_1'=4,'pcol_2'=2] {'pcol_0','..., dimensions={0} | all-to-all | bytes 32768 | tf_op jit(solution)/shard_map/all_to_all | solution.py:363
  79.6 4.3 %all-to-all-start.3 = ((bf16[16,80,256]{2,1,0:T(8,128)(2,1)}), bf16[16,80,256]{2,1,0:T(8,128)(2,1)S(1)}, u32[]{:S(2)}, u32[]{:S(2)}) async-start(bf16[16,80,256]{2,1,0:T(8,128)(2,1)} %shard_map.117), calls=%async_computation.3 | async-start | bytes 1310720 | tf_op jit(solution)/shard_map/all_to_all | solution.py:363
  84.0 2.2 collective-permute-start.4
  86.2 4.2 %collective-permute-done.4.right_ref = bf16[1,256,128]{2,1,0:T(8,128)(2,1)S(1)} collective-permute-done((bf16[1,256,128]{2,1,0:T(8,128)(2,1)S(1)}, bf16[1,256,128]{2,1,0:T(8,128)(2,1)S(1)}, u32[]{:S(2)}, u32[]{:S(2)}) %collective-permute-start.4) | collective-permute-done | bytes 65568 | tf_op jit(solution)/shard_map/ppermute | solution.py:387
  91.0 2.4 %collective-permute-start.5 = (bf16[2,256,128]{2,1,0:T(8,128)(2,1)}, bf16[2,256,128]{2,1,0:T(8,128)(2,1)S(1)}, u32[]{:S(2)}, u32[]{:S(2)}) collective-permute-start(bf16[2,256,128]{2,1,0:T(8,128)(2,1)} %shard_map.122.left_ref), channel_id=1, source_target_pairs={{0,16},{8,24},{16,0},{24,8},{1,17},{9,25},{17,1},{25,9},{2,18},{10... | collective-permute-start | bytes 393224 | tf_op jit(solution)/shard_map/ppermute | solution.py:387
  93.5 13.8 %collective-permute-done.5.right_ref = bf16[2,256,128]{2,1,0:T(8,128)(2,1)S(1)} collective-permute-done((bf16[2,256,128]{2,1,0:T(8,128)(2,1)}, bf16[2,256,128]{2,1,0:T(8,128)(2,1)S(1)}, u32[]{:S(2)}, u32[]{:S(2)}) %collective-permute-start.5) | collective-permute-done | bytes 131104 | tf_op jit(solution)/shard_map/ppermute | solution.py:387
  108.9 2.2 collective-permute-start.6
  111.1 5.1 %collective-permute-done.6.right_ref = bf16[4,256,128]{2,1,0:T(8,128)(2,1)S(1)} collective-permute-done((bf16[4,256,128]{2,1,0:T(8,128)(2,1)}, bf16[4,256,128]{2,1,0:T(8,128)(2,1)S(1)}, u32[]{:S(2)}, u32[]{:S(2)}) %collective-permute-start.6) | collective-permute-done | bytes 262176 | tf_op jit(solution)/shard_map/ppermute | solution.py:387
  118.0 2.8 %collective-permute-start.7 = (bf16[8,256,128]{2,1,0:T(8,128)(2,1)}, bf16[8,256,128]{2,1,0:T(8,128)(2,1)S(1)}, u32[]{:S(2)}, u32[]{:S(2)}) collective-permute-start(bf16[8,256,128]{2,1,0:T(8,128)(2,1)} %shard_map.124.left_ref), channel_id=1, source_target_pairs={{0,4},{2,6},{4,0},{6,2},{1,5},{3,7},{5,1},{7,3},{8,12},{10,14},{12... | collective-permute-start | bytes 1572872 | tf_op jit(solution)/shard_map/ppermute | solution.py:387
  123.1 6.8 %collective-permute-start.2 = (f32[80,64]{1,0:T(8,128)S(1)}, f32[80,64]{1,0:T(8,128)S(1)}, u32[]{:S(2)}, u32[]{:S(2)}) collective-permute-start(f32[80,64]{1,0:T(8,128)S(1)} %get-tuple-element.21), channel_id=1, source_target_pairs={{0,1},{1,0},{2,3},{3,2},{4,5},{5,4},{6,7},{7,6},{8,9},{9,8},{10,11... | collective-permute-start | bytes 61448 | tf_op jit(solution)/shard_map/ppermute | solution.py:369
  130.0 2.9 %collective-permute-start.3 = (f32[80,64]{1,0:T(8,128)S(1)}, f32[80,64]{1,0:T(8,128)S(1)}, u32[]{:S(2)}, u32[]{:S(2)}) collective-permute-start(f32[80,64]{1,0:T(8,128)S(1)} %get-tuple-element.22), channel_id=1, source_target_pairs={{1,2},{2,1},{3,4},{4,3},{5,6},{6,5},{7,8},{8,7},{9,10},{10,9},{11,... | collective-permute-start | bytes 61448 | tf_op jit(solution)/shard_map/ppermute | solution.py:368
  132.9 2.7 %collective-permute-done.3.outer_ref = f32[80,64]{1,0:T(8,128)S(1)} collective-permute-done((f32[80,64]{1,0:T(8,128)S(1)}, f32[80,64]{1,0:T(8,128)S(1)}, u32[]{:S(2)}, u32[]{:S(2)}) %collective-permute-start.3) | collective-permute-done | bytes 20512 | tf_op jit(solution)/shard_map/ppermute | solution.py:368
  135.8 11.7 %all_to_all.37.sums_ref = f32[32,1,128]{2,1,0:T(1,128)S(1)} all-to-all(f32[32,1,128]{2,1,0:T(1,128)S(1)} %get-tuple-element.25), channel_id=1, replica_groups=mesh['prow_0'=2,'prow_1'=8,'pcol_0'=4,'pcol_1'=4,'pcol_2'=2] {'pcol_0','..., dimensions={0} | all-to-all | bytes 32768 | tf_op jit(solution)/shard_map/all_to_all | solution.py:363
  148.7 18.7 %all-to-all-start.5 = ((bf16[16,80,256]{2,1,0:T(8,128)(2,1)}), bf16[16,80,256]{2,1,0:T(8,128)(2,1)S(1)}, u32[]{:S(2)}, u32[]{:S(2)}) async-start(bf16[16,80,256]{2,1,0:T(8,128)(2,1)} %shard_map.120), calls=%async_computation.5 | async-start | bytes 1310720 | tf_op jit(solution)/shard_map/all_to_all | solution.py:363
  168.5 2.8 %collective-permute-start.8 = (bf16[16,256,128]{2,1,0:T(8,128)(2,1)}, bf16[16,256,128]{2,1,0:T(8,128)(2,1)S(1)}, u32[]{:S(2)}, u32[]{:S(2)}) collective-permute-start(bf16[16,256,128]{2,1,0:T(8,128)(2,1)} %shard_map.125.near_hbm), channel_id=1, source_target_pairs={{0,1},{1,0},{2,3},{3,2},{4,5},{5,4},{6,7},{7,6},{8,9},{9,8},{10,11... | collective-permute-start | bytes 3145736 | tf_op jit(solution)/shard_map/ppermute | solution.py:387
  173.8 14.6 %all-to-all-done.5 = bf16[16,80,256]{2,1,0:T(8,128)(2,1)S(1)} async-done(((bf16[16,80,256]{2,1,0:T(8,128)(2,1)}), bf16[16,80,256]{2,1,0:T(8,128)(2,1)S(1)}, u32[]{:S(2)}, u32[]{:S(2)}) %all-to-all-start.5) | async-done | bytes 655392 | tf_op jit(solution)/shard_map/all_to_all | solution.py:363
  190.4 5.8 %shard_map.126 = (bf16[16,16,1280]{2,1,0:T(8,128)(2,1)S(1)}, bf16[256,128]{1,0:T(8,128)(2,1)}) custom-call(bf16[1280,256]{1,0:T(8,128)(2,1)S(1)} %bitcast.8, bf16[192,1280]{1,0:T(8,128)(2,1)S(1)} %copy-done.6, bf16[1280,128]{1,0:T(8,128)(2,1)S(1)} %copy-done.3, bf16[80,256]{1,0:T(8,128)(2,1)S(1)} %get-tuple-element.24.total_ref.own_ref, ...), custom_call_target="tpu_custom_call" | custom-call | tf_op jit(solution)/shard_map/pallas_call | solution.py:348
  196.2 26.9 %all_to_all.38.parts_ref = bf16[16,16,1280]{2,1,0:T(8,128)(2,1)S(1)} all-to-all(bf16[16,16,1280]{2,1,0:T(8,128)(2,1)S(1)} %get-tuple-element.26), channel_id=1, replica_groups=mesh['prow_0'=2,'prow_1'=8,'pcol_0'=4,'pcol_1'=4,'pcol_2'=2] {'prow_0','..., dimensions={0} | all-to-all | bytes 1310720 | tf_op jit(solution)/shard_map/all_to_all | solution.py:363
  (44 shorter events, 18.2 us)
Async XLA Ops:
  0.6 57.5 %copy-start.11 = (f32[1280]{0:T(1024)S(1)}, f32[1280]{0:T(1024)}, u32[]{:S(2)}) copy-start(f32[1280]{0:T(1024)} %param.13) | copy-start | bytes 15364
  0.6 57.5 %copy-start.8 = (f32[3,1280]{1,0:T(4,128)S(1)}, f32[3,1280]{1,0:T(4,128)}, u32[]{:S(2)}) copy-start(f32[3,1280]{1,0:T(4,128)} %shift_ref.3) | copy-start | bytes 46084
  0.7 57.5 %copy-start.7 = (f32[3,1280]{1,0:T(4,128)S(1)}, f32[3,1280]{1,0:T(4,128)}, u32[]{:S(2)}) copy-start(f32[3,1280]{1,0:T(4,128)} %scale_ref.3) | copy-start | bytes 46084
  0.7 57.5 %copy-start.10 = (f32[2,1280]{1,0:T(2,128)S(1)}, f32[2,1280]{1,0:T(2,128)}, u32[]{:S(2)}) copy-start(f32[2,1280]{1,0:T(2,128)} %bias_ref.1) | copy-start | bytes 30724
  0.7 64.7 %copy-start.2 = (bf16[3,3,80,1280]{3,2,1,0:T(8,128)(2,1)S(1)}, bf16[3,3,80,1280]{3,2,1,0:T(8,128)(2,1)}, u32[]{:S(2)}) copy-start(bf16[3,3,80,1280]{3,2,1,0:T(8,128)(2,1)} %param.15) | copy-start | bytes 5529604
  44.4 21.0 %collective-permute-start = (bf16[64,1280]{1,0:T(8,128)(2,1)S(1)}, bf16[64,1280]{1,0:T(8,128)(2,1)S(1)}, u32[]{:S(2)}, u32[]{:S(2)}) collective-permute-start(bf16[64,1280]{1,0:T(8,128)(2,1)S(1)} %get-tuple-element.16), channel_id=1, source_target_pairs={{0,1},{1,0},{2,3},{3,2},{4,5},{5,4},{6,7},{7,6},{8,9},{9,8},{10,11... | collective-permute-start | bytes 491528 | tf_op jit(solution)/shard_map/ppermute | solution.py:369
  48.3 17.1 %collective-permute-start.1 = (bf16[64,1280]{1,0:T(8,128)(2,1)S(1)}, bf16[64,1280]{1,0:T(8,128)(2,1)S(1)}, u32[]{:S(2)}, u32[]{:S(2)}) collective-permute-start(bf16[64,1280]{1,0:T(8,128)(2,1)S(1)} %get-tuple-element.17), channel_id=1, source_target_pairs={{1,2},{2,1},{3,4},{4,3},{5,6},{6,5},{7,8},{8,7},{9,10},{10,9},{11,... | collective-permute-start | bytes 491528 | tf_op jit(solution)/shard_map/ppermute | solution.py:368
  51.3 14.1 %all-to-all-start.1 = ((f32[32,1,128]{2,1,0:T(1,128)}), f32[32,1,128]{2,1,0:T(1,128)S(1)}, u32[]{:S(2)}, u32[]{:S(2)}) async-start(f32[32,1,128]{2,1,0:T(1,128)} %get-tuple-element.15), calls=%async_computation.1 | async-start | bytes 32768 | tf_op jit(solution)/shard_map/all_to_all | solution.py:363
  67.6 16.4 %copy-start.9 = (bf16[64,4,1,128]{3,1,2,0:T(4,128)(2,1)S(1)}, bf16[64,4,1,128]{3,1,2,0:T(4,128)(2,1)}, u32[]{:S(2)}) copy-start(bf16[64,4,1,128]{3,1,2,0:T(4,128)(2,1)} %param.19) | copy-start | bytes 196612
  79.6 41.1 %all-to-all-start.3 = ((bf16[16,80,256]{2,1,0:T(8,128)(2,1)}), bf16[16,80,256]{2,1,0:T(8,128)(2,1)S(1)}, u32[]{:S(2)}, u32[]{:S(2)}) async-start(bf16[16,80,256]{2,1,0:T(8,128)(2,1)} %shard_map.117), calls=%async_computation.3 | async-start | bytes 1310720 | tf_op jit(solution)/shard_map/all_to_all | solution.py:363
  84.0 6.4 %collective-permute-start.4 = (bf16[1,256,128]{2,1,0:T(8,128)(2,1)S(1)}, bf16[1,256,128]{2,1,0:T(8,128)(2,1)S(1)}, u32[]{:S(2)}, u32[]{:S(2)}) collective-permute-start(bf16[1,256,128]{2,1,0:T(8,128)(2,1)S(1)} %bitcast.12), channel_id=1, source_target_pairs={{0,8},{8,0},{16,24},{24,16},{1,9},{9,1},{17,25},{25,17},{2,10},{10... | collective-permute-start | bytes 196616 | tf_op jit(solution)/shard_map/ppermute | solution.py:387
  91.0 16.2 %collective-permute-start.5 = (bf16[2,256,128]{2,1,0:T(8,128)(2,1)}, bf16[2,256,128]{2,1,0:T(8,128)(2,1)S(1)}, u32[]{:S(2)}, u32[]{:S(2)}) collective-permute-start(bf16[2,256,128]{2,1,0:T(8,128)(2,1)} %shard_map.122.left_ref), channel_id=1, source_target_pairs={{0,16},{8,24},{16,0},{24,8},{1,17},{9,25},{17,1},{25,9},{2,18},{10... | collective-permute-start | bytes 393224 | tf_op jit(solution)/shard_map/ppermute | solution.py:387
  107.3 0.9 copy-start.5
  108.9 7.3 %collective-permute-start.6 = (bf16[4,256,128]{2,1,0:T(8,128)(2,1)}, bf16[4,256,128]{2,1,0:T(8,128)(2,1)S(1)}, u32[]{:S(2)}, u32[]{:S(2)}) collective-permute-start(bf16[4,256,128]{2,1,0:T(8,128)(2,1)} %shard_map.123.left_ref), channel_id=1, source_target_pairs={{0,2},{2,0},{4,6},{6,4},{1,3},{3,1},{5,7},{7,5},{8,10},{10,8},{12,... | collective-permute-start | bytes 786440 | tf_op jit(solution)/shard_map/ppermute | solution.py:387
  116.2 1.0 copy-start.4
  118.0 49.4 %collective-permute-start.7 = (bf16[8,256,128]{2,1,0:T(8,128)(2,1)}, bf16[8,256,128]{2,1,0:T(8,128)(2,1)S(1)}, u32[]{:S(2)}, u32[]{:S(2)}) collective-permute-start(bf16[8,256,128]{2,1,0:T(8,128)(2,1)} %shard_map.124.left_ref), channel_id=1, source_target_pairs={{0,4},{2,6},{4,0},{6,2},{1,5},{3,7},{5,1},{7,3},{8,12},{10,14},{12... | collective-permute-start | bytes 1572872 | tf_op jit(solution)/shard_map/ppermute | solution.py:387
  120.8 1.5 copy-start.1
  122.3 45.2 %copy-start = (bf16[8,256,128]{2,1,0:T(8,128)(2,1)S(1)}, bf16[8,256,128]{2,1,0:T(8,128)(2,1)}, u32[]{:S(2)}) copy-start(bf16[8,256,128]{2,1,0:T(8,128)(2,1)} %shard_map.124.left_ref) | copy-start | bytes 1572868
  123.1 9.7 %collective-permute-start.2 = (f32[80,64]{1,0:T(8,128)S(1)}, f32[80,64]{1,0:T(8,128)S(1)}, u32[]{:S(2)}, u32[]{:S(2)}) collective-permute-start(f32[80,64]{1,0:T(8,128)S(1)} %get-tuple-element.21), channel_id=1, source_target_pairs={{0,1},{1,0},{2,3},{3,2},{4,5},{5,4},{6,7},{7,6},{8,9},{9,8},{10,11... | collective-permute-start | bytes 61448 | tf_op jit(solution)/shard_map/ppermute | solution.py:369
  130.0 5.6 %collective-permute-start.3 = (f32[80,64]{1,0:T(8,128)S(1)}, f32[80,64]{1,0:T(8,128)S(1)}, u32[]{:S(2)}, u32[]{:S(2)}) collective-permute-start(f32[80,64]{1,0:T(8,128)S(1)} %get-tuple-element.22), channel_id=1, source_target_pairs={{1,2},{2,1},{3,4},{4,3},{5,6},{6,5},{7,8},{8,7},{9,10},{10,9},{11,... | collective-permute-start | bytes 61448 | tf_op jit(solution)/shard_map/ppermute | solution.py:368
  148.7 39.7 %all-to-all-start.5 = ((bf16[16,80,256]{2,1,0:T(8,128)(2,1)}), bf16[16,80,256]{2,1,0:T(8,128)(2,1)S(1)}, u32[]{:S(2)}, u32[]{:S(2)}) async-start(bf16[16,80,256]{2,1,0:T(8,128)(2,1)} %shard_map.120), calls=%async_computation.5 | async-start | bytes 1310720 | tf_op jit(solution)/shard_map/all_to_all | solution.py:363
  168.5 5.3 %collective-permute-start.8 = (bf16[16,256,128]{2,1,0:T(8,128)(2,1)}, bf16[16,256,128]{2,1,0:T(8,128)(2,1)S(1)}, u32[]{:S(2)}, u32[]{:S(2)}) collective-permute-start(bf16[16,256,128]{2,1,0:T(8,128)(2,1)} %shard_map.125.near_hbm), channel_id=1, source_target_pairs={{0,1},{1,0},{2,3},{3,2},{4,5},{5,4},{6,7},{7,6},{8,9},{9,8},{10,11... | collective-permute-start | bytes 3145736 | tf_op jit(solution)/shard_map/ppermute | solution.py:387
  188.4 1.0 copy-start.3
  189.4 1.0 copy-start.6
